TPU v7x, 128 devices: a whole 4x4x4 slice. The times are simulated.
128 devices in a mesh: ax: 16 (over x, z), rad: 8 (over y, core).
Axes of the slice: x: 4, y: 4, z: 4, core: 2. Of those that a mesh axis runs over, the one named last changes fastest.
Arguments:
- forcing: float32 [32, 5, 256, 1024], P(None, None, 'ax', 'rad'), may hold values from -300 to 300, as said below
- vel_axial: float32 [256, 1024], P('ax', 'rad'), may hold values from 0.2 to 1
- vel_radial: float32 [256, 1024], P('ax', 'rad'), may hold values from -0.4 to 0.4
- coupling: float32 [5, 5, 256, 1024], P(None, None, 'ax', 'rad'), may hold values from -1.5 to 1.5
- viscosity: float32 [5], replicated, may hold values from 0.03 to 0.18
Outputs:
- basis: float32 [32, 5, 256, 1024], P(None, None, 'ax', 'rad')
- r_factor: float32 [32, 32], replicated
Inputs may be any that keep to these rules, and one draw needn't show every extreme that they name: `forcing`: forcing of the linearized equations.
All inputs are finite; a program needn't handle non-finite values.
Results may differ from a plain program's by a relative error of at most 0.00024.
Values sent between devices are 32-bit elements; how exact they have to be, the bound alone decides.
No kernel may reach another device: no remote copies, remote signals or barrier semaphores. Data moves between devices by JAX's collectives and lax.ppermute only.
A program may use at most 64 MiB of HBM per device.

v0:
```python
import jax
import jax.numpy as jnp
from jax import lax
from jax.sharding import PartitionSpec as P

STEPS = 3


time_step = 0.8


def padded_2(shard, sides, width):
    for axis, dim in sides:
        size, length = (lax.axis_size(axis), shard.shape[dim])
        up = [(i, (i + 1) % size) for i in range(size - 1)]
        down = [(j, i) for i, j in up]
        last = lax.slice_in_dim(shard, length - width, length, axis=dim)
        initial = lax.slice_in_dim(shard, 0, width, axis=dim)
        before = lax.ppermute(last, axis, up)
        after = lax.ppermute(initial, axis, down)
        shard = jnp.concatenate([before, shard, after], axis=dim)
    return shard


def combined_all(shard, axis, combine):
    everything = lax.all_gather(shard, axis)
    initial = everything[0]

    def turn(k, so_far):
        return combine(so_far, everything[k])

    return lax.fori_loop(1, lax.axis_size(axis), turn, initial)


def operate(padded, vel_axial, vel_radial, coupling, viscosity):
    center = padded[..., 2:-2, 2:-2]
    axial_up = padded[..., 3:-1, 2:-2]
    axial_down = padded[..., 1:-3, 2:-2]
    axial_far_up = padded[..., 4:, 2:-2]
    axial_far_down = padded[..., :-4, 2:-2]
    radial_up = padded[..., 2:-2, 3:-1]
    radial_down = padded[..., 2:-2, 1:-3]
    radial_far_up = padded[..., 2:-2, 4:]
    radial_far_down = padded[..., 2:-2, :-4]
    first_axial = (8.0 * (axial_up - axial_down) - (axial_far_up - axial_far_down)) / 12.0
    first_radial = (8.0 * (radial_up - radial_down) - (radial_far_up - radial_far_down)) / 12.0
    second = (
        16.0 * (axial_up + axial_down + radial_up + radial_down)
        - (axial_far_up + axial_far_down + radial_far_up + radial_far_down)
        - 60.0 * center
    ) / 12.0
    result = (
        -vel_axial * first_axial - vel_radial * first_radial + viscosity[:, None, None] * second
    )
    for source in range(coupling.shape[1]):
        result = result + coupling[:, source] * center[..., source : source + 1, :, :]
    return result


def upper_inverse(upper_factor):
    order = upper_factor.shape[0]
    identity = jnp.eye(order, dtype=jnp.float32)

    def one_row(count, inverse):
        row_index = order - 1 - count
        factor_row = lax.dynamic_slice_in_dim(upper_factor, row_index, 1, 0)
        unit_row = lax.dynamic_slice_in_dim(identity, row_index, 1, 0)
        pivot = jnp.sum(factor_row * unit_row)
        new_row = (unit_row - jnp.dot(factor_row, inverse, precision=lax.Precision.HIGHEST)) / pivot
        return lax.dynamic_update_slice_in_dim(inverse, new_row, row_index, 0)

    return lax.fori_loop(0, order, one_row, jnp.zeros((order, order), jnp.float32))


def rim_operator(field_now, vel_axial, vel_radial, coupling, viscosity):
    padded = padded_2(field_now, (("ax", 2), ("rad", 3)), 2)
    return operate(padded, vel_axial, vel_radial, coupling, viscosity)


def join_factors(first_factor, other_factor):
    summed = jnp.dot(first_factor.T, first_factor, precision=lax.Precision.HIGHEST)
    summed = summed + jnp.dot(other_factor.T, other_factor, precision=lax.Precision.HIGHEST)
    return jnp.linalg.cholesky(summed).T


def per_device(forcing, vel_axial, vel_radial, coupling, viscosity):
    vectors, variables, axial_cells, radial_cells = forcing.shape
    field_now = forcing
    for step_index in range(STEPS):
        slope_one = rim_operator(field_now, vel_axial, vel_radial, coupling, viscosity)
        middle = field_now + time_step * slope_one
        slope_two = rim_operator(middle, vel_axial, vel_radial, coupling, viscosity)
        field_now = field_now + 0.5 * time_step * (slope_one + slope_two)
    flattened = field_now.reshape(vectors, variables * axial_cells * radial_cells)
    rows_all = variables * axial_cells * radial_cells * lax.axis_size("ax") * lax.axis_size("rad")
    local_gram = jnp.dot(flattened, flattened.T, precision=lax.Precision.HIGHEST) / rows_all
    radial_gram = lax.psum(local_gram, "rad")
    start_factor = jnp.linalg.cholesky(radial_gram).T
    upper_factor = combined_all(start_factor, "ax", join_factors)
    inverse = upper_inverse(upper_factor)
    basis = jnp.dot(inverse.T, flattened, precision=lax.Precision.HIGHEST).reshape(field_now.shape)
    return (basis, upper_factor)


def solution(mesh):
    return jax.shard_map(
        per_device,
        mesh=mesh,
        in_specs=(
            P(None, None, "ax", "rad"),
            P("ax", "rad"),
            P("ax", "rad"),
            P(None, None, "ax", "rad"),
            P(),
        ),
        out_specs=(P(None, None, "ax", "rad"), P()),
        check_vma=False,
    )
```

profile of v0, /device:TPU:0, one launch (start us, length us, event | category | flops | bytes accessed | tf_op | source)
XLA Modules:
  0.0 470.0 jit_solution(13325855620133303022)
XLA Ops:
  2.8 4.6 collective-permute-start.1
  9.4 4.3 copy.227
  19.7 3.5 pad_maximum_fusion
  23.2 3.1 copy-done.1
  27.6 3.0 collective-permute-start.3
  35.9 6.5 %copy.229 = f32[32,5,20,128]{3,0,2,1:T(8,128)} copy(f32[32,5,20,128]{0,2,3,1:T(8,128)} %copy-done.1) | data formatting | bytes 3276800 | tf_op jit(solution)/shard_map/concatenate | solution.py:21
  46.1 8.8 %multiply_add_fusion.7 = (f32[32,5,16,128]{3,0,2,1:T(8,128)S(1)}, f32[32,5,16,128]{3,0,2,1:T(8,128)}) fusion(f32[32,5,16,128]{3,2,1,0:T(8,128)S(1)} %copy-done, f32[32,16,128]{2,0,1:T(8,128)} %copy.238, f32[5,16,128]{2,1,0:T(8,128)S(1)} %get-tuple-element.336, f32[32,16,128]{2,0,1:T(8,128)} %copy.237, f32[5,16,128]{2,1,0:T(8,128)S(1)} %get-tuple-element.337, ...), kind=kLoop, calls=%fused_computation.117 | loop fusion | flops 12779520 | bytes 12396564 | tf_op jit(solution)/shard_map/add | solution.py:91
  56.3 5.2 %collective-permute-start.5 = (f32[32,5,2,128]{3,0,2,1:T(8,128)S(1)}, f32[32,5,2,128]{3,0,2,1:T(8,128)S(1)}, u32[]{:S(2)}, u32[]{:S(2)}) collective-permute-start(f32[32,5,2,128]{3,0,2,1:T(8,128)S(1)} %get-tuple-element.322), channel_id=1, source_target_pairs={{0,8},{8,16},{16,24},{24,32},{32,40},{40,48},{48,56},{56,64},{64,7... | collective-permute-start | bytes 491528 | tf_op jit(solution)/shard_map/ppermute | solution.py:19
  75.1 3.7 collective-permute-start.7
  85.2 9.3 %multiply_add_fusion.6 = f32[32,5,16,128]{3,0,2,1:T(8,128)S(1)} fusion(f32[32,5,16,128]{3,0,2,1:T(8,128)} %get-tuple-element.276, f32[32,5,16,128]{3,0,2,1:T(8,128)} %copy-done.2, f32[32,5,20,2]{3,0,2,1:T(8,128)} %copy.241, f32[32,5,2,128]{3,0,2,1:T(8,128)} %copy-done.7, f32[32,5,2,128]{3,0,2,1:T(8,128)} %copy-done.11, f32[32,5,20,2]{3,0,2,1:T(8,128)} %copy.243, ...), kind=kLoop, calls=%fused_computation.116 | loop fusion | flops 17039360 | bytes 7153684 | tf_op jit(solution)/shard_map/add | solution.py:93
  95.8 5.2 %collective-permute-start.9 = (f32[32,5,2,128]{3,0,2,1:T(8,128)S(1)}, f32[32,5,2,128]{3,0,2,1:T(8,128)S(1)}, u32[]{:S(2)}, u32[]{:S(2)}) collective-permute-start(f32[32,5,2,128]{3,0,2,1:T(8,128)S(1)} %get-tuple-element.310), channel_id=1, source_target_pairs={{0,8},{8,16},{16,24},{24,32},{32,40},{40,48},{48,56},{56,64},{64,7... | collective-permute-start | bytes 491528 | tf_op jit(solution)/shard_map/ppermute | solution.py:19
  113.9 3.0 collective-permute-start.11
  121.5 5.9 %multiply_add_fusion.4 = (f32[32,5,16,128]{3,0,2,1:T(8,128)S(1)}, f32[32,5,16,128]{3,0,2,1:T(8,128)}) fusion(f32[32,5,16,128]{3,0,2,1:T(8,128)S(1)} %multiply_add_fusion.6, f32[32,16,128]{2,0,1:T(8,128)} %get-tuple-element.316, f32[5,16,128]{2,1,0:T(8,128)S(1)} %get-tuple-element.336, f32[32,16,128]{2,0,1:T(8,128)S(1)} %get-tuple-element.313, ...), kind=kLoop, calls=%fused_computation.114 | loop fusion | flops 16711680 | bytes 5842964 | tf_op jit(solution)/shard_map/add | solution.py:91
  128.7 5.0 %collective-permute-start.13 = (f32[32,5,2,128]{3,0,2,1:T(8,128)S(1)}, f32[32,5,2,128]{3,0,2,1:T(8,128)S(1)}, u32[]{:S(2)}, u32[]{:S(2)}) collective-permute-start(f32[32,5,2,128]{3,0,2,1:T(8,128)S(1)} %get-tuple-element.308), channel_id=1, source_target_pairs={{0,8},{8,16},{16,24},{24,32},{32,40},{40,48},{48,56},{56,64},{64,7... | collective-permute-start | bytes 491528 | tf_op jit(solution)/shard_map/ppermute | solution.py:19
  147.4 3.7 collective-permute-start.15
  157.5 9.2 %multiply_add_fusion.3 = f32[32,5,16,128]{3,0,2,1:T(8,128)S(1)} fusion(f32[32,5,16,128]{3,0,2,1:T(8,128)S(1)} %multiply_add_fusion.6, f32[32,5,16,128]{3,0,2,1:T(8,128)} %get-tuple-element.274, f32[32,5,16,128]{3,0,2,1:T(8,128)} %copy-done.3, f32[32,5,20,2]{3,0,2,1:T(8,128)} %copy.250, f32[32,5,2,128]{3,0,2,1:T(8,128)} %copy-done.6, ...), kind=kLoop, calls=%fused_computation.113 | loop fusion | flops 17039360 | bytes 7153684 | tf_op jit(solution)/shard_map/add | solution.py:93
  168.1 5.0 %collective-permute-start.17 = (f32[32,5,2,128]{3,0,2,1:T(8,128)S(1)}, f32[32,5,2,128]{3,0,2,1:T(8,128)S(1)}, u32[]{:S(2)}, u32[]{:S(2)}) collective-permute-start(f32[32,5,2,128]{3,0,2,1:T(8,128)S(1)} %get-tuple-element.296), channel_id=1, source_target_pairs={{0,8},{8,16},{16,24},{24,32},{32,40},{40,48},{48,56},{56,64},{64,7... | collective-permute-start | bytes 491528 | tf_op jit(solution)/shard_map/ppermute | solution.py:19
  185.1 3.2 collective-permute-start.19
  193.9 5.9 %multiply_add_fusion.1 = (f32[32,5,16,128]{3,0,2,1:T(8,128)S(1)}, f32[32,5,16,128]{3,0,2,1:T(8,128)}) fusion(f32[32,5,16,128]{3,0,2,1:T(8,128)S(1)} %multiply_add_fusion.3, f32[32,16,128]{2,0,1:T(8,128)} %get-tuple-element.302, f32[5,16,128]{2,1,0:T(8,128)S(1)} %get-tuple-element.336, f32[32,16,128]{2,0,1:T(8,128)S(1)} %get-tuple-element.299, ...), kind=kLoop, calls=%fused_computation.111 | loop fusion | flops 16711680 | bytes 5842964 | tf_op jit(solution)/shard_map/add | solution.py:91
  201.7 6.8 %collective-permute-start.21 = (f32[32,5,2,128]{3,0,2,1:T(8,128)S(1)}, f32[32,5,2,128]{3,0,2,1:T(8,128)S(1)}, u32[]{:S(2)}, u32[]{:S(2)}) collective-permute-start(f32[32,5,2,128]{3,0,2,1:T(8,128)S(1)} %get-tuple-element.294), channel_id=1, source_target_pairs={{0,8},{8,16},{16,24},{24,32},{32,40},{40,48},{48,56},{56,64},{64,7... | collective-permute-start | bytes 491528 | tf_op jit(solution)/shard_map/ppermute | solution.py:19
  222.0 3.7 collective-permute-start.23
  232.1 5.3 %multiply_add_fusion = f32[32,5,16,128]{3,0,2,1:T(8,128)S(1)} fusion(f32[32,5,16,128]{3,0,2,1:T(8,128)S(1)} %multiply_add_fusion.3, f32[32,5,16,128]{3,0,2,1:T(8,128)} %get-tuple-element.272, f32[32,5,16,128]{3,0,2,1:T(8,128)S(1)} %get-tuple-element.271, f32[32,5,20,2]{3,0,2,1:T(8,128)} %copy.258, f32[32,5,2,128]{3,0,2,1:T(8,128)} %copy-done.4, ...), kind=kLoop, calls=%fused_computation.110 | loop fusion | flops 17039360 | bytes 7153684 | tf_op jit(solution)/shard_map/add | solution.py:93
  239.3 24.5 %psum.7 = f32[32,32]{0,1:T(8,128)S(1)} all-reduce(f32[32,32]{0,1:T(8,128)S(1)} %fusion.18), channel_id=1, replica_groups=mesh['ax'=16,'rad'=8] {'rad'}, use_global_device_ids=true, to_apply=%region_0.0 | all-reduce | flops 1024 | bytes 8192 | tf_op jit(solution)/shard_map/psum | solution.py:97
  268.3 36.5 %all-gather = f32[512,32]{1,0:T(8,128)S(1)} all-gather(f32[32,32]{1,0:T(8,128)S(1)} %copy.263), channel_id=2, replica_groups=mesh['ax'=16,'rad'=8] {'ax'}, dimensions={0}, use_global_device_ids=true | all-gather | bytes 69632 | tf_op jit(solution)/shard_map/all_gather | solution.py:26
  304.8 70.9 %while.30 = (s32[]{:T(128)}, f32[32,32]{0,1:T(8,128)S(1)}, f32[16,32,32]{2,1,0:T(8,128)S(1)}, s32[]{:T(128)}, s32[]{:T(128)}, /*index=5*/s32[]{:T(128)}) while((s32[]{:T(128)}, f32[32,32]{0,1:T(8,128)S(1)}, f32[16,32,32]{2,1,0:T(8,128)S(1)}, s32[]{:T(128)}, s32[]{:T(128)}, /*index=5*/s32[]{:T(128)}) %tuple.141), condition=%wide.region_4.6_spmd, body=%wide.region_3.5_spmd.sunk | while | flops 795684 | bytes 78197 | solution.py:32
  305.3 2.9 cholesky.109
  310.0 2.9 cholesky.109
  314.8 2.9 cholesky.109
  329.0 2.9 cholesky.109
  343.1 2.9 cholesky.109
  362.1 2.9 cholesky.109
  375.9 90.0 %while.31 = (s32[]{:T(128)}, f32[32,32]{1,0:T(8,128)S(1)}, f32[32,32]{1,0:T(8,128)}, f32[32,32]{1,0:T(8,128)S(1)}, s32[]{:T(128)}, /*index=5*/s32[]{:T(128)}, s32[]{:T(128)}, s32[]{:T(128)}) while((s32[]{:T(128)}, f32[32,32]{1,0:T(8,128)S(1)}, f32[32,32]{1,0:T(8,128)}, f32[32,32]{1,0:T(8,128)S(1)}, s32[]{:T(128)}, /*index=5*/s32[]{:T(128)}, ...), condition=%wide.region_7.9_spmd, body=%wide.region_5.8_spmd.sunk | while | flops 12421 | bytes 18835 | solution.py:72
  (371 shorter events, 275.0 us)
Async XLA Ops:
  0.6 8.7 %copy-start = (f32[32,5,16,128]{3,2,1,0:T(8,128)S(1)}, f32[32,5,16,128]{3,2,1,0:T(8,128)}, u32[]{:S(2)}) copy-start(f32[32,5,16,128]{3,2,1,0:T(8,128)} %param.10) | copy-start | bytes 3932164
  2.8 14.4 %collective-permute-start.1 = (f32[32,5,2,128]{3,0,2,1:T(8,128)}, f32[32,5,2,128]{3,0,2,1:T(8,128)}, u32[]{:S(2)}, u32[]{:S(2)}) collective-permute-start(f32[32,5,2,128]{3,0,2,1:T(8,128)} %copy.298), channel_id=1, source_target_pairs={{0,8},{8,16},{16,24},{24,32},{32,40},{40,48},{48,56},{56,64},{64,7... | collective-permute-start | bytes 491528 | tf_op jit(solution)/shard_map/ppermute | solution.py:19
  8.1 10.4 %collective-permute-start = (f32[32,5,2,128]{3,0,2,1:T(8,128)}, f32[32,5,2,128]{3,0,2,1:T(8,128)}, u32[]{:S(2)}, u32[]{:S(2)}) collective-permute-start(f32[32,5,2,128]{3,0,2,1:T(8,128)} %copy.297), channel_id=1, source_target_pairs={{8,0},{16,8},{24,16},{32,24},{40,32},{48,40},{56,48},{64,56},{72,6... | collective-permute-start | bytes 491528 | tf_op jit(solution)/shard_map/ppermute | solution.py:20
  17.2 28.9 %copy-start.16 = (f32[5]{0:T(128)}, f32[5]{0:T(128)S(1)}, u32[]{:S(2)}) copy-start(f32[5]{0:T(128)S(1)} %broadcast_multiply_fusion.1) | copy-start | bytes 64
  23.2 3.1 copy-start.1
  26.3 16.1 %collective-permute-start.2 = (f32[32,5,20,2]{0,2,3,1:T(8,128)S(1)}, f32[32,5,20,2]{0,2,3,1:T(8,128)S(1)}, u32[]{:S(2)}, u32[]{:S(2)}) collective-permute-start(f32[32,5,20,2]{0,2,3,1:T(8,128)S(1)} %get-tuple-element.277), channel_id=1, source_target_pairs={{1,0},{2,1},{3,2},{4,3},{5,4},{6,5},{7,6},{9,8},{10,9},{11,10},{12... | collective-permute-start | bytes 76808 | tf_op jit(solution)/shard_map/ppermute | solution.py:20
  27.6 16.7 %collective-permute-start.3 = (f32[32,5,20,2]{0,2,3,1:T(8,128)S(1)}, f32[32,5,20,2]{0,2,3,1:T(8,128)S(1)}, u32[]{:S(2)}, u32[]{:S(2)}) collective-permute-start(f32[32,5,20,2]{0,2,3,1:T(8,128)S(1)} %get-tuple-element.278), channel_id=1, source_target_pairs={{0,1},{1,2},{2,3},{3,4},{4,5},{5,6},{6,7},{8,9},{9,10},{10,11},{11... | collective-permute-start | bytes 76808 | tf_op jit(solution)/shard_map/ppermute | solution.py:19
  54.9 23.8 %copy-start.2 = (f32[32,5,16,128]{3,0,2,1:T(8,128)}, f32[32,5,16,128]{3,0,2,1:T(8,128)S(1)}, u32[]{:S(2)}) copy-start(f32[32,5,16,128]{3,0,2,1:T(8,128)S(1)} %get-tuple-element.275) | copy-start | bytes 3932164
  55.0 9.2 %collective-permute-start.4 = (f32[32,5,2,128]{3,0,2,1:T(8,128)S(1)}, f32[32,5,2,128]{3,0,2,1:T(8,128)S(1)}, u32[]{:S(2)}, u32[]{:S(2)}) collective-permute-start(f32[32,5,2,128]{3,0,2,1:T(8,128)S(1)} %get-tuple-element.323), channel_id=1, source_target_pairs={{8,0},{16,8},{24,16},{32,24},{40,32},{48,40},{56,48},{64,56},{72,6... | collective-permute-start | bytes 491528 | tf_op jit(solution)/shard_map/ppermute | solution.py:20
  56.3 9.5 %collective-permute-start.5 = (f32[32,5,2,128]{3,0,2,1:T(8,128)S(1)}, f32[32,5,2,128]{3,0,2,1:T(8,128)S(1)}, u32[]{:S(2)}, u32[]{:S(2)}) collective-permute-start(f32[32,5,2,128]{3,0,2,1:T(8,128)S(1)} %get-tuple-element.322), channel_id=1, source_target_pairs={{0,8},{8,16},{16,24},{24,32},{32,40},{40,48},{48,56},{56,64},{64,7... | collective-permute-start | bytes 491528 | tf_op jit(solution)/shard_map/ppermute | solution.py:19
  70.9 8.8 %collective-permute-start.6 = (f32[32,5,20,2]{0,2,3,1:T(8,128)S(1)}, f32[32,5,20,2]{0,2,3,1:T(8,128)}, u32[]{:S(2)}, u32[]{:S(2)}) collective-permute-start(f32[32,5,20,2]{0,2,3,1:T(8,128)S(1)} %copy.277), channel_id=1, source_target_pairs={{1,0},{2,1},{3,2},{4,3},{5,4},{6,5},{7,6},{9,8},{10,9},{11,10},{12... | collective-permute-start | bytes 76808 | tf_op jit(solution)/shard_map/ppermute | solution.py:20
  75.1 7.4 %collective-permute-start.7 = (f32[32,5,20,2]{0,2,3,1:T(8,128)}, f32[32,5,20,2]{0,2,3,1:T(8,128)}, u32[]{:S(2)}, u32[]{:S(2)}) collective-permute-start(f32[32,5,20,2]{0,2,3,1:T(8,128)} %copy.278), channel_id=1, source_target_pairs={{0,1},{1,2},{2,3},{3,4},{4,5},{5,6},{6,7},{8,9},{9,10},{10,11},{11... | collective-permute-start | bytes 76808 | tf_op jit(solution)/shard_map/ppermute | solution.py:19
  82.5 2.7 copy-start.17
  94.5 9.4 %collective-permute-start.8 = (f32[32,5,2,128]{3,0,2,1:T(8,128)S(1)}, f32[32,5,2,128]{3,0,2,1:T(8,128)S(1)}, u32[]{:S(2)}, u32[]{:S(2)}) collective-permute-start(f32[32,5,2,128]{3,0,2,1:T(8,128)S(1)} %get-tuple-element.311), channel_id=1, source_target_pairs={{8,0},{16,8},{24,16},{32,24},{40,32},{48,40},{56,48},{64,56},{72,6... | collective-permute-start | bytes 491528 | tf_op jit(solution)/shard_map/ppermute | solution.py:20
  95.8 9.3 %collective-permute-start.9 = (f32[32,5,2,128]{3,0,2,1:T(8,128)S(1)}, f32[32,5,2,128]{3,0,2,1:T(8,128)S(1)}, u32[]{:S(2)}, u32[]{:S(2)}) collective-permute-start(f32[32,5,2,128]{3,0,2,1:T(8,128)S(1)} %get-tuple-element.310), channel_id=1, source_target_pairs={{0,8},{8,16},{16,24},{24,32},{32,40},{40,48},{48,56},{56,64},{64,7... | collective-permute-start | bytes 491528 | tf_op jit(solution)/shard_map/ppermute | solution.py:19
  110.4 7.5 %collective-permute-start.10 = (f32[32,5,20,2]{0,2,3,1:T(8,128)S(1)}, f32[32,5,20,2]{0,2,3,1:T(8,128)S(1)}, u32[]{:S(2)}, u32[]{:S(2)}) collective-permute-start(f32[32,5,20,2]{0,2,3,1:T(8,128)S(1)} %copy.279), channel_id=1, source_target_pairs={{1,0},{2,1},{3,2},{4,3},{5,4},{6,5},{7,6},{9,8},{10,9},{11,10},{12... | collective-permute-start | bytes 76808 | tf_op jit(solution)/shard_map/ppermute | solution.py:20
  113.9 5.8 %collective-permute-start.11 = (f32[32,5,20,2]{0,2,3,1:T(8,128)S(1)}, f32[32,5,20,2]{0,2,3,1:T(8,128)S(1)}, u32[]{:S(2)}, u32[]{:S(2)}) collective-permute-start(f32[32,5,20,2]{0,2,3,1:T(8,128)S(1)} %copy.280), channel_id=1, source_target_pairs={{0,1},{1,2},{2,3},{3,4},{4,5},{5,6},{6,7},{8,9},{9,10},{10,11},{11... | collective-permute-start | bytes 76808 | tf_op jit(solution)/shard_map/ppermute | solution.py:19
  127.4 23.7 %copy-start.3 = (f32[32,5,16,128]{3,0,2,1:T(8,128)}, f32[32,5,16,128]{3,0,2,1:T(8,128)S(1)}, u32[]{:S(2)}) copy-start(f32[32,5,16,128]{3,0,2,1:T(8,128)S(1)} %get-tuple-element.273) | copy-start | bytes 3932164
  127.4 9.0 %collective-permute-start.12 = (f32[32,5,2,128]{3,0,2,1:T(8,128)S(1)}, f32[32,5,2,128]{3,0,2,1:T(8,128)S(1)}, u32[]{:S(2)}, u32[]{:S(2)}) collective-permute-start(f32[32,5,2,128]{3,0,2,1:T(8,128)S(1)} %get-tuple-element.309), channel_id=1, source_target_pairs={{8,0},{16,8},{24,16},{32,24},{40,32},{48,40},{56,48},{64,56},{72,6... | collective-permute-start | bytes 491528 | tf_op jit(solution)/shard_map/ppermute | solution.py:20
  128.7 9.4 %collective-permute-start.13 = (f32[32,5,2,128]{3,0,2,1:T(8,128)S(1)}, f32[32,5,2,128]{3,0,2,1:T(8,128)S(1)}, u32[]{:S(2)}, u32[]{:S(2)}) collective-permute-start(f32[32,5,2,128]{3,0,2,1:T(8,128)S(1)} %get-tuple-element.308), channel_id=1, source_target_pairs={{0,8},{8,16},{16,24},{24,32},{32,40},{40,48},{48,56},{56,64},{64,7... | collective-permute-start | bytes 491528 | tf_op jit(solution)/shard_map/ppermute | solution.py:19
  143.2 8.8 %collective-permute-start.14 = (f32[32,5,20,2]{0,2,3,1:T(8,128)S(1)}, f32[32,5,20,2]{0,2,3,1:T(8,128)}, u32[]{:S(2)}, u32[]{:S(2)}) collective-permute-start(f32[32,5,20,2]{0,2,3,1:T(8,128)S(1)} %copy.281), channel_id=1, source_target_pairs={{1,0},{2,1},{3,2},{4,3},{5,4},{6,5},{7,6},{9,8},{10,9},{11,10},{12... | collective-permute-start | bytes 76808 | tf_op jit(solution)/shard_map/ppermute | solution.py:20
  147.4 7.4 %collective-permute-start.15 = (f32[32,5,20,2]{0,2,3,1:T(8,128)}, f32[32,5,20,2]{0,2,3,1:T(8,128)}, u32[]{:S(2)}, u32[]{:S(2)}) collective-permute-start(f32[32,5,20,2]{0,2,3,1:T(8,128)} %copy.282), channel_id=1, source_target_pairs={{0,1},{1,2},{2,3},{3,4},{4,5},{5,6},{6,7},{8,9},{9,10},{10,11},{11... | collective-permute-start | bytes 76808 | tf_op jit(solution)/shard_map/ppermute | solution.py:19
  154.8 2.7 copy-start.18
  166.8 9.1 %collective-permute-start.16 = (f32[32,5,2,128]{3,0,2,1:T(8,128)S(1)}, f32[32,5,2,128]{3,0,2,1:T(8,128)S(1)}, u32[]{:S(2)}, u32[]{:S(2)}) collective-permute-start(f32[32,5,2,128]{3,0,2,1:T(8,128)S(1)} %get-tuple-element.297), channel_id=1, source_target_pairs={{8,0},{16,8},{24,16},{32,24},{40,32},{48,40},{56,48},{64,56},{72,6... | collective-permute-start | bytes 491528 | tf_op jit(solution)/shard_map/ppermute | solution.py:20
  168.1 9.5 %collective-permute-start.17 = (f32[32,5,2,128]{3,0,2,1:T(8,128)S(1)}, f32[32,5,2,128]{3,0,2,1:T(8,128)S(1)}, u32[]{:S(2)}, u32[]{:S(2)}) collective-permute-start(f32[32,5,2,128]{3,0,2,1:T(8,128)S(1)} %get-tuple-element.296), channel_id=1, source_target_pairs={{0,8},{8,16},{16,24},{24,32},{32,40},{40,48},{48,56},{56,64},{64,7... | collective-permute-start | bytes 491528 | tf_op jit(solution)/shard_map/ppermute | solution.py:19
  182.4 6.9 %collective-permute-start.18 = (f32[32,5,20,2]{0,2,3,1:T(8,128)S(1)}, f32[32,5,20,2]{0,2,3,1:T(8,128)}, u32[]{:S(2)}, u32[]{:S(2)}) collective-permute-start(f32[32,5,20,2]{0,2,3,1:T(8,128)S(1)} %copy.283), channel_id=1, source_target_pairs={{1,0},{2,1},{3,2},{4,3},{5,4},{6,5},{7,6},{9,8},{10,9},{11,10},{12... | collective-permute-start | bytes 76808 | tf_op jit(solution)/shard_map/ppermute | solution.py:20
  185.1 6.9 %collective-permute-start.19 = (f32[32,5,20,2]{0,2,3,1:T(8,128)}, f32[32,5,20,2]{0,2,3,1:T(8,128)S(1)}, u32[]{:S(2)}, u32[]{:S(2)}) collective-permute-start(f32[32,5,20,2]{0,2,3,1:T(8,128)} %copy.284), channel_id=1, source_target_pairs={{0,1},{1,2},{2,3},{3,4},{4,5},{5,6},{6,7},{8,9},{9,10},{10,11},{11... | collective-permute-start | bytes 76808 | tf_op jit(solution)/shard_map/ppermute | solution.py:19
  200.4 10.7 %collective-permute-start.20 = (f32[32,5,2,128]{3,0,2,1:T(8,128)}, f32[32,5,2,128]{3,0,2,1:T(8,128)S(1)}, u32[]{:S(2)}, u32[]{:S(2)}) collective-permute-start(f32[32,5,2,128]{3,0,2,1:T(8,128)} %get-tuple-element.295), channel_id=1, source_target_pairs={{8,0},{16,8},{24,16},{32,24},{40,32},{48,40},{56,48},{64,56},{72,6... | collective-permute-start | bytes 491528 | tf_op jit(solution)/shard_map/ppermute | solution.py:20
  201.7 11.0 %collective-permute-start.21 = (f32[32,5,2,128]{3,0,2,1:T(8,128)S(1)}, f32[32,5,2,128]{3,0,2,1:T(8,128)S(1)}, u32[]{:S(2)}, u32[]{:S(2)}) collective-permute-start(f32[32,5,2,128]{3,0,2,1:T(8,128)S(1)} %get-tuple-element.294), channel_id=1, source_target_pairs={{0,8},{8,16},{16,24},{24,32},{32,40},{40,48},{48,56},{56,64},{64,7... | collective-permute-start | bytes 491528 | tf_op jit(solution)/shard_map/ppermute | solution.py:19
  217.9 8.7 %collective-permute-start.22 = (f32[32,5,20,2]{0,2,3,1:T(8,128)S(1)}, f32[32,5,20,2]{0,2,3,1:T(8,128)}, u32[]{:S(2)}, u32[]{:S(2)}) collective-permute-start(f32[32,5,20,2]{0,2,3,1:T(8,128)S(1)} %copy.285), channel_id=1, source_target_pairs={{1,0},{2,1},{3,2},{4,3},{5,4},{6,5},{7,6},{9,8},{10,9},{11,10},{12... | collective-permute-start | bytes 76808 | tf_op jit(solution)/shard_map/ppermute | solution.py:20
  222.0 7.4 %collective-permute-start.23 = (f32[32,5,20,2]{0,2,3,1:T(8,128)}, f32[32,5,20,2]{0,2,3,1:T(8,128)}, u32[]{:S(2)}, u32[]{:S(2)}) collective-permute-start(f32[32,5,20,2]{0,2,3,1:T(8,128)} %copy.286), channel_id=1, source_target_pairs={{0,1},{1,2},{2,3},{3,4},{4,5},{5,6},{6,7},{8,9},{9,10},{10,11},{11... | collective-permute-start | bytes 76808 | tf_op jit(solution)/shard_map/ppermute | solution.py:19
  229.4 2.7 copy-start.20
  (16 other events, 22.7 us)
where the time goes:
time: 474 us; the launch traced here: 470 us
  other arithmetic  159 us (34%)
  local copies, waits for them, and re-layouts  104 us (22%)
  starting transfers between devices  67.7 us (14%)
  blocking collectives  61 us (13%)
  matrix products  54.9 us (12%)
  waiting for transfers between devices  20.9 us (4%)
    another operation x45, other arithmetic, join_factors(): return jnp.linalg.cholesky(summed).T  53.9 us
    ppermute x12, starting transfers between devices, padded_2(): before = lax.ppermute(last, axis, up)  52.2 us
    dot_general x32, matrix products, one_row(): jnp.dot(factor_row, inverse, precision=lax.Precision.HIGHEST)  46.9 us
    unnamed x66, local copies, waits for them, and re-layouts  41.9 us
    reduce_sum x32, other arithmetic, one_row(): pivot = jnp.sum(factor_row * unit_row)  41.6 us
    all_gather x1, blocking collectives, combined_all(): everything = lax.all_gather(shard, axis)  36.5 us
    psum x1, blocking collectives, per_device(): radial_gram = lax.psum(local_gram, 'rad')  24.5 us
    add x3, other arithmetic, per_device(): field_now = field_now + 0.5 * time_step * (slope_one + slope_two)  23.8 us
  transfers between devices with their start and end apart: 24, of which 10 were waited for; matrix products, arithmetic and copies ran while one was open for 11% of the time, Pallas kernels for 0%

commit v1 on v0

--- a/solution.py
+++ b/solution.py
@@ -1,6 +1,10 @@
+import functools
+
 import jax
 import jax.numpy as jnp
 from jax import lax
+from jax.experimental import pallas as pl
+from jax.experimental.pallas import tpu as pltpu
 from jax.sharding import PartitionSpec as P
 
 STEPS = 3
@@ -20,16 +24,6 @@
         after = lax.ppermute(initial, axis, down)
         shard = jnp.concatenate([before, shard, after], axis=dim)
     return shard
-
-
-def combined_all(shard, axis, combine):
-    everything = lax.all_gather(shard, axis)
-    initial = everything[0]
-
-    def turn(k, so_far):
-        return combine(so_far, everything[k])
-
-    return lax.fori_loop(1, lax.axis_size(axis), turn, initial)
 
 
 def operate(padded, vel_axial, vel_radial, coupling, viscosity):
@@ -57,30 +51,37 @@
     return result
 
 
-def upper_inverse(upper_factor):
-    order = upper_factor.shape[0]
-    identity = jnp.eye(order, dtype=jnp.float32)
+def factor_kernel(parts_ref, factor_ref, inverse_ref, *, rows_all):
+    total = jnp.sum(parts_ref[...], axis=0) * (1.0 / rows_all)
+    order = factor_ref.shape[0]
+    lane = lax.broadcasted_iota(jnp.int32, (order, 128), 1)
+    row = lax.broadcasted_iota(jnp.int32, (order, 128), 0)
+    pieces = [total] + [pltpu.roll(total, 128 - 32 * i, axis=1) for i in range(1, 4)]
+    work = jnp.concatenate(pieces, axis=0)
+    work = jnp.where(lane < order, work, jnp.where(lane == row + order, 1.0, 0.0))
+    for j in range(order - 1):
+        pivot_row = work[j : j + 1, :]
+        scale = pivot_row / pivot_row[:, j : j + 1]
+        column = jnp.where(row > j, jnp.broadcast_to(work[:, j : j + 1], work.shape), 0.0)
+        work = work - column * scale
+    diagonal = jnp.sum(jnp.where(lane == row, work, 0.0), axis=1, keepdims=True)
+    work = work / jnp.sqrt(diagonal)
+    factor_ref[...] = jnp.where(lane >= row, work, 0.0)[:, :order]
+    inverse_ref[...] = jnp.where(lane <= row, pltpu.roll(work, 128 - order, axis=1), 0.0)[:, :order]
 
-    def one_row(count, inverse):
-        row_index = order - 1 - count
-        factor_row = lax.dynamic_slice_in_dim(upper_factor, row_index, 1, 0)
-        unit_row = lax.dynamic_slice_in_dim(identity, row_index, 1, 0)
-        pivot = jnp.sum(factor_row * unit_row)
-        new_row = (unit_row - jnp.dot(factor_row, inverse, precision=lax.Precision.HIGHEST)) / pivot
-        return lax.dynamic_update_slice_in_dim(inverse, new_row, row_index, 0)
 
-    return lax.fori_loop(0, order, one_row, jnp.zeros((order, order), jnp.float32))
+def factor_and_inverse(parts, order, rows_all):
+    square = jax.ShapeDtypeStruct((order, order), jnp.float32)
+    return pl.pallas_call(
+        functools.partial(factor_kernel, rows_all=rows_all),
+        out_shape=(square, square),
+        name="factor",
+    )(parts)
 
 
 def rim_operator(field_now, vel_axial, vel_radial, coupling, viscosity):
     padded = padded_2(field_now, (("ax", 2), ("rad", 3)), 2)
     return operate(padded, vel_axial, vel_radial, coupling, viscosity)
-
-
-def join_factors(first_factor, other_factor):
-    summed = jnp.dot(first_factor.T, first_factor, precision=lax.Precision.HIGHEST)
-    summed = summed + jnp.dot(other_factor.T, other_factor, precision=lax.Precision.HIGHEST)
-    return jnp.linalg.cholesky(summed).T
 
 
 def per_device(forcing, vel_axial, vel_radial, coupling, viscosity):
@@ -93,12 +94,13 @@
         field_now = field_now + 0.5 * time_step * (slope_one + slope_two)
     flattened = field_now.reshape(vectors, variables * axial_cells * radial_cells)
     rows_all = variables * axial_cells * radial_cells * lax.axis_size("ax") * lax.axis_size("rad")
-    local_gram = jnp.dot(flattened, flattened.T, precision=lax.Precision.HIGHEST) / rows_all
-    radial_gram = lax.psum(local_gram, "rad")
-    start_factor = jnp.linalg.cholesky(radial_gram).T
-    upper_factor = combined_all(start_factor, "ax", join_factors)
-    inverse = upper_inverse(upper_factor)
-    basis = jnp.dot(inverse.T, flattened, precision=lax.Precision.HIGHEST).reshape(field_now.shape)
+    local_gram = jnp.dot(flattened, flattened.T, precision=lax.Precision.HIGHEST)
+    packed = jnp.concatenate([local_gram[8 * i : 8 * i + 8] for i in range(4)], axis=1)
+    devices = lax.axis_size("ax") * lax.axis_size("rad")
+    copies = jnp.broadcast_to(packed, (devices, 8, 128))
+    parts = lax.all_to_all(copies, ("ax", "rad"), 0, 0)
+    upper_factor, lower_inverse = factor_and_inverse(parts, vectors, rows_all)
+    basis = jnp.dot(lower_inverse, flattened, precision=lax.Precision.HIGHEST).reshape(field_now.shape)
     return (basis, upper_factor)
 
 

time: 474 us -> 283 us (0.60)
  other arithmetic: 159 us -> 49.1 us
  blocking collectives: 61 us -> 0 us
  matrix products: 54.9 us -> 3.35 us
  starting transfers between devices: 67.7 us -> 86.8 us
  waiting for transfers between devices: 20.9 us -> 33.4 us
    another operation x48 -> x0, other arithmetic: 57.5 us -> none  [the longest x45 53.9 us: join_factors(): return jnp.linalg.cholesky(summed).T]
    dot_general x64 -> x2, matrix products: 54.9 us -> 3.35 us  [the longest x1 2.19 us: per_device(): jnp.dot(lower_inverse, flattened, precision=lax.Precision.HIGHEST)]
    reduce_sum x32 -> x0, other arithmetic: 41.6 us -> none  [one_row(): pivot = jnp.sum(factor_row * unit_row)]
    all_gather x1 -> x0, blocking collectives: 36.5 us -> none  [combined_all(): everything = lax.all_gather(shard, axis)]
    psum x1 -> x0, blocking collectives: 24.5 us -> none  [per_device(): radial_gram = lax.psum(local_gram, 'rad')]
    all_to_all x0 -> x1, starting transfers between devices: none -> 19 us  [per_device(): parts = lax.all_to_all(copies, ('ax', 'rad'), 0, 0)]
    all_to_all x0 -> x1, waiting for transfers between devices: none -> 11.9 us  [per_device(): parts = lax.all_to_all(copies, ('ax', 'rad'), 0, 0)]
    transpose x16 -> x0, other arithmetic: 10.4 us -> none  [the longest x15 9.74 us: join_factors(): return jnp.linalg.cholesky(summed).T]
  transfers between devices with their start and end apart: 24 -> 25, of which waited for: 10 -> 11; matrix products, arithmetic and copies ran while one was open for 11% -> 19% of each run, Pallas kernels for 0% -> 0%
where the time goes in v1:
time: 283 us; the launch traced here: 281 us
  local copies, waits for them, and re-layouts  103 us (36%)
  starting transfers between devices  86.8 us (31%)
  other arithmetic  49.1 us (17%)
  waiting for transfers between devices  33.4 us (12%)
  Pallas kernels  4.48 us (2%)
  matrix products  3.35 us (1%)
    ppermute x12, starting transfers between devices, padded_2(): before = lax.ppermute(last, axis, up)  52.3 us
    unnamed x70, local copies, waits for them, and re-layouts  42.4 us
    add x3, other arithmetic, per_device(): field_now = field_now + 0.5 * time_step * (slope_one + slope_two)  24.3 us
    add x3, other arithmetic, per_device(): middle = field_now + time_step * slope_one  20.6 us
    all_to_all x1, starting transfers between devices, per_device(): parts = lax.all_to_all(copies, ('ax', 'rad'), 0, 0)  19 us
    ppermute x7, local copies, waits for them, and re-layouts, padded_2(): after = lax.ppermute(initial, axis, down)  15.8 us
    ppermute x12, starting transfers between devices, padded_2(): after = lax.ppermute(initial, axis, down)  15.5 us
    ppermute x7, local copies, waits for them, and re-layouts, padded_2(): before = lax.ppermute(last, axis, up)  14.9 us
  transfers between devices with their start and end apart: 25, of which 11 were waited for; matrix products, arithmetic and copies ran while one was open for 19% of the time, Pallas kernels for 0%

profile of v1, /device:TPU:0, one launch (start us, length us, event | category | flops | bytes accessed | tf_op | source)
XLA Modules:
  0.0 280.9 jit_solution(12881795774040180010)
XLA Ops:
  2.8 4.6 %collective-permute-start.1 = (f32[32,5,2,128]{3,0,2,1:T(8,128)}, f32[32,5,2,128]{3,0,2,1:T(8,128)}, u32[]{:S(2)}, u32[]{:S(2)}) collective-permute-start(f32[32,5,2,128]{3,0,2,1:T(8,128)} %copy.236), channel_id=1, source_target_pairs={{0,8},{8,16},{16,24},{24,32},{32,40},{40,48},{48,56},{56,64},{64,7... | collective-permute-start | bytes 491528 | tf_op jit(solution)/shard_map/ppermute | solution.py:23
  9.4 4.3 %copy.176 = f32[32,5,16,128]{0,2,3,1:T(8,128)} copy(f32[32,5,16,128]{3,2,1,0:T(8,128)S(1)} %copy-done) | data formatting | bytes 2621440 | tf_op args[0]
  19.6 3.5 %pad_maximum_fusion = f32[32,5,20,128]{0,2,3,1:T(8,128)S(1)} fusion(f32[32,5,2,128]{0,2,3,1:T(2,128)S(1)} %copy.177, f32[32,5,16,128]{0,2,3,1:T(8,128)} %copy.176, f32[32,5,2,128]{0,2,3,1:T(2,128)S(1)} %copy.175), kind=kLoop, calls=%fused_computation | loop fusion | flops 819200 | bytes 3276800 | tf_op jit(solution)/shard_map/concatenate | solution.py:25
  23.2 3.1 %copy-done.1 = f32[32,5,20,128]{0,2,3,1:T(8,128)} copy-done((f32[32,5,20,128]{0,2,3,1:T(8,128)}, f32[32,5,20,128]{0,2,3,1:T(8,128)S(1)}, u32[]{:S(2)}) %copy-start.1) | copy-done | bytes 1638424
  27.6 3.0 %collective-permute-start.3 = (f32[32,5,20,2]{0,2,3,1:T(8,128)S(1)}, f32[32,5,20,2]{0,2,3,1:T(8,128)S(1)}, u32[]{:S(2)}, u32[]{:S(2)}) collective-permute-start(f32[32,5,20,2]{0,2,3,1:T(8,128)S(1)} %get-tuple-element.25), channel_id=1, source_target_pairs={{0,1},{1,2},{2,3},{3,4},{4,5},{5,6},{6,7},{8,9},{9,10},{10,11},{11... | collective-permute-start | bytes 76808 | tf_op jit(solution)/shard_map/ppermute | solution.py:23
  35.9 6.5 %copy.178 = f32[32,5,20,128]{3,0,2,1:T(8,128)} copy(f32[32,5,20,128]{0,2,3,1:T(8,128)} %copy-done.1) | data formatting | bytes 3276800 | tf_op jit(solution)/shard_map/concatenate | solution.py:25
  46.1 8.9 %multiply_add_fusion.7 = (f32[32,5,16,128]{3,0,2,1:T(8,128)S(1)}, f32[32,5,16,128]{3,0,2,1:T(8,128)}) fusion(f32[32,5,16,128]{3,2,1,0:T(8,128)S(1)} %copy-done, f32[32,16,128]{2,0,1:T(8,128)} %copy.187, f32[5,16,128]{2,1,0:T(8,128)S(1)} %get-tuple-element.83, f32[32,16,128]{2,0,1:T(8,128)} %copy.186, f32[5,16,128]{2,1,0:T(8,128)S(1)} %get-tuple-element.84, ...), kind=kLoop, calls=%fused_computation.100 | loop fusion | flops 12779520 | bytes 12396564 | tf_op jit(solution)/shard_map/add | solution.py:92
  56.3 5.2 %collective-permute-start.5 = (f32[32,5,2,128]{3,0,2,1:T(8,128)S(1)}, f32[32,5,2,128]{3,0,2,1:T(8,128)S(1)}, u32[]{:S(2)}, u32[]{:S(2)}) collective-permute-start(f32[32,5,2,128]{3,0,2,1:T(8,128)S(1)} %get-tuple-element.69), channel_id=1, source_target_pairs={{0,8},{8,16},{16,24},{24,32},{32,40},{40,48},{48,56},{56,64},{64,7... | collective-permute-start | bytes 491528 | tf_op jit(solution)/shard_map/ppermute | solution.py:23
  72.2 2.9 %copy.216 = f32[32,5,20,2]{0,2,3,1:T(8,128)} copy(f32[32,5,20,2]{3,0,2,1:T(8,128)} %get-tuple-element.34) | data formatting | bytes 51200
  75.1 3.7 %collective-permute-start.7 = (f32[32,5,20,2]{0,2,3,1:T(8,128)}, f32[32,5,20,2]{0,2,3,1:T(8,128)}, u32[]{:S(2)}, u32[]{:S(2)}) collective-permute-start(f32[32,5,20,2]{0,2,3,1:T(8,128)} %copy.216), channel_id=1, source_target_pairs={{0,1},{1,2},{2,3},{3,4},{4,5},{5,6},{6,7},{8,9},{9,10},{10,11},{11... | collective-permute-start | bytes 76808 | tf_op jit(solution)/shard_map/ppermute | solution.py:23
  82.4 2.7 copy.192
  85.2 9.5 %multiply_add_fusion.6 = f32[32,5,16,128]{3,0,2,1:T(8,128)S(1)} fusion(f32[32,5,16,128]{3,0,2,1:T(8,128)} %get-tuple-element.23, f32[32,5,16,128]{3,0,2,1:T(8,128)} %copy-done.2, f32[32,5,20,2]{3,0,2,1:T(8,128)} %copy.190, f32[32,5,2,128]{3,0,2,1:T(8,128)} %copy-done.10, f32[32,5,2,128]{3,0,2,1:T(8,128)} %copy-done.14, f32[32,5,20,2]{3,0,2,1:T(8,128)} %copy.192, ...), kind=kLoop, calls=%fused_computation.99 | loop fusion | flops 17039360 | bytes 7153684 | tf_op jit(solution)/shard_map/add | solution.py:94
  96.0 5.2 %collective-permute-start.9 = (f32[32,5,2,128]{3,0,2,1:T(8,128)S(1)}, f32[32,5,2,128]{3,0,2,1:T(8,128)S(1)}, u32[]{:S(2)}, u32[]{:S(2)}) collective-permute-start(f32[32,5,2,128]{3,0,2,1:T(8,128)S(1)} %get-tuple-element.57), channel_id=1, source_target_pairs={{0,8},{8,16},{16,24},{24,32},{32,40},{40,48},{48,56},{56,64},{64,7... | collective-permute-start | bytes 491528 | tf_op jit(solution)/shard_map/ppermute | solution.py:23
  101.2 2.9 %collective-permute-done.8 = f32[32,5,2,128]{3,0,2,1:T(8,128)S(1)} collective-permute-done((f32[32,5,2,128]{3,0,2,1:T(8,128)S(1)}, f32[32,5,2,128]{3,0,2,1:T(8,128)S(1)}, u32[]{:S(2)}, u32[]{:S(2)}) %collective-permute-start.8) | collective-permute-done | bytes 163872 | tf_op jit(solution)/shard_map/ppermute | solution.py:24
  114.0 3.0 %collective-permute-start.11 = (f32[32,5,20,2]{0,2,3,1:T(8,128)S(1)}, f32[32,5,20,2]{0,2,3,1:T(8,128)S(1)}, u32[]{:S(2)}, u32[]{:S(2)}) collective-permute-start(f32[32,5,20,2]{0,2,3,1:T(8,128)S(1)} %copy.218), channel_id=1, source_target_pairs={{0,1},{1,2},{2,3},{3,4},{4,5},{5,6},{6,7},{8,9},{9,10},{10,11},{11... | collective-permute-start | bytes 76808 | tf_op jit(solution)/shard_map/ppermute | solution.py:23
  121.7 5.9 %multiply_add_fusion.4 = (f32[32,5,16,128]{3,0,2,1:T(8,128)S(1)}, f32[32,5,16,128]{3,0,2,1:T(8,128)}) fusion(f32[32,5,16,128]{3,0,2,1:T(8,128)S(1)} %multiply_add_fusion.6, f32[32,16,128]{2,0,1:T(8,128)} %get-tuple-element.63, f32[5,16,128]{2,1,0:T(8,128)S(1)} %get-tuple-element.83, f32[32,16,128]{2,0,1:T(8,128)S(1)} %get-tuple-element.60, ...), kind=kLoop, calls=%fused_computation.97 | loop fusion | flops 16711680 | bytes 5842964 | tf_op jit(solution)/shard_map/add | solution.py:92
  128.9 5.0 %collective-permute-start.13 = (f32[32,5,2,128]{3,0,2,1:T(8,128)S(1)}, f32[32,5,2,128]{3,0,2,1:T(8,128)S(1)}, u32[]{:S(2)}, u32[]{:S(2)}) collective-permute-start(f32[32,5,2,128]{3,0,2,1:T(8,128)S(1)} %get-tuple-element.55), channel_id=1, source_target_pairs={{0,8},{8,16},{16,24},{24,32},{32,40},{40,48},{48,56},{56,64},{64,7... | collective-permute-start | bytes 491528 | tf_op jit(solution)/shard_map/ppermute | solution.py:23
  144.7 2.9 %copy.220 = f32[32,5,20,2]{0,2,3,1:T(8,128)} copy(f32[32,5,20,2]{3,0,2,1:T(8,128)} %get-tuple-element.30) | data formatting | bytes 51200
  147.5 3.7 %collective-permute-start.15 = (f32[32,5,20,2]{0,2,3,1:T(8,128)}, f32[32,5,20,2]{0,2,3,1:T(8,128)}, u32[]{:S(2)}, u32[]{:S(2)}) collective-permute-start(f32[32,5,20,2]{0,2,3,1:T(8,128)} %copy.220), channel_id=1, source_target_pairs={{0,1},{1,2},{2,3},{3,4},{4,5},{5,6},{6,7},{8,9},{9,10},{10,11},{11... | collective-permute-start | bytes 76808 | tf_op jit(solution)/shard_map/ppermute | solution.py:23
  157.6 9.5 %multiply_add_fusion.3 = f32[32,5,16,128]{3,0,2,1:T(8,128)S(1)} fusion(f32[32,5,16,128]{3,0,2,1:T(8,128)S(1)} %multiply_add_fusion.6, f32[32,5,16,128]{3,0,2,1:T(8,128)} %get-tuple-element.21, f32[32,5,16,128]{3,0,2,1:T(8,128)} %copy-done.3, f32[32,5,20,2]{3,0,2,1:T(8,128)} %copy.199, f32[32,5,2,128]{3,0,2,1:T(8,128)} %copy-done.9, ...), kind=kLoop, calls=%fused_computation.96 | loop fusion | flops 17039360 | bytes 7153684 | tf_op jit(solution)/shard_map/add | solution.py:94
  168.4 5.0 %collective-permute-start.17 = (f32[32,5,2,128]{3,0,2,1:T(8,128)S(1)}, f32[32,5,2,128]{3,0,2,1:T(8,128)S(1)}, u32[]{:S(2)}, u32[]{:S(2)}) collective-permute-start(f32[32,5,2,128]{3,0,2,1:T(8,128)S(1)} %get-tuple-element.43), channel_id=1, source_target_pairs={{0,8},{8,16},{16,24},{24,32},{32,40},{40,48},{48,56},{56,64},{64,7... | collective-permute-start | bytes 491528 | tf_op jit(solution)/shard_map/ppermute | solution.py:23
  173.5 2.8 collective-permute-done.16
  185.4 3.2 %collective-permute-start.19 = (f32[32,5,20,2]{0,2,3,1:T(8,128)}, f32[32,5,20,2]{0,2,3,1:T(8,128)S(1)}, u32[]{:S(2)}, u32[]{:S(2)}) collective-permute-start(f32[32,5,20,2]{0,2,3,1:T(8,128)} %copy.222), channel_id=1, source_target_pairs={{0,1},{1,2},{2,3},{3,4},{4,5},{5,6},{6,7},{8,9},{9,10},{10,11},{11... | collective-permute-start | bytes 76808 | tf_op jit(solution)/shard_map/ppermute | solution.py:23
  194.2 5.9 %multiply_add_fusion.1 = (f32[32,5,16,128]{3,0,2,1:T(8,128)S(1)}, f32[32,5,16,128]{3,0,2,1:T(8,128)}) fusion(f32[32,5,16,128]{3,0,2,1:T(8,128)S(1)} %multiply_add_fusion.3, f32[32,16,128]{2,0,1:T(8,128)} %get-tuple-element.49, f32[5,16,128]{2,1,0:T(8,128)S(1)} %get-tuple-element.83, f32[32,16,128]{2,0,1:T(8,128)S(1)} %get-tuple-element.46, ...), kind=kLoop, calls=%fused_computation.94 | loop fusion | flops 16711680 | bytes 5842964 | tf_op jit(solution)/shard_map/add | solution.py:92
  201.4 6.9 %collective-permute-start.21 = (f32[32,5,2,128]{3,0,2,1:T(8,128)S(1)}, f32[32,5,2,128]{3,0,2,1:T(8,128)S(1)}, u32[]{:S(2)}, u32[]{:S(2)}) collective-permute-start(f32[32,5,2,128]{3,0,2,1:T(8,128)S(1)} %get-tuple-element.41), channel_id=1, source_target_pairs={{0,8},{8,16},{16,24},{24,32},{32,40},{40,48},{48,56},{56,64},{64,7... | collective-permute-start | bytes 491528 | tf_op jit(solution)/shard_map/ppermute | solution.py:23
  219.0 2.9 %copy.224 = f32[32,5,20,2]{0,2,3,1:T(8,128)} copy(f32[32,5,20,2]{3,0,2,1:T(8,128)} %get-tuple-element.26) | data formatting | bytes 51200
  221.8 3.7 %collective-permute-start.23 = (f32[32,5,20,2]{0,2,3,1:T(8,128)}, f32[32,5,20,2]{0,2,3,1:T(8,128)}, u32[]{:S(2)}, u32[]{:S(2)}) collective-permute-start(f32[32,5,20,2]{0,2,3,1:T(8,128)} %copy.224), channel_id=1, source_target_pairs={{0,1},{1,2},{2,3},{3,4},{4,5},{5,6},{6,7},{8,9},{9,10},{10,11},{11... | collective-permute-start | bytes 76808 | tf_op jit(solution)/shard_map/ppermute | solution.py:23
  229.2 2.7 copy.209
  231.9 5.3 %multiply_add_fusion = f32[32,5,16,128]{3,0,2,1:T(8,128)S(1)} fusion(f32[32,5,16,128]{3,0,2,1:T(8,128)S(1)} %multiply_add_fusion.3, f32[32,5,16,128]{3,0,2,1:T(8,128)} %get-tuple-element.19, f32[32,5,16,128]{3,0,2,1:T(8,128)S(1)} %get-tuple-element.18, f32[32,5,20,2]{3,0,2,1:T(8,128)} %copy.207, f32[32,5,2,128]{3,0,2,1:T(8,128)} %copy-done.7, ...), kind=kLoop, calls=%fused_computation.93 | loop fusion | flops 17039360 | bytes 7153684 | tf_op jit(solution)/shard_map/add | solution.py:94
  239.3 19.0 %all-to-all-start = ((f32[128,8,128]{2,1,0:T(8,128)}), f32[128,8,128]{2,1,0:T(8,128)S(1)}, u32[]{:S(2)}, u32[]{:S(2)}) async-start(f32[128,8,128]{2,1,0:T(8,128)} %broadcast_in_dim.2), calls=%async_computation | async-start | bytes 1048576 | tf_op jit(solution)/shard_map/all_to_all | solution.py:101
  259.8 11.9 %all-to-all-done.parts_ref = f32[128,8,128]{2,1,0:T(8,128)S(1)} async-done(((f32[128,8,128]{2,1,0:T(8,128)}), f32[128,8,128]{2,1,0:T(8,128)S(1)}, u32[]{:S(2)}, u32[]{:S(2)}) %all-to-all-start) | async-done | bytes 524320 | tf_op jit(solution)/shard_map/all_to_all | solution.py:101
  272.4 4.5 %factor.1 = (f32[32,32]{1,0:T(8,128)}, f32[32,32]{1,0:T(8,128)}) custom-call(f32[128,8,128]{2,1,0:T(8,128)} %copy-done.6), custom_call_target="tpu_custom_call" | custom-call | tf_op jit(solution)/shard_map/factor/pallas_call | solution.py:75
  (149 shorter events, 110.1 us)
Async XLA Ops:
  0.6 8.7 %copy-start = (f32[32,5,16,128]{3,2,1,0:T(8,128)S(1)}, f32[32,5,16,128]{3,2,1,0:T(8,128)}, u32[]{:S(2)}) copy-start(f32[32,5,16,128]{3,2,1,0:T(8,128)} %param.5) | copy-start | bytes 3932164
  2.8 14.3 %collective-permute-start.1 = (f32[32,5,2,128]{3,0,2,1:T(8,128)}, f32[32,5,2,128]{3,0,2,1:T(8,128)}, u32[]{:S(2)}, u32[]{:S(2)}) collective-permute-start(f32[32,5,2,128]{3,0,2,1:T(8,128)} %copy.236), channel_id=1, source_target_pairs={{0,8},{8,16},{16,24},{24,32},{32,40},{40,48},{48,56},{56,64},{64,7... | collective-permute-start | bytes 491528 | tf_op jit(solution)/shard_map/ppermute | solution.py:23
  8.1 10.3 %collective-permute-start = (f32[32,5,2,128]{3,0,2,1:T(8,128)}, f32[32,5,2,128]{3,0,2,1:T(8,128)}, u32[]{:S(2)}, u32[]{:S(2)}) collective-permute-start(f32[32,5,2,128]{3,0,2,1:T(8,128)} %copy.235), channel_id=1, source_target_pairs={{8,0},{16,8},{24,16},{32,24},{40,32},{48,40},{56,48},{64,56},{72,6... | collective-permute-start | bytes 491528 | tf_op jit(solution)/shard_map/ppermute | solution.py:24
  17.2 28.9 %copy-start.18 = (f32[5]{0:T(128)}, f32[5]{0:T(128)S(1)}, u32[]{:S(2)}) copy-start(f32[5]{0:T(128)S(1)} %broadcast_multiply_fusion.1) | copy-start | bytes 64
  23.1 3.1 %copy-start.1 = (f32[32,5,20,128]{0,2,3,1:T(8,128)}, f32[32,5,20,128]{0,2,3,1:T(8,128)S(1)}, u32[]{:S(2)}) copy-start(f32[32,5,20,128]{0,2,3,1:T(8,128)S(1)} %pad_maximum_fusion) | copy-start | bytes 4915204
  26.3 16.1 %collective-permute-start.2 = (f32[32,5,20,2]{0,2,3,1:T(8,128)S(1)}, f32[32,5,20,2]{0,2,3,1:T(8,128)S(1)}, u32[]{:S(2)}, u32[]{:S(2)}) collective-permute-start(f32[32,5,20,2]{0,2,3,1:T(8,128)S(1)} %get-tuple-element.24), channel_id=1, source_target_pairs={{1,0},{2,1},{3,2},{4,3},{5,4},{6,5},{7,6},{9,8},{10,9},{11,10},{12... | collective-permute-start | bytes 76808 | tf_op jit(solution)/shard_map/ppermute | solution.py:24
  27.6 16.7 %collective-permute-start.3 = (f32[32,5,20,2]{0,2,3,1:T(8,128)S(1)}, f32[32,5,20,2]{0,2,3,1:T(8,128)S(1)}, u32[]{:S(2)}, u32[]{:S(2)}) collective-permute-start(f32[32,5,20,2]{0,2,3,1:T(8,128)S(1)} %get-tuple-element.25), channel_id=1, source_target_pairs={{0,1},{1,2},{2,3},{3,4},{4,5},{5,6},{6,7},{8,9},{9,10},{10,11},{11... | collective-permute-start | bytes 76808 | tf_op jit(solution)/shard_map/ppermute | solution.py:23
  54.9 23.8 %copy-start.2 = (f32[32,5,16,128]{3,0,2,1:T(8,128)}, f32[32,5,16,128]{3,0,2,1:T(8,128)S(1)}, u32[]{:S(2)}) copy-start(f32[32,5,16,128]{3,0,2,1:T(8,128)S(1)} %get-tuple-element.22) | copy-start | bytes 3932164
  55.0 9.2 %collective-permute-start.4 = (f32[32,5,2,128]{3,0,2,1:T(8,128)S(1)}, f32[32,5,2,128]{3,0,2,1:T(8,128)S(1)}, u32[]{:S(2)}, u32[]{:S(2)}) collective-permute-start(f32[32,5,2,128]{3,0,2,1:T(8,128)S(1)} %get-tuple-element.70), channel_id=1, source_target_pairs={{8,0},{16,8},{24,16},{32,24},{40,32},{48,40},{56,48},{64,56},{72,6... | collective-permute-start | bytes 491528 | tf_op jit(solution)/shard_map/ppermute | solution.py:24
  56.3 9.5 %collective-permute-start.5 = (f32[32,5,2,128]{3,0,2,1:T(8,128)S(1)}, f32[32,5,2,128]{3,0,2,1:T(8,128)S(1)}, u32[]{:S(2)}, u32[]{:S(2)}) collective-permute-start(f32[32,5,2,128]{3,0,2,1:T(8,128)S(1)} %get-tuple-element.69), channel_id=1, source_target_pairs={{0,8},{8,16},{16,24},{24,32},{32,40},{40,48},{48,56},{56,64},{64,7... | collective-permute-start | bytes 491528 | tf_op jit(solution)/shard_map/ppermute | solution.py:23
  70.9 8.8 %collective-permute-start.6 = (f32[32,5,20,2]{0,2,3,1:T(8,128)S(1)}, f32[32,5,20,2]{0,2,3,1:T(8,128)}, u32[]{:S(2)}, u32[]{:S(2)}) collective-permute-start(f32[32,5,20,2]{0,2,3,1:T(8,128)S(1)} %copy.215), channel_id=1, source_target_pairs={{1,0},{2,1},{3,2},{4,3},{5,4},{6,5},{7,6},{9,8},{10,9},{11,10},{12... | collective-permute-start | bytes 76808 | tf_op jit(solution)/shard_map/ppermute | solution.py:24
  75.1 7.3 %collective-permute-start.7 = (f32[32,5,20,2]{0,2,3,1:T(8,128)}, f32[32,5,20,2]{0,2,3,1:T(8,128)}, u32[]{:S(2)}, u32[]{:S(2)}) collective-permute-start(f32[32,5,20,2]{0,2,3,1:T(8,128)} %copy.216), channel_id=1, source_target_pairs={{0,1},{1,2},{2,3},{3,4},{4,5},{5,6},{6,7},{8,9},{9,10},{10,11},{11... | collective-permute-start | bytes 76808 | tf_op jit(solution)/shard_map/ppermute | solution.py:23
  82.4 2.7 copy-start.19
  94.7 9.4 %collective-permute-start.8 = (f32[32,5,2,128]{3,0,2,1:T(8,128)S(1)}, f32[32,5,2,128]{3,0,2,1:T(8,128)S(1)}, u32[]{:S(2)}, u32[]{:S(2)}) collective-permute-start(f32[32,5,2,128]{3,0,2,1:T(8,128)S(1)} %get-tuple-element.58), channel_id=1, source_target_pairs={{8,0},{16,8},{24,16},{32,24},{40,32},{48,40},{56,48},{64,56},{72,6... | collective-permute-start | bytes 491528 | tf_op jit(solution)/shard_map/ppermute | solution.py:24
  96.0 9.3 %collective-permute-start.9 = (f32[32,5,2,128]{3,0,2,1:T(8,128)S(1)}, f32[32,5,2,128]{3,0,2,1:T(8,128)S(1)}, u32[]{:S(2)}, u32[]{:S(2)}) collective-permute-start(f32[32,5,2,128]{3,0,2,1:T(8,128)S(1)} %get-tuple-element.57), channel_id=1, source_target_pairs={{0,8},{8,16},{16,24},{24,32},{32,40},{40,48},{48,56},{56,64},{64,7... | collective-permute-start | bytes 491528 | tf_op jit(solution)/shard_map/ppermute | solution.py:23
  110.5 7.5 %collective-permute-start.10 = (f32[32,5,20,2]{0,2,3,1:T(8,128)S(1)}, f32[32,5,20,2]{0,2,3,1:T(8,128)S(1)}, u32[]{:S(2)}, u32[]{:S(2)}) collective-permute-start(f32[32,5,20,2]{0,2,3,1:T(8,128)S(1)} %copy.217), channel_id=1, source_target_pairs={{1,0},{2,1},{3,2},{4,3},{5,4},{6,5},{7,6},{9,8},{10,9},{11,10},{12... | collective-permute-start | bytes 76808 | tf_op jit(solution)/shard_map/ppermute | solution.py:24
  114.0 5.8 %collective-permute-start.11 = (f32[32,5,20,2]{0,2,3,1:T(8,128)S(1)}, f32[32,5,20,2]{0,2,3,1:T(8,128)S(1)}, u32[]{:S(2)}, u32[]{:S(2)}) collective-permute-start(f32[32,5,20,2]{0,2,3,1:T(8,128)S(1)} %copy.218), channel_id=1, source_target_pairs={{0,1},{1,2},{2,3},{3,4},{4,5},{5,6},{6,7},{8,9},{9,10},{10,11},{11... | collective-permute-start | bytes 76808 | tf_op jit(solution)/shard_map/ppermute | solution.py:23
  127.6 23.7 %copy-start.3 = (f32[32,5,16,128]{3,0,2,1:T(8,128)}, f32[32,5,16,128]{3,0,2,1:T(8,128)S(1)}, u32[]{:S(2)}) copy-start(f32[32,5,16,128]{3,0,2,1:T(8,128)S(1)} %get-tuple-element.20) | copy-start | bytes 3932164
  127.6 9.0 %collective-permute-start.12 = (f32[32,5,2,128]{3,0,2,1:T(8,128)S(1)}, f32[32,5,2,128]{3,0,2,1:T(8,128)S(1)}, u32[]{:S(2)}, u32[]{:S(2)}) collective-permute-start(f32[32,5,2,128]{3,0,2,1:T(8,128)S(1)} %get-tuple-element.56), channel_id=1, source_target_pairs={{8,0},{16,8},{24,16},{32,24},{40,32},{48,40},{56,48},{64,56},{72,6... | collective-permute-start | bytes 491528 | tf_op jit(solution)/shard_map/ppermute | solution.py:24
  128.9 9.4 %collective-permute-start.13 = (f32[32,5,2,128]{3,0,2,1:T(8,128)S(1)}, f32[32,5,2,128]{3,0,2,1:T(8,128)S(1)}, u32[]{:S(2)}, u32[]{:S(2)}) collective-permute-start(f32[32,5,2,128]{3,0,2,1:T(8,128)S(1)} %get-tuple-element.55), channel_id=1, source_target_pairs={{0,8},{8,16},{16,24},{24,32},{32,40},{40,48},{48,56},{56,64},{64,7... | collective-permute-start | bytes 491528 | tf_op jit(solution)/shard_map/ppermute | solution.py:23
  143.4 8.8 %collective-permute-start.14 = (f32[32,5,20,2]{0,2,3,1:T(8,128)S(1)}, f32[32,5,20,2]{0,2,3,1:T(8,128)}, u32[]{:S(2)}, u32[]{:S(2)}) collective-permute-start(f32[32,5,20,2]{0,2,3,1:T(8,128)S(1)} %copy.219), channel_id=1, source_target_pairs={{1,0},{2,1},{3,2},{4,3},{5,4},{6,5},{7,6},{9,8},{10,9},{11,10},{12... | collective-permute-start | bytes 76808 | tf_op jit(solution)/shard_map/ppermute | solution.py:24
  147.5 7.3 %collective-permute-start.15 = (f32[32,5,20,2]{0,2,3,1:T(8,128)}, f32[32,5,20,2]{0,2,3,1:T(8,128)}, u32[]{:S(2)}, u32[]{:S(2)}) collective-permute-start(f32[32,5,20,2]{0,2,3,1:T(8,128)} %copy.220), channel_id=1, source_target_pairs={{0,1},{1,2},{2,3},{3,4},{4,5},{5,6},{6,7},{8,9},{9,10},{10,11},{11... | collective-permute-start | bytes 76808 | tf_op jit(solution)/shard_map/ppermute | solution.py:23
  167.1 9.1 %collective-permute-start.16 = (f32[32,5,2,128]{3,0,2,1:T(8,128)S(1)}, f32[32,5,2,128]{3,0,2,1:T(8,128)S(1)}, u32[]{:S(2)}, u32[]{:S(2)}) collective-permute-start(f32[32,5,2,128]{3,0,2,1:T(8,128)S(1)} %get-tuple-element.44), channel_id=1, source_target_pairs={{8,0},{16,8},{24,16},{32,24},{40,32},{48,40},{56,48},{64,56},{72,6... | collective-permute-start | bytes 491528 | tf_op jit(solution)/shard_map/ppermute | solution.py:24
  168.4 9.5 %collective-permute-start.17 = (f32[32,5,2,128]{3,0,2,1:T(8,128)S(1)}, f32[32,5,2,128]{3,0,2,1:T(8,128)S(1)}, u32[]{:S(2)}, u32[]{:S(2)}) collective-permute-start(f32[32,5,2,128]{3,0,2,1:T(8,128)S(1)} %get-tuple-element.43), channel_id=1, source_target_pairs={{0,8},{8,16},{16,24},{24,32},{32,40},{40,48},{48,56},{56,64},{64,7... | collective-permute-start | bytes 491528 | tf_op jit(solution)/shard_map/ppermute | solution.py:23
  182.7 6.9 %collective-permute-start.18 = (f32[32,5,20,2]{0,2,3,1:T(8,128)S(1)}, f32[32,5,20,2]{0,2,3,1:T(8,128)}, u32[]{:S(2)}, u32[]{:S(2)}) collective-permute-start(f32[32,5,20,2]{0,2,3,1:T(8,128)S(1)} %copy.221), channel_id=1, source_target_pairs={{1,0},{2,1},{3,2},{4,3},{5,4},{6,5},{7,6},{9,8},{10,9},{11,10},{12... | collective-permute-start | bytes 76808 | tf_op jit(solution)/shard_map/ppermute | solution.py:24
  185.4 6.9 %collective-permute-start.19 = (f32[32,5,20,2]{0,2,3,1:T(8,128)}, f32[32,5,20,2]{0,2,3,1:T(8,128)S(1)}, u32[]{:S(2)}, u32[]{:S(2)}) collective-permute-start(f32[32,5,20,2]{0,2,3,1:T(8,128)} %copy.222), channel_id=1, source_target_pairs={{0,1},{1,2},{2,3},{3,4},{4,5},{5,6},{6,7},{8,9},{9,10},{10,11},{11... | collective-permute-start | bytes 76808 | tf_op jit(solution)/shard_map/ppermute | solution.py:23
  200.1 10.7 %collective-permute-start.20 = (f32[32,5,2,128]{3,0,2,1:T(8,128)S(1)}, f32[32,5,2,128]{3,0,2,1:T(8,128)S(1)}, u32[]{:S(2)}, u32[]{:S(2)}) collective-permute-start(f32[32,5,2,128]{3,0,2,1:T(8,128)S(1)} %get-tuple-element.42), channel_id=1, source_target_pairs={{8,0},{16,8},{24,16},{32,24},{40,32},{48,40},{56,48},{64,56},{72,6... | collective-permute-start | bytes 491528 | tf_op jit(solution)/shard_map/ppermute | solution.py:24
  201.4 11.2 %collective-permute-start.21 = (f32[32,5,2,128]{3,0,2,1:T(8,128)S(1)}, f32[32,5,2,128]{3,0,2,1:T(8,128)S(1)}, u32[]{:S(2)}, u32[]{:S(2)}) collective-permute-start(f32[32,5,2,128]{3,0,2,1:T(8,128)S(1)} %get-tuple-element.41), channel_id=1, source_target_pairs={{0,8},{8,16},{16,24},{24,32},{32,40},{40,48},{48,56},{56,64},{64,7... | collective-permute-start | bytes 491528 | tf_op jit(solution)/shard_map/ppermute | solution.py:23
  217.7 8.7 %collective-permute-start.22 = (f32[32,5,20,2]{0,2,3,1:T(8,128)S(1)}, f32[32,5,20,2]{0,2,3,1:T(8,128)}, u32[]{:S(2)}, u32[]{:S(2)}) collective-permute-start(f32[32,5,20,2]{0,2,3,1:T(8,128)S(1)} %copy.223), channel_id=1, source_target_pairs={{1,0},{2,1},{3,2},{4,3},{5,4},{6,5},{7,6},{9,8},{10,9},{11,10},{12... | collective-permute-start | bytes 76808 | tf_op jit(solution)/shard_map/ppermute | solution.py:24
  221.8 7.3 %collective-permute-start.23 = (f32[32,5,20,2]{0,2,3,1:T(8,128)}, f32[32,5,20,2]{0,2,3,1:T(8,128)}, u32[]{:S(2)}, u32[]{:S(2)}) collective-permute-start(f32[32,5,20,2]{0,2,3,1:T(8,128)} %copy.224), channel_id=1, source_target_pairs={{0,1},{1,2},{2,3},{3,4},{4,5},{5,6},{6,7},{8,9},{9,10},{10,11},{11... | collective-permute-start | bytes 76808 | tf_op jit(solution)/shard_map/ppermute | solution.py:23
  238.4 20.0 %copy-start.5 = (f32[32,5,16,128]{3,0,2,1:T(8,128)S(1)}, f32[32,5,16,128]{3,0,2,1:T(8,128)}, u32[]{:S(2)}) copy-start(f32[32,5,16,128]{3,0,2,1:T(8,128)} %copy-done.4) | copy-start | bytes 3932164
  239.3 32.3 %all-to-all-start = ((f32[128,8,128]{2,1,0:T(8,128)}), f32[128,8,128]{2,1,0:T(8,128)S(1)}, u32[]{:S(2)}, u32[]{:S(2)}) async-start(f32[128,8,128]{2,1,0:T(8,128)} %broadcast_in_dim.2), calls=%async_computation | async-start | bytes 1048576 | tf_op jit(solution)/shard_map/all_to_all | solution.py:101
  (19 other events, 29.8 us)

commit v2 on v1

v2 whole, which is shorter than its diff:
```python
import functools

import jax
import jax.numpy as jnp
from jax import lax
from jax.experimental import pallas as pl
from jax.experimental.pallas import tpu as pltpu
from jax.sharding import PartitionSpec as P

STEPS = 3
TIME_STEP = 0.8
SECTIONS = 2 * STEPS
WIDTH = 2 * SECTIONS
V = 5
GROUP = 16
PER = 128 // GROUP
PLANES = V * V + 3
WEIGHTS = V * (V + 8)
VMEM_LIMIT = 56 << 20


def whole(count):
    return [pl.BlockSpec(memory_space=pltpu.VMEM) for _ in range(count)]


def lanes_of(shape):
    return lax.broadcasted_iota(jnp.int32, shape, 1)


def pack_axial_kernel(field_ref, coupling_ref, axial_ref, radial_ref, up_ref, down_ref):
    planes, length, _ = field_ref.shape
    low = length - WIDTH

    def put(slot, read):
        base = slot * WIDTH
        for start in range(0, WIDTH, 8):
            size = min(8, WIDTH - start)
            up_ref[pl.ds(base + start, size), :] = read(low + start, size)
            down_ref[pl.ds(base + start, size), :] = read(start, size)

    @pl.loop(0, planes // 8)
    def _(block):
        for inner in range(8):
            plane = block * 8 + inner
            put(plane, lambda start, size: field_ref[plane, pl.ds(start, size), :])

    for plane in range(V * V):
        put(planes + plane, lambda start, size: coupling_ref[plane, pl.ds(start, size), :])
    put(planes + V * V, lambda start, size: axial_ref[pl.ds(start, size), :])
    put(planes + V * V + 1, lambda start, size: radial_ref[pl.ds(start, size), :])
    put(planes + V * V + 2, lambda start, size: jnp.ones((size, 128), jnp.float32))


def chunks(length):
    rim = sorted({*range(0, WIDTH - 7, 8), WIDTH - 8})
    return (
        [(0, row, row) for row in rim]
        + [(1, row, WIDTH + row) for row in range(0, length, 8)]
        + [(2, row, WIDTH + length + row) for row in rim]
    )


def coefficient(plane, source, row, planes, coupling_ref, axial_ref, radial_ref, low_ref, high_ref):
    if source != 1:
        ref = low_ref if source == 0 else high_ref
        return ref[pl.ds((planes + plane) * WIDTH + row, 8), :]
    if plane < V * V:
        return coupling_ref[plane, pl.ds(row, 8), :]
    if plane == V * V + 2:
        return jnp.ones((8, 128), jnp.float32)
    return (axial_ref if plane == V * V else radial_ref)[pl.ds(row, 8), :]


def pack_radial_kernel(
    field_ref, coupling_ref, axial_ref, radial_ref, low_ref, high_ref, right_ref, left_ref
):
    planes, length, _ = field_ref.shape
    groups = planes // (V * PER)
    lane = lanes_of((8, 128))

    def merge(tiles, offset):
        merged = pltpu.roll(tiles[0], offset, axis=1)
        for j in range(1, len(tiles)):
            merged = jnp.where(
                lane >= GROUP * j, pltpu.roll(tiles[j], (GROUP * j + offset) % 128, axis=1), merged
            )
        return merged

    def put(slot, row, tiles):
        right_ref[slot, pl.ds(row, 8), :] = merge(tiles, WIDTH)
        left_ref[slot, pl.ds(row, 8), :] = merge(tiles, 2)

    @pl.loop(0, groups * V)
    def _(slot):
        group, v = slot // V, slot % V
        for source, row, target in chunks(length):
            tiles = []
            for j in range(PER):
                plane = (group * PER + j) * V + v
                if source == 1:
                    tiles.append(field_ref[plane, pl.ds(row, 8), :])
                else:
                    ref = low_ref if source == 0 else high_ref
                    tiles.append(ref[pl.ds(plane * WIDTH + row, 8), :])
            put(slot, target, tiles)

    for slot in range(-(-PLANES // PER)):
        for source, row, target in chunks(length):
            tiles = [
                coefficient(
                    plane, source, row, planes, coupling_ref, axial_ref, radial_ref, low_ref, high_ref
                )
                for plane in range(slot * PER, min(PLANES, (slot + 1) * PER))
            ]
            put(groups * V + slot, target, tiles)


def weights_of(raw, viscosity):
    axial = raw[V * V] * (-TIME_STEP / 12.0)
    radial = raw[V * V + 1] * (-TIME_STEP / 12.0)
    inside = raw[V * V + 2]
    found = []
    for v in range(V):
        spread = inside * (viscosity[v] * (TIME_STEP / 12.0))
        for w in range(V):
            value = raw[v * V + w] * TIME_STEP
            found.append(value + (1.0 - 60.0 * spread) if v == w else value)
        for speed in (axial, radial):
            found.append(16.0 * spread + 8.0 * speed)
            found.append(16.0 * spread - 8.0 * speed)
            found.append(-spread - speed)
            found.append(speed - spread)
    return found


def steps_kernel(
    viscosity_ref,
    field_ref,
    coupling_ref,
    axial_ref,
    radial_ref,
    low_ref,
    high_ref,
    left_ref,
    right_ref,
    out_ref,
    now_ref,
    middle_ref,
    now_rim_ref,
    middle_rim_ref,
    weight_ref,
):
    planes, length, _ = field_ref.shape
    vectors = planes // V
    groups = vectors // PER
    slots = groups * V
    extended = length + 2 * WIDTH
    lane = lanes_of((8, 128))
    place = lane % GROUP
    viscosity = [viscosity_ref[v] for v in range(V)]

    @pl.loop(0, planes // 8)
    def _(block):
        for inner in range(8):
            plane = block * 8 + inner
            for source, row, target in chunks(length):
                if source == 1:
                    value = field_ref[plane, pl.ds(row, 8), :]
                else:
                    ref = low_ref if source == 0 else high_ref
                    value = ref[pl.ds(plane * WIDTH + row, 8), :]
                now_ref[plane, pl.ds(target, 8), :] = value

    @pl.loop(0, slots)
    def _(slot):
        for row in range(0, extended, 8):
            now_rim_ref[0, slot, pl.ds(row, 8), :] = left_ref[slot, pl.ds(row, 8), :]
            now_rim_ref[1, slot, pl.ds(row, 8), :] = right_ref[slot, pl.ds(row, 8), :]

    for source, row, target in chunks(length):
        raw = [
            coefficient(
                plane, source, row, planes, coupling_ref, axial_ref, radial_ref, low_ref, high_ref
            )
            for plane in range(PLANES)
        ]
        for index, value in enumerate(weights_of(raw, viscosity)):
            weight_ref[0, index, pl.ds(target, 8), :] = value

    @pl.loop(0, extended // 8)
    def _(block):
        start = pl.multiple_of(block * 8, 8)
        for side, ref in ((0, left_ref), (1, right_ref)):
            raw = []
            for plane in range(PLANES):
                tile = ref[slots + plane // PER, pl.ds(start, 8), :]
                tile = pltpu.roll(tile, (128 - GROUP * (plane % PER)) % 128, axis=1)
                tile = jnp.where(lane < GROUP, tile, 0.0)
                reach = GROUP
                while reach < 128:
                    tile = tile + pltpu.roll(tile, reach, axis=1)
                    reach *= 2
                raw.append(tile)
            for index, value in enumerate(weights_of(raw, viscosity)):
                weight_ref[1 + side, index, pl.ds(start, 8), :] = value

    def euler(v, kind, start, count, centers, vertical, sideways):
        def weight(index):
            return weight_ref[kind, v * (V + 8) + index, pl.ds(start, 8), :]

        totals = None
        for w in range(V):
            factor = weight(w)
            terms = [factor * centers[i][w] for i in range(count)]
            totals = terms if totals is None else [a + b for a, b in zip(totals, terms)]
        for index, step in enumerate((1, -1, 2, -2)):
            factor = weight(V + index)
            totals = [totals[i] + factor * vertical(i, step) for i in range(count)]
        for index, step in enumerate((1, -1, 2, -2)):
            factor = weight(V + 4 + index)
            totals = [totals[i] + factor * sideways(i, step) for i in range(count)]
        return totals

    for section in range(1, SECTIONS + 1):
        odd = section % 2 == 1
        last = section == SECTIONS
        source, source_rim = (now_ref, now_rim_ref) if odd else (middle_ref, middle_rim_ref)
        target, target_rim = (middle_ref, middle_rim_ref) if odd else (now_ref, now_rim_ref)
        first = 2 * section
        blocks = -(-(extended - 2 * first) // 8)

        @pl.loop(0, groups * blocks)
        def _(index):
            group, block = index // blocks, index % blocks
            start = first + block * 8
            joints = []
            for v in range(V):
                slot = group * V + v
                own = None
                for j in range(PER):
                    tile = source[(group * PER + j) * V + v, pl.ds(start, 8), :]
                    tile = pltpu.roll(tile, (GROUP * j + WIDTH) % 128, axis=1)
                    own = tile if own is None else jnp.where(lane >= GROUP * j, tile, own)
                left = source_rim[0, slot, pl.ds(start, 8), :]
                right = source_rim[1, slot, pl.ds(start, 8), :]
                inner = (place == WIDTH) | (place == WIDTH + 1)
                joints.append(jnp.where(inner, pltpu.roll(right, WIDTH - 2, axis=1), left))
                if not last:
                    source_rim[0, slot, pl.ds(start, 8), :] = jnp.where(inner, own, left)
                    source_rim[1, slot, pl.ds(start, 8), :] = jnp.where(
                        place < 2, pltpu.roll(own, 128 - (WIDTH - 2), axis=1), right
                    )

            if not last:
                for side in range(2):
                    slot = group * V
                    centers = [
                        [source_rim[side, slot + w, pl.ds(start, 8), :] for w in range(V)]
                    ]
                    for v in range(V):
                        (value,) = euler(
                            v,
                            1 + side,
                            start,
                            1,
                            centers,
                            lambda i, step: source_rim[side, slot + v, pl.ds(start + step, 8), :],
                            lambda i, step: pltpu.roll(centers[0][v], (128 - step) % 128, axis=1),
                        )
                        if not odd:
                            value = 0.5 * (value + target_rim[side, slot + v, pl.ds(start, 8), :])
                        target_rim[side, slot + v, pl.ds(start, 8), :] = value

            @pl.loop(0, PER // TOGETHER)
            def _(part):
                bases = [(group * PER + part * TOGETHER + i) * V for i in range(TOGETHER)]
                centers = [
                    [source[base + w, pl.ds(start, 8), :] for w in range(V)] for base in bases
                ]
                for v in range(V):
                    rims = [
                        pltpu.roll(
                            joints[v],
                            256 - WIDTH - GROUP * (part * TOGETHER + i),
                            axis=1,
                        )
                        for i in range(TOGETHER)
                    ]
                    edges = {1: lane == 0, 2: lane <= 1, -1: lane == 127, -2: lane >= 126}

                    def sideways(i, step):
                        tile = jnp.where(edges[step], rims[i], centers[i][v])
                        return pltpu.roll(tile, (128 - step) % 128, axis=1)

                    values = euler(
                        v,
                        0,
                        start,
                        TOGETHER,
                        centers,
                        lambda i, step: source[bases[i] + v, pl.ds(start + step, 8), :],
                        sideways,
                    )
                    for i in range(TOGETHER):
                        value = values[i]
                        if not odd:
                            value = 0.5 * (value + target[bases[i] + v, pl.ds(start, 8), :])
                        if last:
                            out_ref[bases[i] + v, pl.ds(start - WIDTH, 8), :] = value
                        else:
                            target[bases[i] + v, pl.ds(start, 8), :] = value


TOGETHER = 2


def factor_kernel(parts_ref, factor_ref, inverse_ref, *, rows_all):
    total = jnp.sum(parts_ref[...], axis=0) * (1.0 / rows_all)
    order = factor_ref.shape[0]
    lane = lax.broadcasted_iota(jnp.int32, (order, 128), 1)
    row = lax.broadcasted_iota(jnp.int32, (order, 128), 0)
    pieces = [total] + [pltpu.roll(total, 128 - 32 * i, axis=1) for i in range(1, 4)]
    work = jnp.concatenate(pieces, axis=0)
    work = jnp.where(lane < order, work, jnp.where(lane == row + order, 1.0, 0.0))
    for j in range(order - 1):
        pivot_row = work[j : j + 1, :]
        scale = pivot_row / pivot_row[:, j : j + 1]
        column = jnp.where(row > j, jnp.broadcast_to(work[:, j : j + 1], work.shape), 0.0)
        work = work - column * scale
    diagonal = jnp.sum(jnp.where(lane == row, work, 0.0), axis=1, keepdims=True)
    work = work / jnp.sqrt(diagonal)
    factor_ref[...] = jnp.where(lane >= row, work, 0.0)[:, :order]
    inverse_ref[...] = jnp.where(lane <= row, pltpu.roll(work, 128 - order, axis=1), 0.0)[:, :order]


def factor_and_inverse(parts, order, rows_all):
    square = jax.ShapeDtypeStruct((order, order), jnp.float32)
    return pl.pallas_call(
        functools.partial(factor_kernel, rows_all=rows_all),
        out_shape=(square, square),
        name="factor",
    )(parts)


def shape_of(*dims):
    return jax.ShapeDtypeStruct(dims, jnp.float32)


def shifted(block, axis, step):
    size = lax.axis_size(axis)
    return lax.ppermute(
        block, axis, [(i, i + step) for i in range(size) if 0 <= i + step < size]
    )


def per_device(forcing, vel_axial, vel_radial, coupling, viscosity):
    vectors, variables, length, columns = forcing.shape
    planes = vectors * variables
    extended = length + 2 * WIDTH
    field = forcing.reshape(planes, length, columns)
    local = (field, coupling.reshape(V * V, length, columns), vel_axial, vel_radial)
    params = pltpu.CompilerParams(vmem_limit_bytes=VMEM_LIMIT)

    strip = shape_of((planes + PLANES) * WIDTH, columns)
    up, down = pl.pallas_call(
        pack_axial_kernel,
        in_specs=whole(4),
        out_specs=whole(2),
        out_shape=(strip, strip),
        compiler_params=params,
        name="pack_axial",
    )(*local)
    low = shifted(up, "ax", 1)
    high = shifted(down, "ax", -1)

    rim_slots = planes // PER + -(-PLANES // PER)
    rim = shape_of(rim_slots, extended, columns)
    to_right, to_left = pl.pallas_call(
        pack_radial_kernel,
        in_specs=whole(6),
        out_specs=whole(2),
        out_shape=(rim, rim),
        compiler_params=params,
        name="pack_radial",
    )(*local, low, high)
    left = shifted(to_right, "rad", 1)
    right = shifted(to_left, "rad", -1)

    rows = extended + 8
    response = pl.pallas_call(
        steps_kernel,
        in_specs=[pl.BlockSpec(memory_space=pltpu.SMEM)] + whole(8),
        out_specs=whole(1)[0],
        out_shape=shape_of(planes, length, columns),
        scratch_shapes=[
            pltpu.VMEM((planes, rows, columns), jnp.float32),
            pltpu.VMEM((planes, rows, columns), jnp.float32),
            pltpu.VMEM((2, planes // PER, rows, columns), jnp.float32),
            pltpu.VMEM((2, planes // PER, rows, columns), jnp.float32),
            pltpu.VMEM((3, WEIGHTS, rows, columns), jnp.float32),
        ],
        compiler_params=params,
        name="steps",
    )(viscosity, *local, low, high, left, right)

    flattened = response.reshape(vectors, variables * length * columns)
    devices = lax.axis_size("ax") * lax.axis_size("rad")
    rows_all = variables * length * columns * devices
    local_gram = jnp.dot(flattened, flattened.T, precision=lax.Precision.HIGHEST)
    packed = jnp.concatenate([local_gram[8 * i : 8 * i + 8] for i in range(4)], axis=1)
    copies = jnp.broadcast_to(packed, (devices, 8, 128))
    parts = lax.all_to_all(copies, ("ax", "rad"), 0, 0)
    upper_factor, lower_inverse = factor_and_inverse(parts, vectors, rows_all)
    basis = jnp.dot(lower_inverse, flattened, precision=lax.Precision.HIGHEST).reshape(forcing.shape)
    return (basis, upper_factor)


def solution(mesh):
    return jax.shard_map(
        per_device,
        mesh=mesh,
        in_specs=(
            P(None, None, "ax", "rad"),
            P("ax", "rad"),
            P("ax", "rad"),
            P(None, None, "ax", "rad"),
            P(),
        ),
        out_specs=(P(None, None, "ax", "rad"), P()),
        check_vma=False,
    )
```

time: 283 us -> 187 us (0.66)
  Pallas kernels: 4.48 us -> 104 us
  local copies, waits for them, and re-layouts: 103 us -> 7 us
  starting transfers between devices: 86.8 us -> 25.4 us
  other arithmetic: 49.1 us -> 0.08 us
  waiting for transfers between devices: 33.4 us -> 45.6 us
    pallas_call x0 -> x3, Pallas kernels: none -> 99.7 us  [the longest x1 89.6 us: per_device(): pl.pallas_call(steps_kernel, in_specs=[pl.BlockSpec(memory_space=pltpu.SM...]
    ppermute x24 -> x4, starting transfers between devices: 67.8 us -> 7.86 us  [shifted(): lax.ppermute(block, axis, [(i, i + step) for i in range(size) if 0 <= i +...]
    add x6 -> x0, other arithmetic: 44.9 us -> none  [the longest x3 24.3 us: per_device(): field_now = field_now + 0.5 * time_step * (slope_one + slope_two)]
    unnamed x70 -> x12, local copies, waits for them, and re-layouts: 42.4 us -> 4.65 us
    ppermute x14 -> x0, local copies, waits for them, and re-layouts: 30.8 us -> none  [the longest x7 15.8 us: padded_2(): after = lax.ppermute(initial, axis, down)]
    slice x12 -> x0, local copies, waits for them, and re-layouts: 12.4 us -> none  [the longest x9 8.35 us: padded_2(): last = lax.slice_in_dim(shard, length - width, length, axis=dim)]
    ppermute x24 -> x4, waiting for transfers between devices: 21.6 us -> 32.3 us  [shifted(): lax.ppermute(block, axis, [(i, i + step) for i in range(size) if 0 <= i +...]
    concatenate x2 -> x0, local copies, waits for them, and re-layouts: 8.14 us -> none  [padded_2(): shard = jnp.concatenate([before, shard, after], axis=dim)]
  transfers between devices with their start and end apart: 25 -> 5, of which waited for: 11 -> 5; matrix products, arithmetic and copies ran while one was open for 19% -> 0% of each run, Pallas kernels for 0% -> 0%
where the time goes in v2:
time: 187 us; the launch traced here: 186 us
  Pallas kernels  104 us (56%)
  waiting for transfers between devices  45.6 us (24%)
  starting transfers between devices  25.4 us (14%)
  local copies, waits for them, and re-layouts  7 us (4%)
  matrix products  3.35 us (2%)
    pallas_call x1, Pallas kernels, per_device(): pl.pallas_call(steps_kernel, in_specs=[pl.BlockSpec(memory_space=pltpu.SM...  89.6 us
    ppermute x4, waiting for transfers between devices, shifted(): lax.ppermute(block, axis, [(i, i + step) for i in range(size) if 0 <= i +...  32.3 us
    all_to_all x1, starting transfers between devices, per_device(): parts = lax.all_to_all(copies, ('ax', 'rad'), 0, 0)  17.6 us
    all_to_all x1, waiting for transfers between devices, per_device(): parts = lax.all_to_all(copies, ('ax', 'rad'), 0, 0)  13.3 us
    ppermute x4, starting transfers between devices, shifted(): lax.ppermute(block, axis, [(i, i + step) for i in range(size) if 0 <= i +...  7.86 us
    pallas_call x1, Pallas kernels, per_device(): pl.pallas_call(pack_radial_kernel, in_specs=whole(6), out_specs=whole(2),...  6.96 us
    unnamed x12, local copies, waits for them, and re-layouts  4.65 us
    pallas_call x1, Pallas kernels, factor_and_inverse(): pl.pallas_call(functools.partial(factor_kernel, rows_all=rows_all), out_s...  4.47 us
  transfers between devices with their start and end apart: 5, of which 5 were waited for; matrix products, arithmetic and copies ran while one was open for 0% of the time, Pallas kernels for 0%

profile of v2, /device:TPU:0, one launch (start us, length us, event | category | flops | bytes accessed | tf_op | source)
XLA Modules:
  0.0 186.3 jit_solution(1133231685807419890)
XLA Ops:
  0.6 3.1 %pack_axial.1 = (f32[2256,128]{1,0:T(8,128)}, f32[2256,128]{1,0:T(8,128)}) custom-call(f32[160,16,128]{2,1,0:T(8,128)} %bitcast.16, f32[25,16,128]{2,1,0:T(8,128)} %bitcast.20, f32[16,128]{1,0:T(8,128)} %axial_ref.5, f32[16,128]{1,0:T(8,128)} %radial_ref.5), custom_call_target="tpu_custom_call" | custom-call | tf_op jit(solution)/shard_map/pack_axial/pallas_call | solution.py:365
  3.7 4.0 %collective-permute-start = (f32[2256,128]{1,0:T(8,128)}, f32[2256,128]{1,0:T(8,128)S(1)}, u32[]{:S(2)}, u32[]{:S(2)}) collective-permute-start(f32[2256,128]{1,0:T(8,128)} %get-tuple-element.8), channel_id=1, source_target_pairs={{0,8},{8,16},{16,24},{24,32},{32,40},{40,48},{48,56},{56,64},{64,7... | collective-permute-start | bytes 3465224 | tf_op jit(solution)/shard_map/ppermute | solution.py:351
  7.7 1.3 collective-permute-start.1
  9.0 23.6 %collective-permute-done.low_ref = f32[2256,128]{1,0:T(8,128)S(1)} collective-permute-done((f32[2256,128]{1,0:T(8,128)}, f32[2256,128]{1,0:T(8,128)S(1)}, u32[]{:S(2)}, u32[]{:S(2)}) %collective-permute-start) | collective-permute-done | bytes 1155104 | tf_op jit(solution)/shard_map/ppermute | solution.py:351
  32.6 0.0 copy-start
  32.6 4.2 %collective-permute-done.1.high_ref = f32[2256,128]{1,0:T(8,128)S(1)} collective-permute-done((f32[2256,128]{1,0:T(8,128)}, f32[2256,128]{1,0:T(8,128)S(1)}, u32[]{:S(2)}, u32[]{:S(2)}) %collective-permute-start.1) | collective-permute-done | bytes 1155104 | tf_op jit(solution)/shard_map/ppermute | solution.py:351
  36.8 0.0 copy-done
  36.8 0.0 copy-start.1
  36.8 1.0 copy-done.1
  37.8 7.0 %pack_radial.1 = (f32[24,40,128]{2,1,0:T(8,128)}, f32[24,40,128]{2,1,0:T(8,128)}) custom-call(f32[160,16,128]{2,1,0:T(8,128)} %bitcast.17, f32[25,16,128]{2,1,0:T(8,128)} %bitcast.21, f32[16,128]{1,0:T(8,128)} %axial_ref.5, f32[16,128]{1,0:T(8,128)} %radial_ref.5, f32[2256,128]{1,0:T(8,128)} %copy-done, f32[2256,128]{1,0:T(8,128)} %copy-done.1), custom_call_target="tpu_custom_call" | custom-call | tf_op jit(solution)/shard_map/pack_radial/pallas_call | solution.py:378
  44.8 1.3 collective-permute-start.2
  46.1 1.3 collective-permute-start.3
  47.4 0.4 collective-permute-done.2.left_ref
  47.8 0.0 copy-start.3
  47.8 4.1 %collective-permute-done.3.right_ref = f32[24,40,128]{2,1,0:T(8,128)S(1)} collective-permute-done((f32[24,40,128]{2,1,0:T(8,128)}, f32[24,40,128]{2,1,0:T(8,128)S(1)}, u32[]{:S(2)}, u32[]{:S(2)}) %collective-permute-start.3) | collective-permute-done | bytes 491552 | tf_op jit(solution)/shard_map/ppermute | solution.py:351
  51.8 0.0 copy-done.3
  51.8 0.0 copy-start.4
  51.9 0.8 copy-done.4
  52.6 89.6 %steps.1 = f32[160,16,128]{2,1,0:T(8,128)} custom-call(f32[5]{0:T(128)} %viscosity_ref.1, f32[160,16,128]{2,1,0:T(8,128)} %bitcast.18, f32[25,16,128]{2,1,0:T(8,128)} %bitcast.22, f32[16,128]{1,0:T(8,128)} %axial_ref.5, f32[16,128]{1,0:T(8,128)} %radial_ref.5, f32[2256,128]{1,0:T(8,128)} %copy-done, f32[2256,128]{1,0:T(8,128)} %copy-done.1, ...), custom_call_target="tpu_custom_call" | custom-call | tf_op jit(solution)/shard_map/steps/pallas_call | solution.py:390
  142.3 1.5 reshape.17
  143.8 1.2 fusion.4
  144.9 0.1 pad_maximum_fusion
  145.0 0.8 broadcast_in_dim.3
  145.9 17.6 %all-to-all-start = ((f32[128,8,128]{2,1,0:T(8,128)}), f32[128,8,128]{2,1,0:T(8,128)S(1)}, u32[]{:S(2)}, u32[]{:S(2)}) async-start(f32[128,8,128]{2,1,0:T(8,128)} %broadcast_in_dim.3), calls=%async_computation | async-start | bytes 1048576 | tf_op jit(solution)/shard_map/all_to_all | solution.py:412
  163.4 0.2 copy.11
  163.7 13.3 %all-to-all-done.parts_ref = f32[128,8,128]{2,1,0:T(8,128)S(1)} async-done(((f32[128,8,128]{2,1,0:T(8,128)}), f32[128,8,128]{2,1,0:T(8,128)S(1)}, u32[]{:S(2)}, u32[]{:S(2)}) %all-to-all-start) | async-done | bytes 524320 | tf_op jit(solution)/shard_map/all_to_all | solution.py:412
  177.0 0.0 copy-start.2
  177.0 0.8 copy-done.2
  177.8 4.5 %factor.1 = (f32[32,32]{1,0:T(8,128)}, f32[32,32]{1,0:T(8,128)}) custom-call(f32[128,8,128]{2,1,0:T(8,128)} %copy-done.2), custom_call_target="tpu_custom_call" | custom-call | tf_op jit(solution)/shard_map/factor/pallas_call | solution.py:338
  182.2 2.2 %fusion = f32[32,5,16,128]{3,0,2,1:T(8,128)S(1)} fusion(f32[5,16,128,32]{2,1,0,3:T(8,128)S(1)} %bitcast.19, f32[32,32]{1,0:T(8,128)} %get-tuple-element.12), kind=kOutput, calls=%fused_computation | convolution fusion | flops 125829120 | bytes 2625536 | tf_op jit(solution)/shard_map/dot_general | solution.py:414
  184.4 1.8 copy.9
  (1 shorter events, 0.0 us)
Async XLA Ops:
  3.7 28.9 %collective-permute-start = (f32[2256,128]{1,0:T(8,128)}, f32[2256,128]{1,0:T(8,128)S(1)}, u32[]{:S(2)}, u32[]{:S(2)}) collective-permute-start(f32[2256,128]{1,0:T(8,128)} %get-tuple-element.8), channel_id=1, source_target_pairs={{0,8},{8,16},{16,24},{24,32},{32,40},{40,48},{48,56},{56,64},{64,7... | collective-permute-start | bytes 3465224 | tf_op jit(solution)/shard_map/ppermute | solution.py:351
  7.7 29.1 %collective-permute-start.1 = (f32[2256,128]{1,0:T(8,128)}, f32[2256,128]{1,0:T(8,128)S(1)}, u32[]{:S(2)}, u32[]{:S(2)}) collective-permute-start(f32[2256,128]{1,0:T(8,128)} %get-tuple-element.9), channel_id=1, source_target_pairs={{8,0},{16,8},{24,16},{32,24},{40,32},{48,40},{56,48},{64,56},{72,6... | collective-permute-start | bytes 3465224 | tf_op jit(solution)/shard_map/ppermute | solution.py:351
  32.6 4.2 %copy-start = (f32[2256,128]{1,0:T(8,128)}, f32[2256,128]{1,0:T(8,128)S(1)}, u32[]{:S(2)}) copy-start(f32[2256,128]{1,0:T(8,128)S(1)} %collective-permute-done.low_ref) | copy-start | bytes 3465220
  36.8 1.0 copy-start.1
  44.8 3.0 %collective-permute-start.2 = (f32[24,40,128]{2,1,0:T(8,128)}, f32[24,40,128]{2,1,0:T(8,128)S(1)}, u32[]{:S(2)}, u32[]{:S(2)}) collective-permute-start(f32[24,40,128]{2,1,0:T(8,128)} %get-tuple-element.10), channel_id=1, source_target_pairs={{0,1},{1,2},{2,3},{3,4},{4,5},{5,6},{6,7},{8,9},{9,10},{10,11},{11... | collective-permute-start | bytes 1474568 | tf_op jit(solution)/shard_map/ppermute | solution.py:351
  46.1 5.7 %collective-permute-start.3 = (f32[24,40,128]{2,1,0:T(8,128)}, f32[24,40,128]{2,1,0:T(8,128)S(1)}, u32[]{:S(2)}, u32[]{:S(2)}) collective-permute-start(f32[24,40,128]{2,1,0:T(8,128)} %get-tuple-element.11), channel_id=1, source_target_pairs={{1,0},{2,1},{3,2},{4,3},{5,4},{6,5},{7,6},{9,8},{10,9},{11,10},{12... | collective-permute-start | bytes 1474568 | tf_op jit(solution)/shard_map/ppermute | solution.py:351
  47.8 4.1 %copy-start.3 = (f32[24,40,128]{2,1,0:T(8,128)}, f32[24,40,128]{2,1,0:T(8,128)S(1)}, u32[]{:S(2)}) copy-start(f32[24,40,128]{2,1,0:T(8,128)S(1)} %collective-permute-done.2.left_ref) | copy-start | bytes 1474564
  51.8 0.8 copy-start.4
  145.9 31.1 %all-to-all-start = ((f32[128,8,128]{2,1,0:T(8,128)}), f32[128,8,128]{2,1,0:T(8,128)S(1)}, u32[]{:S(2)}, u32[]{:S(2)}) async-start(f32[128,8,128]{2,1,0:T(8,128)} %broadcast_in_dim.3), calls=%async_computation | async-start | bytes 1048576 | tf_op jit(solution)/shard_map/all_to_all | solution.py:412
  177.0 0.8 copy-start.2

commit v3 on v2

--- a/solution.py
+++ b/solution.py
@@ -71,9 +71,7 @@
     return (axial_ref if plane == V * V else radial_ref)[pl.ds(row, 8), :]
 
 
-def pack_radial_kernel(
-    field_ref, coupling_ref, axial_ref, radial_ref, low_ref, high_ref, right_ref, left_ref
-):
+def pack_radial_kernel(field_ref, coupling_ref, axial_ref, radial_ref, right_ref, left_ref):
     planes, length, _ = field_ref.shape
     groups = planes // (V * PER)
     lane = lanes_of((8, 128))
@@ -90,29 +88,37 @@
         right_ref[slot, pl.ds(row, 8), :] = merge(tiles, WIDTH)
         left_ref[slot, pl.ds(row, 8), :] = merge(tiles, 2)
 
-    @pl.loop(0, groups * V)
-    def _(slot):
-        group, v = slot // V, slot % V
-        for source, row, target in chunks(length):
-            tiles = []
-            for j in range(PER):
-                plane = (group * PER + j) * V + v
-                if source == 1:
-                    tiles.append(field_ref[plane, pl.ds(row, 8), :])
-                else:
-                    ref = low_ref if source == 0 else high_ref
-                    tiles.append(ref[pl.ds(plane * WIDTH + row, 8), :])
-            put(slot, target, tiles)
+    @pl.loop(0, groups)
+    def _(group):
+        for v in range(V):
+            for row in range(0, length, 8):
+                put(
+                    group * V + v,
+                    row,
+                    [field_ref[(group * PER + j) * V + v, pl.ds(row, 8), :] for j in range(PER)],
+                )
 
     for slot in range(-(-PLANES // PER)):
-        for source, row, target in chunks(length):
+        for row in range(0, length, 8):
             tiles = [
-                coefficient(
-                    plane, source, row, planes, coupling_ref, axial_ref, radial_ref, low_ref, high_ref
-                )
+                coefficient(plane, 1, row, planes, coupling_ref, axial_ref, radial_ref, None, None)
                 for plane in range(slot * PER, min(PLANES, (slot + 1) * PER))
             ]
-            put(groups * V + slot, target, tiles)
+            put(groups * V + slot, row, tiles)
+
+
+def pack_corner_kernel(left_ref, right_ref, up_ref, down_ref):
+    slots, length, _ = left_ref.shape
+    low = length - WIDTH
+    for side, ref in ((0, left_ref), (1, right_ref)):
+        for slot in range(slots):
+            base = (side * slots + slot) * WIDTH
+            for start in range(0, WIDTH, 8):
+                size = min(8, WIDTH - start)
+                up_ref[base + start : base + start + size, :] = ref[
+                    slot, low + start : low + start + size, :
+                ]
+                down_ref[base + start : base + start + size, :] = ref[slot, start : start + size, :]
 
 
 def weights_of(raw, viscosity):
@@ -143,6 +149,8 @@
     high_ref,
     left_ref,
     right_ref,
+    rim_low_ref,
+    rim_high_ref,
     out_ref,
     now_ref,
     middle_ref,
@@ -171,11 +179,18 @@
                     value = ref[pl.ds(plane * WIDTH + row, 8), :]
                 now_ref[plane, pl.ds(target, 8), :] = value
 
-    @pl.loop(0, slots)
-    def _(slot):
-        for row in range(0, extended, 8):
-            now_rim_ref[0, slot, pl.ds(row, 8), :] = left_ref[slot, pl.ds(row, 8), :]
-            now_rim_ref[1, slot, pl.ds(row, 8), :] = right_ref[slot, pl.ds(row, 8), :]
+    packed = left_ref.shape[0]
+    for side, own_ref in ((0, left_ref), (1, right_ref)):
+
+        @pl.loop(0, packed)
+        def _(slot):
+            for source, row, target in chunks(length):
+                if source == 1:
+                    value = own_ref[slot, pl.ds(row, 8), :]
+                else:
+                    ref = rim_low_ref if source == 0 else rim_high_ref
+                    value = ref[pl.ds((side * packed + slot) * WIDTH + row, 8), :]
+                now_rim_ref[side, slot, pl.ds(target, 8), :] = value
 
     for source, row, target in chunks(length):
         raw = [
@@ -190,10 +205,10 @@
     @pl.loop(0, extended // 8)
     def _(block):
         start = pl.multiple_of(block * 8, 8)
-        for side, ref in ((0, left_ref), (1, right_ref)):
+        for side in range(2):
             raw = []
             for plane in range(PLANES):
-                tile = ref[slots + plane // PER, pl.ds(start, 8), :]
+                tile = now_rim_ref[side, slots + plane // PER, pl.ds(start, 8), :]
                 tile = pltpu.roll(tile, (128 - GROUP * (plane % PER)) % 128, axis=1)
                 tile = jnp.where(lane < GROUP, tile, 0.0)
                 reach = GROUP
@@ -311,7 +326,7 @@
                             target[bases[i] + v, pl.ds(start, 8), :] = value
 
 
-TOGETHER = 2
+TOGETHER = 8
 
 
 def factor_kernel(parts_ref, factor_ref, inverse_ref, *, rows_all):
@@ -353,10 +368,29 @@
     )
 
 
+def steps_call(viscosity, local, *received):
+    planes, length, columns = local[0].shape
+    rows = length + 2 * WIDTH + 8
+    return pl.pallas_call(
+        steps_kernel,
+        in_specs=[pl.BlockSpec(memory_space=pltpu.SMEM)] + whole(10),
+        out_specs=whole(1)[0],
+        out_shape=shape_of(planes, length, columns),
+        scratch_shapes=[
+            pltpu.VMEM((planes, rows, columns), jnp.float32),
+            pltpu.VMEM((planes, rows, columns), jnp.float32),
+            pltpu.VMEM((2, received[2].shape[0], rows, columns), jnp.float32),
+            pltpu.VMEM((2, planes // PER, rows, columns), jnp.float32),
+            pltpu.VMEM((3, WEIGHTS, rows, columns), jnp.float32),
+        ],
+        compiler_params=pltpu.CompilerParams(vmem_limit_bytes=VMEM_LIMIT),
+        name="steps",
+    )(viscosity, *local, *received)
+
+
 def per_device(forcing, vel_axial, vel_radial, coupling, viscosity):
     vectors, variables, length, columns = forcing.shape
     planes = vectors * variables
-    extended = length + 2 * WIDTH
     field = forcing.reshape(planes, length, columns)
     local = (field, coupling.reshape(V * V, length, columns), vel_axial, vel_radial)
     params = pltpu.CompilerParams(vmem_limit_bytes=VMEM_LIMIT)
@@ -373,35 +407,30 @@
     low = shifted(up, "ax", 1)
     high = shifted(down, "ax", -1)
 
-    rim_slots = planes // PER + -(-PLANES // PER)
-    rim = shape_of(rim_slots, extended, columns)
+    rim = shape_of(planes // PER + -(-PLANES // PER), length, columns)
     to_right, to_left = pl.pallas_call(
         pack_radial_kernel,
-        in_specs=whole(6),
+        in_specs=whole(4),
         out_specs=whole(2),
         out_shape=(rim, rim),
         compiler_params=params,
         name="pack_radial",
-    )(*local, low, high)
+    )(*local)
     left = shifted(to_right, "rad", 1)
     right = shifted(to_left, "rad", -1)
 
-    rows = extended + 8
-    response = pl.pallas_call(
-        steps_kernel,
-        in_specs=[pl.BlockSpec(memory_space=pltpu.SMEM)] + whole(8),
-        out_specs=whole(1)[0],
-        out_shape=shape_of(planes, length, columns),
-        scratch_shapes=[
-            pltpu.VMEM((planes, rows, columns), jnp.float32),
-            pltpu.VMEM((planes, rows, columns), jnp.float32),
-            pltpu.VMEM((2, planes // PER, rows, columns), jnp.float32),
-            pltpu.VMEM((2, planes // PER, rows, columns), jnp.float32),
-            pltpu.VMEM((3, WEIGHTS, rows, columns), jnp.float32),
-        ],
+    corner = shape_of(2 * rim.shape[0] * WIDTH, columns)
+    rim_up, rim_down = pl.pallas_call(
+        pack_corner_kernel,
+        in_specs=whole(2),
+        out_specs=whole(2),
+        out_shape=(corner, corner),
         compiler_params=params,
-        name="steps",
-    )(viscosity, *local, low, high, left, right)
+        name="pack_corner",
+    )(left, right)
+    rim_low = shifted(rim_up, "ax", 1)
+    rim_high = shifted(rim_down, "ax", -1)
+    response = steps_call(viscosity, local, low, high, left, right, rim_low, rim_high)
 
     flattened = response.reshape(vectors, variables * length * columns)
     devices = lax.axis_size("ax") * lax.axis_size("rad")

time: 187 us -> 139 us (0.74)
  Pallas kernels: 104 us -> 67.5 us
  waiting for transfers between devices: 45.6 us -> 32.9 us
    pallas_call x2 -> x3, Pallas kernels: 96.6 us -> 59.8 us  [the longest x1 54.6 us: steps_call(): pl.pallas_call(steps_kernel, in_specs=[pl.BlockSpec(memory_space=pltpu.SM...]
    ppermute x4 -> x6, waiting for transfers between devices: 32.3 us -> 19.6 us  [shifted(): lax.ppermute(block, axis, [(i, i + step) for i in range(size) if 0 <= i +...]
    all_to_all x1, starting transfers between devices: 17.6 us -> 11.4 us  [per_device(): parts = lax.all_to_all(copies, ('ax', 'rad'), 0, 0)]
    ppermute x4 -> x6, starting transfers between devices: 7.86 us -> 13.9 us  [shifted(): lax.ppermute(block, axis, [(i, i + step) for i in range(size) if 0 <= i +...]
    unnamed x12 -> x16, local copies, waits for them, and re-layouts: 4.65 us -> 5.68 us
  transfers between devices with their start and end apart: 5 -> 7, of which waited for: 5 -> 4; matrix products, arithmetic and copies ran while one was open for 0% -> 0% of each run, Pallas kernels for 0% -> 4%
where the time goes in v3:
time: 139 us; the launch traced here: 138 us
  Pallas kernels  67.5 us (49%)
  waiting for transfers between devices  32.9 us (24%)
  starting transfers between devices  25.2 us (18%)
  local copies, waits for them, and re-layouts  8.03 us (6%)
  matrix products  3.35 us (2%)
    pallas_call x1, Pallas kernels, steps_call(): pl.pallas_call(steps_kernel, in_specs=[pl.BlockSpec(memory_space=pltpu.SM...  54.6 us
    ppermute x6, waiting for transfers between devices, shifted(): lax.ppermute(block, axis, [(i, i + step) for i in range(size) if 0 <= i +...  19.6 us
    ppermute x6, starting transfers between devices, shifted(): lax.ppermute(block, axis, [(i, i + step) for i in range(size) if 0 <= i +...  13.9 us
    all_to_all x1, waiting for transfers between devices, per_device(): parts = lax.all_to_all(copies, ('ax', 'rad'), 0, 0)  13.3 us
    all_to_all x1, starting transfers between devices, per_device(): parts = lax.all_to_all(copies, ('ax', 'rad'), 0, 0)  11.4 us
    unnamed x16, local copies, waits for them, and re-layouts  5.68 us
    pallas_call x1, Pallas kernels, factor_and_inverse(): pl.pallas_call(functools.partial(factor_kernel, rows_all=rows_all), out_s...  4.47 us
    pallas_call x1, Pallas kernels, per_device(): pl.pallas_call(pack_radial_kernel, in_specs=whole(4), out_specs=whole(2),...  3.3 us
  transfers between devices with their start and end apart: 7, of which 4 were waited for; matrix products, arithmetic and copies ran while one was open for 0% of the time, Pallas kernels for 4%

profile of v3, /device:TPU:0, one launch (start us, length us, event | category | flops | bytes accessed | tf_op | source)
XLA Modules:
  0.0 137.8 jit_solution(4737409630920050963)
XLA Ops:
  0.6 3.1 %pack_axial.1 = (f32[2256,128]{1,0:T(8,128)}, f32[2256,128]{1,0:T(8,128)}) custom-call(f32[160,16,128]{2,1,0:T(8,128)} %bitcast.16, f32[25,16,128]{2,1,0:T(8,128)} %bitcast.20, f32[16,128]{1,0:T(8,128)} %axial_ref.5, f32[16,128]{1,0:T(8,128)} %radial_ref.5), custom_call_target="tpu_custom_call" | custom-call | tf_op jit(solution)/shard_map/pack_axial/pallas_call | solution.py:399
  3.8 4.0 %collective-permute-start = (f32[2256,128]{1,0:T(8,128)}, f32[2256,128]{1,0:T(8,128)S(1)}, u32[]{:S(2)}, u32[]{:S(2)}) collective-permute-start(f32[2256,128]{1,0:T(8,128)} %get-tuple-element.10), channel_id=1, source_target_pairs={{0,8},{8,16},{16,24},{24,32},{32,40},{40,48},{48,56},{56,64},{64,7... | collective-permute-start | bytes 3465224 | tf_op jit(solution)/shard_map/ppermute | solution.py:366
  7.7 1.3 collective-permute-start.1
  9.0 3.3 %pack_radial.1 = (f32[24,16,128]{2,1,0:T(8,128)}, f32[24,16,128]{2,1,0:T(8,128)}) custom-call(f32[160,16,128]{2,1,0:T(8,128)} %bitcast.17, f32[25,16,128]{2,1,0:T(8,128)} %bitcast.21, f32[16,128]{1,0:T(8,128)} %axial_ref.5, f32[16,128]{1,0:T(8,128)} %radial_ref.5), custom_call_target="tpu_custom_call" | custom-call | tf_op jit(solution)/shard_map/pack_radial/pallas_call | solution.py:411
  12.3 1.5 %collective-permute-start.2 = (f32[24,16,128]{2,1,0:T(8,128)}, f32[24,16,128]{2,1,0:T(8,128)S(1)}, u32[]{:S(2)}, u32[]{:S(2)}) collective-permute-start(f32[24,16,128]{2,1,0:T(8,128)} %get-tuple-element.12), channel_id=1, source_target_pairs={{0,1},{1,2},{2,3},{3,4},{4,5},{5,6},{6,7},{8,9},{9,10},{10,11},{11... | collective-permute-start | bytes 589832 | tf_op jit(solution)/shard_map/ppermute | solution.py:366
  13.8 1.3 collective-permute-start.3
  15.1 0.0 collective-permute-done.2.left_ref
  15.1 0.0 copy-start.3
  15.1 3.9 %collective-permute-done.3.right_ref = f32[24,16,128]{2,1,0:T(8,128)S(1)} collective-permute-done((f32[24,16,128]{2,1,0:T(8,128)}, f32[24,16,128]{2,1,0:T(8,128)S(1)}, u32[]{:S(2)}, u32[]{:S(2)}) %collective-permute-start.3) | collective-permute-done | bytes 196640 | tf_op jit(solution)/shard_map/ppermute | solution.py:366
  19.0 0.7 copy-done.4
  19.7 1.9 %pack_corner.1 = (f32[576,128]{1,0:T(8,128)}, f32[576,128]{1,0:T(8,128)}) custom-call(f32[24,16,128]{2,1,0:T(8,128)} %copy-done.3, f32[24,16,128]{2,1,0:T(8,128)} %copy-done.4), custom_call_target="tpu_custom_call" | custom-call | tf_op jit(solution)/shard_map/pack_corner/pallas_call | solution.py:423
  21.6 4.6 %collective-permute-start.4 = (f32[576,128]{1,0:T(8,128)}, f32[576,128]{1,0:T(8,128)S(1)}, u32[]{:S(2)}, u32[]{:S(2)}) collective-permute-start(f32[576,128]{1,0:T(8,128)} %get-tuple-element.14), channel_id=1, source_target_pairs={{0,8},{8,16},{16,24},{24,32},{32,40},{40,48},{48,56},{56,64},{64,7... | collective-permute-start | bytes 884744 | tf_op jit(solution)/shard_map/ppermute | solution.py:366
  26.2 1.3 collective-permute-start.5
  27.5 11.5 %collective-permute-done.4.rim_low_ref = f32[576,128]{1,0:T(8,128)S(1)} collective-permute-done((f32[576,128]{1,0:T(8,128)}, f32[576,128]{1,0:T(8,128)S(1)}, u32[]{:S(2)}, u32[]{:S(2)}) %collective-permute-start.4) | collective-permute-done | bytes 294944 | tf_op jit(solution)/shard_map/ppermute | solution.py:366
  39.0 4.2 %collective-permute-done.5.rim_high_ref = f32[576,128]{1,0:T(8,128)S(1)} collective-permute-done((f32[576,128]{1,0:T(8,128)}, f32[576,128]{1,0:T(8,128)S(1)}, u32[]{:S(2)}, u32[]{:S(2)}) %collective-permute-start.5) | collective-permute-done | bytes 294944 | tf_op jit(solution)/shard_map/ppermute | solution.py:366
  43.2 0.0 collective-permute-done.low_ref
  43.2 0.0 collective-permute-done.1.high_ref
  43.2 0.7 copy-done.6
  43.9 0.4 copy-done.1
  44.3 1.0 copy-done.2
  45.4 54.6 %steps.1 = f32[160,16,128]{2,1,0:T(8,128)} custom-call(f32[5]{0:T(128)} %viscosity_ref.1, f32[160,16,128]{2,1,0:T(8,128)} %bitcast.18, f32[25,16,128]{2,1,0:T(8,128)} %bitcast.22, f32[16,128]{1,0:T(8,128)} %axial_ref.5, f32[16,128]{1,0:T(8,128)} %radial_ref.5, f32[2256,128]{1,0:T(8,128)} %copy-done.1, f32[2256,128]{1,0:T(8,128)} %copy-done.2, ...), custom_call_target="tpu_custom_call" | custom-call | tf_op jit(solution)/shard_map/steps/pallas_call | solution.py:374
  100.0 1.5 %reshape.17 = f32[32,10240]{1,0:T(8,128)S(1)} reshape(f32[160,16,128]{2,1,0:T(8,128)} %steps.1) | data formatting | bytes 2621440 | tf_op jit(solution)/shard_map/reshape | solution.py:435
  101.5 1.2 fusion.4
  102.7 0.1 pad_maximum_fusion
  102.7 0.8 broadcast_in_dim.3
  103.6 11.4 %all-to-all-start = ((f32[128,8,128]{2,1,0:T(8,128)}), f32[128,8,128]{2,1,0:T(8,128)S(1)}, u32[]{:S(2)}, u32[]{:S(2)}) async-start(f32[128,8,128]{2,1,0:T(8,128)} %broadcast_in_dim.3), calls=%async_computation | async-start | bytes 1048576 | tf_op jit(solution)/shard_map/all_to_all | solution.py:441
  114.9 0.2 copy.11
  115.2 13.3 %all-to-all-done.parts_ref = f32[128,8,128]{2,1,0:T(8,128)S(1)} async-done(((f32[128,8,128]{2,1,0:T(8,128)}), f32[128,8,128]{2,1,0:T(8,128)S(1)}, u32[]{:S(2)}, u32[]{:S(2)}) %all-to-all-start) | async-done | bytes 524320 | tf_op jit(solution)/shard_map/all_to_all | solution.py:441
  128.5 0.8 copy-done
  129.3 4.5 %factor.1 = (f32[32,32]{1,0:T(8,128)}, f32[32,32]{1,0:T(8,128)}) custom-call(f32[128,8,128]{2,1,0:T(8,128)} %copy-done), custom_call_target="tpu_custom_call" | custom-call | tf_op jit(solution)/shard_map/factor/pallas_call | solution.py:353
  133.8 2.2 %fusion = f32[32,5,16,128]{3,0,2,1:T(8,128)S(1)} fusion(f32[5,16,128,32]{2,1,0,3:T(8,128)S(1)} %bitcast.19, f32[32,32]{1,0:T(8,128)} %get-tuple-element.16), kind=kOutput, calls=%fused_computation | convolution fusion | flops 125829120 | bytes 2625536 | tf_op jit(solution)/shard_map/dot_general | solution.py:443
  136.0 1.8 %copy.9 = f32[32,5,16,128]{3,2,1,0:T(8,128)} copy(f32[32,5,16,128]{3,0,2,1:T(8,128)S(1)} %fusion) | data formatting | bytes 2621440
  (9 shorter events, 0.0 us)
Async XLA Ops:
  3.8 39.4 %collective-permute-start = (f32[2256,128]{1,0:T(8,128)}, f32[2256,128]{1,0:T(8,128)S(1)}, u32[]{:S(2)}, u32[]{:S(2)}) collective-permute-start(f32[2256,128]{1,0:T(8,128)} %get-tuple-element.10), channel_id=1, source_target_pairs={{0,8},{8,16},{16,24},{24,32},{32,40},{40,48},{48,56},{56,64},{64,7... | collective-permute-start | bytes 3465224 | tf_op jit(solution)/shard_map/ppermute | solution.py:366
  7.7 35.5 %collective-permute-start.1 = (f32[2256,128]{1,0:T(8,128)}, f32[2256,128]{1,0:T(8,128)S(1)}, u32[]{:S(2)}, u32[]{:S(2)}) collective-permute-start(f32[2256,128]{1,0:T(8,128)} %get-tuple-element.11), channel_id=1, source_target_pairs={{8,0},{16,8},{24,16},{32,24},{40,32},{48,40},{56,48},{64,56},{72,6... | collective-permute-start | bytes 3465224 | tf_op jit(solution)/shard_map/ppermute | solution.py:366
  12.3 2.8 %collective-permute-start.2 = (f32[24,16,128]{2,1,0:T(8,128)}, f32[24,16,128]{2,1,0:T(8,128)S(1)}, u32[]{:S(2)}, u32[]{:S(2)}) collective-permute-start(f32[24,16,128]{2,1,0:T(8,128)} %get-tuple-element.12), channel_id=1, source_target_pairs={{0,1},{1,2},{2,3},{3,4},{4,5},{5,6},{6,7},{8,9},{9,10},{10,11},{11... | collective-permute-start | bytes 589832 | tf_op jit(solution)/shard_map/ppermute | solution.py:366
  13.8 5.2 %collective-permute-start.3 = (f32[24,16,128]{2,1,0:T(8,128)}, f32[24,16,128]{2,1,0:T(8,128)S(1)}, u32[]{:S(2)}, u32[]{:S(2)}) collective-permute-start(f32[24,16,128]{2,1,0:T(8,128)} %get-tuple-element.13), channel_id=1, source_target_pairs={{1,0},{2,1},{3,2},{4,3},{5,4},{6,5},{7,6},{9,8},{10,9},{11,10},{12... | collective-permute-start | bytes 589832 | tf_op jit(solution)/shard_map/ppermute | solution.py:366
  15.1 3.9 %copy-start.3 = (f32[24,16,128]{2,1,0:T(8,128)}, f32[24,16,128]{2,1,0:T(8,128)S(1)}, u32[]{:S(2)}) copy-start(f32[24,16,128]{2,1,0:T(8,128)S(1)} %collective-permute-done.2.left_ref) | copy-start | bytes 589828
  19.0 0.7 copy-start.4
  21.6 17.4 %collective-permute-start.4 = (f32[576,128]{1,0:T(8,128)}, f32[576,128]{1,0:T(8,128)S(1)}, u32[]{:S(2)}, u32[]{:S(2)}) collective-permute-start(f32[576,128]{1,0:T(8,128)} %get-tuple-element.14), channel_id=1, source_target_pairs={{0,8},{8,16},{16,24},{24,32},{32,40},{40,48},{48,56},{56,64},{64,7... | collective-permute-start | bytes 884744 | tf_op jit(solution)/shard_map/ppermute | solution.py:366
  26.2 17.0 %collective-permute-start.5 = (f32[576,128]{1,0:T(8,128)}, f32[576,128]{1,0:T(8,128)S(1)}, u32[]{:S(2)}, u32[]{:S(2)}) collective-permute-start(f32[576,128]{1,0:T(8,128)} %get-tuple-element.15), channel_id=1, source_target_pairs={{8,0},{16,8},{24,16},{32,24},{40,32},{48,40},{56,48},{64,56},{72,6... | collective-permute-start | bytes 884744 | tf_op jit(solution)/shard_map/ppermute | solution.py:366
  39.0 4.2 %copy-start.5 = (f32[576,128]{1,0:T(8,128)}, f32[576,128]{1,0:T(8,128)S(1)}, u32[]{:S(2)}) copy-start(f32[576,128]{1,0:T(8,128)S(1)} %collective-permute-done.4.rim_low_ref) | copy-start | bytes 884740
  43.2 0.7 copy-start.6
  43.2 1.1 copy-start.1
  44.3 1.1 copy-start.2
  103.6 24.9 %all-to-all-start = ((f32[128,8,128]{2,1,0:T(8,128)}), f32[128,8,128]{2,1,0:T(8,128)S(1)}, u32[]{:S(2)}, u32[]{:S(2)}) async-start(f32[128,8,128]{2,1,0:T(8,128)} %broadcast_in_dim.3), calls=%async_computation | async-start | bytes 1048576 | tf_op jit(solution)/shard_map/all_to_all | solution.py:441
  128.5 0.8 copy-start

commit v4 on v3

--- a/solution.py
+++ b/solution.py
@@ -121,6 +121,15 @@
                 down_ref[base + start : base + start + size, :] = ref[slot, start : start + size, :]
 
 
+def neighbours(spread, speed):
+    return (
+        16.0 * spread + 8.0 * speed,
+        16.0 * spread - 8.0 * speed,
+        -spread - speed,
+        speed - spread,
+    )
+
+
 def weights_of(raw, viscosity):
     axial = raw[V * V] * (-TIME_STEP / 12.0)
     radial = raw[V * V + 1] * (-TIME_STEP / 12.0)
@@ -132,10 +141,7 @@
             value = raw[v * V + w] * TIME_STEP
             found.append(value + (1.0 - 60.0 * spread) if v == w else value)
         for speed in (axial, radial):
-            found.append(16.0 * spread + 8.0 * speed)
-            found.append(16.0 * spread - 8.0 * speed)
-            found.append(-spread - speed)
-            found.append(speed - spread)
+            found.extend(neighbours(spread, speed))
     return found
 
 
@@ -157,6 +163,10 @@
     now_rim_ref,
     middle_rim_ref,
     weight_ref,
+    edge_ref,
+    first_ref,
+    second_ref,
+    band_ref,
 ):
     planes, length, _ = field_ref.shape
     vectors = planes // V
@@ -166,6 +176,25 @@
     lane = lanes_of((8, 128))
     place = lane % GROUP
     viscosity = [viscosity_ref[v] for v in range(V)]
+
+    def spread_out(tile):
+        reach = GROUP
+        while reach < 128:
+            tile = tile + pltpu.roll(tile, reach, axis=1)
+            reach *= 2
+        return tile
+
+    shape = (128, 256)
+    offset = lax.broadcasted_iota(jnp.int32, shape, 0) - lax.broadcasted_iota(
+        jnp.int32, shape, 1
+    )
+    offset_column = lax.broadcasted_iota(jnp.int32, shape, 1)
+    band = jnp.zeros(shape, jnp.float32)
+    for gap, odd_part, even_part in ((1, 8.0, 16.0), (-1, -8.0, 16.0), (2, -1.0, -1.0), (-2, 1.0, -1.0)):
+        band = jnp.where((offset == gap) & (offset_column < 128), odd_part, band)
+        band = jnp.where((offset + 128 == gap) & (offset_column >= 128), even_part, band)
+    for part in range(SPLIT):
+        band_ref[pl.ds(128 * part, 128), :] = band.astype(jnp.bfloat16)
 
     @pl.loop(0, planes // 8)
     def _(block):
@@ -200,7 +229,30 @@
             for plane in range(PLANES)
         ]
         for index, value in enumerate(weights_of(raw, viscosity)):
-            weight_ref[0, index, pl.ds(target, 8), :] = value
+            if index % (V + 8) < V + 4:
+                weight_ref[0, index, pl.ds(target, 8), :] = value
+        near = (lane >= WIDTH - 2) & (lane < WIDTH + 2)
+        edge_speed, edge_inside = [
+            spread_out(jnp.where(near, pltpu.roll(raw[plane], WIDTH, axis=1), 0.0))
+            for plane in (V * V + 1, V * V + 2)
+        ]
+        edge_speed = edge_speed * (-TIME_STEP / 12.0)
+        keeps = (
+            place == WIDTH - 1,
+            place == WIDTH,
+            (place == WIDTH - 2) | (place == WIDTH - 1),
+            (place == WIDTH) | (place == WIDTH + 1),
+        )
+        for v in range(V):
+            spread = edge_inside * (viscosity[v] * (TIME_STEP / 12.0))
+            for kind, value in enumerate(neighbours(spread, edge_speed)):
+                edge_ref[v * 4 + kind, pl.ds(target, 8), :] = jnp.where(keeps[kind], value, 0.0)
+        radial = raw[V * V + 1] * (-TIME_STEP / 12.0)
+        weight_ref[0, V + 4, pl.ds(target, 8), :] = radial
+        for v in range(V):
+            weight_ref[0, v * (V + 8) + V + 5, pl.ds(target, 8), :] = raw[V * V + 2] * (
+                viscosity[v] * (TIME_STEP / 12.0)
+            )
 
     @pl.loop(0, extended // 8)
     def _(block):
@@ -210,12 +262,7 @@
             for plane in range(PLANES):
                 tile = now_rim_ref[side, slots + plane // PER, pl.ds(start, 8), :]
                 tile = pltpu.roll(tile, (128 - GROUP * (plane % PER)) % 128, axis=1)
-                tile = jnp.where(lane < GROUP, tile, 0.0)
-                reach = GROUP
-                while reach < 128:
-                    tile = tile + pltpu.roll(tile, reach, axis=1)
-                    reach *= 2
-                raw.append(tile)
+                raw.append(spread_out(jnp.where(lane < GROUP, tile, 0.0)))
             for index, value in enumerate(weights_of(raw, viscosity)):
                 weight_ref[1 + side, index, pl.ds(start, 8), :] = value
 
@@ -231,9 +278,15 @@
         for index, step in enumerate((1, -1, 2, -2)):
             factor = weight(V + index)
             totals = [totals[i] + factor * vertical(i, step) for i in range(count)]
-        for index, step in enumerate((1, -1, 2, -2)):
-            factor = weight(V + 4 + index)
-            totals = [totals[i] + factor * sideways(i, step) for i in range(count)]
+        if kind > 0:
+            for index, step in enumerate((1, -1, 2, -2)):
+                factor = weight(V + 4 + index)
+                totals = [totals[i] + factor * sideways(i, step) for i in range(count)]
+            return totals
+        speed, spread = weight_ref[0, V + 4, pl.ds(start, 8), :], weight(V + 5)
+        for i in range(count):
+            one, two, rim = sideways(i, 0)
+            totals[i] = ((totals[i] + rim) + speed * one) + spread * two
         return totals
 
     for section in range(1, SECTIONS + 1):
@@ -243,6 +296,22 @@
         target, target_rim = (middle_ref, middle_rim_ref) if odd else (now_ref, now_rim_ref)
         first = 2 * section
         blocks = -(-(extended - 2 * first) // 8)
+        low_row, high_row = first // 8 * 8, -(-(extended - first) // 8) * 8
+
+        @pl.loop(0, planes // BATCH)
+        def _(batch):
+            here = pl.ds(batch * BATCH, BATCH)
+            rest = source[here, low_row:high_row, :].reshape(BATCH * (high_row - low_row), 128)
+            halves = []
+            for part in range(SPLIT):
+                halves.append(rest.astype(jnp.bfloat16))
+                if part < SPLIT - 1:
+                    rest = rest - halves[-1].astype(jnp.float32)
+            both = jnp.dot(
+                jnp.concatenate(halves, axis=1), band_ref[...], preferred_element_type=jnp.float32
+            )
+            first_ref[here, low_row:high_row, :] = both[:, :128].reshape(BATCH, -1, 128)
+            second_ref[here, low_row:high_row, :] = both[:, 128:].reshape(BATCH, -1, 128)
 
         @pl.loop(0, groups * blocks)
         def _(index):
@@ -259,7 +328,14 @@
                 left = source_rim[0, slot, pl.ds(start, 8), :]
                 right = source_rim[1, slot, pl.ds(start, 8), :]
                 inner = (place == WIDTH) | (place == WIDTH + 1)
-                joints.append(jnp.where(inner, pltpu.roll(right, WIDTH - 2, axis=1), left))
+                joint = jnp.where(inner, pltpu.roll(right, WIDTH - 2, axis=1), left)
+                joints.append(
+                    sum(
+                        edge_ref[v * 4 + index, pl.ds(start, 8), :]
+                        * pltpu.roll(joint, (128 - step) % 128, axis=1)
+                        for index, step in enumerate((1, -1, 2, -2))
+                    )
+                )
                 if not last:
                     source_rim[0, slot, pl.ds(start, 8), :] = jnp.where(inner, own, left)
                     source_rim[1, slot, pl.ds(start, 8), :] = jnp.where(
@@ -286,8 +362,7 @@
                             value = 0.5 * (value + target_rim[side, slot + v, pl.ds(start, 8), :])
                         target_rim[side, slot + v, pl.ds(start, 8), :] = value
 
-            @pl.loop(0, PER // TOGETHER)
-            def _(part):
+            for part in range(PER // TOGETHER):
                 bases = [(group * PER + part * TOGETHER + i) * V for i in range(TOGETHER)]
                 centers = [
                     [source[base + w, pl.ds(start, 8), :] for w in range(V)] for base in bases
@@ -296,16 +371,20 @@
                     rims = [
                         pltpu.roll(
                             joints[v],
-                            256 - WIDTH - GROUP * (part * TOGETHER + i),
+                            (256 - WIDTH - GROUP * (part * TOGETHER + i)) % 128,
                             axis=1,
                         )
                         for i in range(TOGETHER)
                     ]
-                    edges = {1: lane == 0, 2: lane <= 1, -1: lane == 127, -2: lane >= 126}
+                    edge = (lane < 2) | (lane >= 126)
 
                     def sideways(i, step):
-                        tile = jnp.where(edges[step], rims[i], centers[i][v])
-                        return pltpu.roll(tile, (128 - step) % 128, axis=1)
+                        plane = bases[i] + v
+                        return (
+                            first_ref[plane, pl.ds(start, 8), :],
+                            second_ref[plane, pl.ds(start, 8), :],
+                            jnp.where(edge, rims[i], 0.0),
+                        )
 
                     values = euler(
                         v,
@@ -327,6 +406,8 @@
 
 
 TOGETHER = 8
+SPLIT = 2
+BATCH = 80
 
 
 def factor_kernel(parts_ref, factor_ref, inverse_ref, *, rows_all):
@@ -382,6 +463,10 @@
             pltpu.VMEM((2, received[2].shape[0], rows, columns), jnp.float32),
             pltpu.VMEM((2, planes // PER, rows, columns), jnp.float32),
             pltpu.VMEM((3, WEIGHTS, rows, columns), jnp.float32),
+            pltpu.VMEM((4 * V, rows, columns), jnp.float32),
+            pltpu.VMEM((planes, rows, columns), jnp.float32),
+            pltpu.VMEM((planes, rows, columns), jnp.float32),
+            pltpu.VMEM((SPLIT * columns, 2 * columns), jnp.bfloat16),
         ],
         compiler_params=pltpu.CompilerParams(vmem_limit_bytes=VMEM_LIMIT),
         name="steps",

time: 139 us -> 130 us (0.935)
  Pallas kernels: 67.5 us -> 58.6 us
    pallas_call x1, Pallas kernels: 54.6 us -> 45.7 us  [steps_call(): pl.pallas_call(steps_kernel, in_specs=[pl.BlockSpec(memory_space=pltpu.SM...]
where the time goes in v4:
time: 130 us; the launch traced here: 129 us
  Pallas kernels  58.6 us (45%)
  waiting for transfers between devices  32.9 us (25%)
  starting transfers between devices  25.2 us (19%)
  local copies, waits for them, and re-layouts  8.03 us (6%)
  matrix products  3.35 us (3%)
    pallas_call x1, Pallas kernels, steps_call(): pl.pallas_call(steps_kernel, in_specs=[pl.BlockSpec(memory_space=pltpu.SM...  45.7 us
    ppermute x6, waiting for transfers between devices, shifted(): lax.ppermute(block, axis, [(i, i + step) for i in range(size) if 0 <= i +...  19.6 us
    ppermute x6, starting transfers between devices, shifted(): lax.ppermute(block, axis, [(i, i + step) for i in range(size) if 0 <= i +...  13.9 us
    all_to_all x1, waiting for transfers between devices, per_device(): parts = lax.all_to_all(copies, ('ax', 'rad'), 0, 0)  13.3 us
    all_to_all x1, starting transfers between devices, per_device(): parts = lax.all_to_all(copies, ('ax', 'rad'), 0, 0)  11.4 us
    unnamed x16, local copies, waits for them, and re-layouts  5.68 us
    pallas_call x1, Pallas kernels, factor_and_inverse(): pl.pallas_call(functools.partial(factor_kernel, rows_all=rows_all), out_s...  4.47 us
    pallas_call x1, Pallas kernels, per_device(): pl.pallas_call(pack_radial_kernel, in_specs=whole(4), out_specs=whole(2),...  3.3 us
  transfers between devices with their start and end apart: 7, of which 4 were waited for; matrix products, arithmetic and copies ran while one was open for 0% of the time, Pallas kernels for 4%

profile of v4, /device:TPU:0, one launch (start us, length us, event | category | flops | bytes accessed | tf_op | source)
XLA Modules:
  0.0 128.9 jit_solution(2353056485578843945)
XLA Ops:
  0.6 3.1 %pack_axial.1 = (f32[2256,128]{1,0:T(8,128)}, f32[2256,128]{1,0:T(8,128)}) custom-call(f32[160,16,128]{2,1,0:T(8,128)} %bitcast.16, f32[25,16,128]{2,1,0:T(8,128)} %bitcast.20, f32[16,128]{1,0:T(8,128)} %axial_ref.5, f32[16,128]{1,0:T(8,128)} %radial_ref.5), custom_call_target="tpu_custom_call" | custom-call | tf_op jit(solution)/shard_map/pack_axial/pallas_call | solution.py:484
  3.8 4.0 %collective-permute-start = (f32[2256,128]{1,0:T(8,128)}, f32[2256,128]{1,0:T(8,128)S(1)}, u32[]{:S(2)}, u32[]{:S(2)}) collective-permute-start(f32[2256,128]{1,0:T(8,128)} %get-tuple-element.10), channel_id=1, source_target_pairs={{0,8},{8,16},{16,24},{24,32},{32,40},{40,48},{48,56},{56,64},{64,7... | collective-permute-start | bytes 3465224 | tf_op jit(solution)/shard_map/ppermute | solution.py:447
  7.7 1.3 %collective-permute-start.1 = (f32[2256,128]{1,0:T(8,128)}, f32[2256,128]{1,0:T(8,128)S(1)}, u32[]{:S(2)}, u32[]{:S(2)}) collective-permute-start(f32[2256,128]{1,0:T(8,128)} %get-tuple-element.11), channel_id=1, source_target_pairs={{8,0},{16,8},{24,16},{32,24},{40,32},{48,40},{56,48},{64,56},{72,6... | collective-permute-start | bytes 3465224 | tf_op jit(solution)/shard_map/ppermute | solution.py:447
  9.0 3.3 %pack_radial.1 = (f32[24,16,128]{2,1,0:T(8,128)}, f32[24,16,128]{2,1,0:T(8,128)}) custom-call(f32[160,16,128]{2,1,0:T(8,128)} %bitcast.17, f32[25,16,128]{2,1,0:T(8,128)} %bitcast.21, f32[16,128]{1,0:T(8,128)} %axial_ref.5, f32[16,128]{1,0:T(8,128)} %radial_ref.5), custom_call_target="tpu_custom_call" | custom-call | tf_op jit(solution)/shard_map/pack_radial/pallas_call | solution.py:496
  12.3 1.5 %collective-permute-start.2 = (f32[24,16,128]{2,1,0:T(8,128)}, f32[24,16,128]{2,1,0:T(8,128)S(1)}, u32[]{:S(2)}, u32[]{:S(2)}) collective-permute-start(f32[24,16,128]{2,1,0:T(8,128)} %get-tuple-element.12), channel_id=1, source_target_pairs={{0,1},{1,2},{2,3},{3,4},{4,5},{5,6},{6,7},{8,9},{9,10},{10,11},{11... | collective-permute-start | bytes 589832 | tf_op jit(solution)/shard_map/ppermute | solution.py:447
  13.8 1.3 %collective-permute-start.3 = (f32[24,16,128]{2,1,0:T(8,128)}, f32[24,16,128]{2,1,0:T(8,128)S(1)}, u32[]{:S(2)}, u32[]{:S(2)}) collective-permute-start(f32[24,16,128]{2,1,0:T(8,128)} %get-tuple-element.13), channel_id=1, source_target_pairs={{1,0},{2,1},{3,2},{4,3},{5,4},{6,5},{7,6},{9,8},{10,9},{11,10},{12... | collective-permute-start | bytes 589832 | tf_op jit(solution)/shard_map/ppermute | solution.py:447
  15.1 0.0 collective-permute-done.2.left_ref
  15.1 0.0 copy-start.3
  15.1 3.9 %collective-permute-done.3.right_ref = f32[24,16,128]{2,1,0:T(8,128)S(1)} collective-permute-done((f32[24,16,128]{2,1,0:T(8,128)}, f32[24,16,128]{2,1,0:T(8,128)S(1)}, u32[]{:S(2)}, u32[]{:S(2)}) %collective-permute-start.3) | collective-permute-done | bytes 196640 | tf_op jit(solution)/shard_map/ppermute | solution.py:447
  19.0 0.7 copy-done.4
  19.7 1.9 %pack_corner.1 = (f32[576,128]{1,0:T(8,128)}, f32[576,128]{1,0:T(8,128)}) custom-call(f32[24,16,128]{2,1,0:T(8,128)} %copy-done.3, f32[24,16,128]{2,1,0:T(8,128)} %copy-done.4), custom_call_target="tpu_custom_call" | custom-call | tf_op jit(solution)/shard_map/pack_corner/pallas_call | solution.py:508
  21.6 4.6 %collective-permute-start.4 = (f32[576,128]{1,0:T(8,128)}, f32[576,128]{1,0:T(8,128)S(1)}, u32[]{:S(2)}, u32[]{:S(2)}) collective-permute-start(f32[576,128]{1,0:T(8,128)} %get-tuple-element.14), channel_id=1, source_target_pairs={{0,8},{8,16},{16,24},{24,32},{32,40},{40,48},{48,56},{56,64},{64,7... | collective-permute-start | bytes 884744 | tf_op jit(solution)/shard_map/ppermute | solution.py:447
  26.2 1.3 %collective-permute-start.5 = (f32[576,128]{1,0:T(8,128)}, f32[576,128]{1,0:T(8,128)S(1)}, u32[]{:S(2)}, u32[]{:S(2)}) collective-permute-start(f32[576,128]{1,0:T(8,128)} %get-tuple-element.15), channel_id=1, source_target_pairs={{8,0},{16,8},{24,16},{32,24},{40,32},{48,40},{56,48},{64,56},{72,6... | collective-permute-start | bytes 884744 | tf_op jit(solution)/shard_map/ppermute | solution.py:447
  27.5 11.5 %collective-permute-done.4.rim_low_ref = f32[576,128]{1,0:T(8,128)S(1)} collective-permute-done((f32[576,128]{1,0:T(8,128)}, f32[576,128]{1,0:T(8,128)S(1)}, u32[]{:S(2)}, u32[]{:S(2)}) %collective-permute-start.4) | collective-permute-done | bytes 294944 | tf_op jit(solution)/shard_map/ppermute | solution.py:447
  39.0 4.2 %collective-permute-done.5.rim_high_ref = f32[576,128]{1,0:T(8,128)S(1)} collective-permute-done((f32[576,128]{1,0:T(8,128)}, f32[576,128]{1,0:T(8,128)S(1)}, u32[]{:S(2)}, u32[]{:S(2)}) %collective-permute-start.5) | collective-permute-done | bytes 294944 | tf_op jit(solution)/shard_map/ppermute | solution.py:447
  43.2 0.0 collective-permute-done.low_ref
  43.2 0.0 collective-permute-done.1.high_ref
  43.2 0.7 copy-done.6
  43.9 0.4 copy-done.1
  44.3 1.0 copy-done.2
  45.4 45.7 %steps.1 = f32[160,16,128]{2,1,0:T(8,128)} custom-call(f32[5]{0:T(128)} %viscosity_ref.1, f32[160,16,128]{2,1,0:T(8,128)} %bitcast.18, f32[25,16,128]{2,1,0:T(8,128)} %bitcast.22, f32[16,128]{1,0:T(8,128)} %axial_ref.5, f32[16,128]{1,0:T(8,128)} %radial_ref.5, f32[2256,128]{1,0:T(8,128)} %copy-done.1, f32[2256,128]{1,0:T(8,128)} %copy-done.2, ...), custom_call_target="tpu_custom_call" | custom-call | tf_op jit(solution)/shard_map/steps/pallas_call | solution.py:455
  91.1 1.5 %reshape.17 = f32[32,10240]{1,0:T(8,128)S(1)} reshape(f32[160,16,128]{2,1,0:T(8,128)} %steps.1) | data formatting | bytes 2621440 | tf_op jit(solution)/shard_map/reshape | solution.py:520
  92.6 1.2 fusion.4
  93.8 0.1 pad_maximum_fusion
  93.9 0.8 broadcast_in_dim.3
  94.7 11.4 %all-to-all-start = ((f32[128,8,128]{2,1,0:T(8,128)}), f32[128,8,128]{2,1,0:T(8,128)S(1)}, u32[]{:S(2)}, u32[]{:S(2)}) async-start(f32[128,8,128]{2,1,0:T(8,128)} %broadcast_in_dim.3), calls=%async_computation | async-start | bytes 1048576 | tf_op jit(solution)/shard_map/all_to_all | solution.py:526
  106.1 0.2 copy.11
  106.3 13.3 %all-to-all-done.parts_ref = f32[128,8,128]{2,1,0:T(8,128)S(1)} async-done(((f32[128,8,128]{2,1,0:T(8,128)}), f32[128,8,128]{2,1,0:T(8,128)S(1)}, u32[]{:S(2)}, u32[]{:S(2)}) %all-to-all-start) | async-done | bytes 524320 | tf_op jit(solution)/shard_map/all_to_all | solution.py:526
  119.6 0.8 copy-done
  120.4 4.5 %factor.1 = (f32[32,32]{1,0:T(8,128)}, f32[32,32]{1,0:T(8,128)}) custom-call(f32[128,8,128]{2,1,0:T(8,128)} %copy-done), custom_call_target="tpu_custom_call" | custom-call | tf_op jit(solution)/shard_map/factor/pallas_call | solution.py:434
  124.9 2.2 %fusion = f32[32,5,16,128]{3,0,2,1:T(8,128)S(1)} fusion(f32[5,16,128,32]{2,1,0,3:T(8,128)S(1)} %bitcast.19, f32[32,32]{1,0:T(8,128)} %get-tuple-element.16), kind=kOutput, calls=%fused_computation | convolution fusion | flops 125829120 | bytes 2625536 | tf_op jit(solution)/shard_map/dot_general | solution.py:528
  127.1 1.8 %copy.9 = f32[32,5,16,128]{3,2,1,0:T(8,128)} copy(f32[32,5,16,128]{3,0,2,1:T(8,128)S(1)} %fusion) | data formatting | bytes 2621440
  (9 shorter events, 0.0 us)
Async XLA Ops:
  3.8 39.4 %collective-permute-start = (f32[2256,128]{1,0:T(8,128)}, f32[2256,128]{1,0:T(8,128)S(1)}, u32[]{:S(2)}, u32[]{:S(2)}) collective-permute-start(f32[2256,128]{1,0:T(8,128)} %get-tuple-element.10), channel_id=1, source_target_pairs={{0,8},{8,16},{16,24},{24,32},{32,40},{40,48},{48,56},{56,64},{64,7... | collective-permute-start | bytes 3465224 | tf_op jit(solution)/shard_map/ppermute | solution.py:447
  7.7 35.5 %collective-permute-start.1 = (f32[2256,128]{1,0:T(8,128)}, f32[2256,128]{1,0:T(8,128)S(1)}, u32[]{:S(2)}, u32[]{:S(2)}) collective-permute-start(f32[2256,128]{1,0:T(8,128)} %get-tuple-element.11), channel_id=1, source_target_pairs={{8,0},{16,8},{24,16},{32,24},{40,32},{48,40},{56,48},{64,56},{72,6... | collective-permute-start | bytes 3465224 | tf_op jit(solution)/shard_map/ppermute | solution.py:447
  12.3 2.8 %collective-permute-start.2 = (f32[24,16,128]{2,1,0:T(8,128)}, f32[24,16,128]{2,1,0:T(8,128)S(1)}, u32[]{:S(2)}, u32[]{:S(2)}) collective-permute-start(f32[24,16,128]{2,1,0:T(8,128)} %get-tuple-element.12), channel_id=1, source_target_pairs={{0,1},{1,2},{2,3},{3,4},{4,5},{5,6},{6,7},{8,9},{9,10},{10,11},{11... | collective-permute-start | bytes 589832 | tf_op jit(solution)/shard_map/ppermute | solution.py:447
  13.8 5.2 %collective-permute-start.3 = (f32[24,16,128]{2,1,0:T(8,128)}, f32[24,16,128]{2,1,0:T(8,128)S(1)}, u32[]{:S(2)}, u32[]{:S(2)}) collective-permute-start(f32[24,16,128]{2,1,0:T(8,128)} %get-tuple-element.13), channel_id=1, source_target_pairs={{1,0},{2,1},{3,2},{4,3},{5,4},{6,5},{7,6},{9,8},{10,9},{11,10},{12... | collective-permute-start | bytes 589832 | tf_op jit(solution)/shard_map/ppermute | solution.py:447
  15.1 3.9 %copy-start.3 = (f32[24,16,128]{2,1,0:T(8,128)}, f32[24,16,128]{2,1,0:T(8,128)S(1)}, u32[]{:S(2)}) copy-start(f32[24,16,128]{2,1,0:T(8,128)S(1)} %collective-permute-done.2.left_ref) | copy-start | bytes 589828
  19.0 0.7 copy-start.4
  21.6 17.4 %collective-permute-start.4 = (f32[576,128]{1,0:T(8,128)}, f32[576,128]{1,0:T(8,128)S(1)}, u32[]{:S(2)}, u32[]{:S(2)}) collective-permute-start(f32[576,128]{1,0:T(8,128)} %get-tuple-element.14), channel_id=1, source_target_pairs={{0,8},{8,16},{16,24},{24,32},{32,40},{40,48},{48,56},{56,64},{64,7... | collective-permute-start | bytes 884744 | tf_op jit(solution)/shard_map/ppermute | solution.py:447
  26.2 17.0 %collective-permute-start.5 = (f32[576,128]{1,0:T(8,128)}, f32[576,128]{1,0:T(8,128)S(1)}, u32[]{:S(2)}, u32[]{:S(2)}) collective-permute-start(f32[576,128]{1,0:T(8,128)} %get-tuple-element.15), channel_id=1, source_target_pairs={{8,0},{16,8},{24,16},{32,24},{40,32},{48,40},{56,48},{64,56},{72,6... | collective-permute-start | bytes 884744 | tf_op jit(solution)/shard_map/ppermute | solution.py:447
  39.0 4.2 %copy-start.5 = (f32[576,128]{1,0:T(8,128)}, f32[576,128]{1,0:T(8,128)S(1)}, u32[]{:S(2)}) copy-start(f32[576,128]{1,0:T(8,128)S(1)} %collective-permute-done.4.rim_low_ref) | copy-start | bytes 884740
  43.2 0.7 copy-start.6
  43.2 1.1 copy-start.1
  44.3 1.1 copy-start.2
  94.7 24.9 %all-to-all-start = ((f32[128,8,128]{2,1,0:T(8,128)}), f32[128,8,128]{2,1,0:T(8,128)S(1)}, u32[]{:S(2)}, u32[]{:S(2)}) async-start(f32[128,8,128]{2,1,0:T(8,128)} %broadcast_in_dim.3), calls=%async_computation | async-start | bytes 1048576 | tf_op jit(solution)/shard_map/all_to_all | solution.py:526
  119.6 0.8 copy-start

commit v5 on v4

--- a/solution.py
+++ b/solution.py
@@ -13,6 +13,7 @@
 WIDTH = 2 * SECTIONS
 V = 5
 GROUP = 16
+PARTS = 2
 PER = 128 // GROUP
 PLANES = V * V + 3
 WEIGHTS = V * (V + 8)
@@ -27,8 +28,9 @@
     return lax.broadcasted_iota(jnp.int32, shape, 1)
 
 
-def pack_axial_kernel(field_ref, coupling_ref, axial_ref, radial_ref, up_ref, down_ref):
-    planes, length, _ = field_ref.shape
+def pack_axial_kernel(field_ref, coupling_ref, axial_ref, radial_ref, *refs, begin, end):
+    up_ref, down_ref = refs[-2:]
+    length = field_ref.shape[1]
     low = length - WIDTH
 
     def put(slot, read):
@@ -38,17 +40,19 @@
             up_ref[pl.ds(base + start, size), :] = read(low + start, size)
             down_ref[pl.ds(base + start, size), :] = read(start, size)
 
-    @pl.loop(0, planes // 8)
+    @pl.loop(0, (end - begin) // 8)
     def _(block):
         for inner in range(8):
-            plane = block * 8 + inner
-            put(plane, lambda start, size: field_ref[plane, pl.ds(start, size), :])
-
+            slot = block * 8 + inner
+            put(slot, lambda start, size: field_ref[begin + slot, pl.ds(start, size), :])
+
+    if begin > 0:
+        return
     for plane in range(V * V):
-        put(planes + plane, lambda start, size: coupling_ref[plane, pl.ds(start, size), :])
-    put(planes + V * V, lambda start, size: axial_ref[pl.ds(start, size), :])
-    put(planes + V * V + 1, lambda start, size: radial_ref[pl.ds(start, size), :])
-    put(planes + V * V + 2, lambda start, size: jnp.ones((size, 128), jnp.float32))
+        put(end + plane, lambda start, size: coupling_ref[plane, pl.ds(start, size), :])
+    put(end + V * V, lambda start, size: axial_ref[pl.ds(start, size), :])
+    put(end + V * V + 1, lambda start, size: radial_ref[pl.ds(start, size), :])
+    put(end + V * V + 2, lambda start, size: jnp.ones((size, 128), jnp.float32))
 
 
 def chunks(length):
@@ -107,7 +111,8 @@
             put(groups * V + slot, row, tiles)
 
 
-def pack_corner_kernel(left_ref, right_ref, up_ref, down_ref):
+def pack_corner_kernel(left_ref, right_ref, up_ref, down_ref, done_ref):
+    done_ref[...] = jnp.zeros(done_ref.shape, jnp.float32)
     slots, length, _ = left_ref.shape
     low = length - WIDTH
     for side, ref in ((0, left_ref), (1, right_ref)):
@@ -153,22 +158,28 @@
     radial_ref,
     low_ref,
     high_ref,
+    first_low_ref,
+    first_high_ref,
     left_ref,
     right_ref,
     rim_low_ref,
     rim_high_ref,
-    out_ref,
-    now_ref,
-    middle_ref,
-    now_rim_ref,
-    middle_rim_ref,
-    weight_ref,
-    edge_ref,
-    first_ref,
-    second_ref,
-    band_ref,
+    *rest,
+    turn,
 ):
-    planes, length, _ = field_ref.shape
+    (
+        out_ref,
+        now_ref,
+        middle_ref,
+        now_rim_ref,
+        middle_rim_ref,
+        weight_ref,
+        edge_ref,
+        first_ref,
+        second_ref,
+        band_ref,
+    ) = rest[-10:]
+    planes, length = field_ref.shape[0] // PARTS, field_ref.shape[1]
     vectors = planes // V
     groups = vectors // PER
     slots = groups * V
@@ -202,7 +213,7 @@
             plane = block * 8 + inner
             for source, row, target in chunks(length):
                 if source == 1:
-                    value = field_ref[plane, pl.ds(row, 8), :]
+                    value = field_ref[turn * planes + plane, pl.ds(row, 8), :]
                 else:
                     ref = low_ref if source == 0 else high_ref
                     value = ref[pl.ds(plane * WIDTH + row, 8), :]
@@ -211,20 +222,21 @@
     packed = left_ref.shape[0]
     for side, own_ref in ((0, left_ref), (1, right_ref)):
 
-        @pl.loop(0, packed)
+        @pl.loop(0, slots + packed - PARTS * slots)
         def _(slot):
+            place_in = jnp.where(slot < slots, slot + turn * slots, slot + (PARTS - 1) * slots)
             for source, row, target in chunks(length):
                 if source == 1:
-                    value = own_ref[slot, pl.ds(row, 8), :]
+                    value = own_ref[place_in, pl.ds(row, 8), :]
                 else:
                     ref = rim_low_ref if source == 0 else rim_high_ref
-                    value = ref[pl.ds((side * packed + slot) * WIDTH + row, 8), :]
+                    value = ref[pl.ds((side * packed + place_in) * WIDTH + row, 8), :]
                 now_rim_ref[side, slot, pl.ds(target, 8), :] = value
 
     for source, row, target in chunks(length):
         raw = [
             coefficient(
-                plane, source, row, planes, coupling_ref, axial_ref, radial_ref, low_ref, high_ref
+                plane, source, row, planes, coupling_ref, axial_ref, radial_ref, first_low_ref, first_high_ref
             )
             for plane in range(PLANES)
         ]
@@ -449,28 +461,35 @@
     )
 
 
-def steps_call(viscosity, local, *received):
+def steps_call(part, before, viscosity, local, *received):
     planes, length, columns = local[0].shape
     rows = length + 2 * WIDTH + 8
+    share = planes // PARTS
+    rim = (2, received[4].shape[0] - (PARTS - 1) * share // PER, rows, columns)
+    chained = [] if before is None else [before]
     return pl.pallas_call(
-        steps_kernel,
-        in_specs=[pl.BlockSpec(memory_space=pltpu.SMEM)] + whole(10),
-        out_specs=whole(1)[0],
+        functools.partial(steps_kernel, turn=part),
+        grid=(1,),
+        in_specs=[pl.BlockSpec(memory_space=pltpu.SMEM)]
+        + whole(12)
+        + [pl.BlockSpec(memory_space=pl.ANY) for _ in chained],
+        out_specs=pl.BlockSpec((share, length, columns), lambda i: (part, 0, 0)),
         out_shape=shape_of(planes, length, columns),
+        input_output_aliases={13: 0} if chained else {},
         scratch_shapes=[
-            pltpu.VMEM((planes, rows, columns), jnp.float32),
-            pltpu.VMEM((planes, rows, columns), jnp.float32),
-            pltpu.VMEM((2, received[2].shape[0], rows, columns), jnp.float32),
-            pltpu.VMEM((2, planes // PER, rows, columns), jnp.float32),
+            pltpu.VMEM((share, rows, columns), jnp.float32),
+            pltpu.VMEM((share, rows, columns), jnp.float32),
+            pltpu.VMEM(rim, jnp.float32),
+            pltpu.VMEM(rim, jnp.float32),
             pltpu.VMEM((3, WEIGHTS, rows, columns), jnp.float32),
             pltpu.VMEM((4 * V, rows, columns), jnp.float32),
-            pltpu.VMEM((planes, rows, columns), jnp.float32),
-            pltpu.VMEM((planes, rows, columns), jnp.float32),
+            pltpu.VMEM((share, rows, columns), jnp.float32),
+            pltpu.VMEM((share, rows, columns), jnp.float32),
             pltpu.VMEM((SPLIT * columns, 2 * columns), jnp.bfloat16),
         ],
         compiler_params=pltpu.CompilerParams(vmem_limit_bytes=VMEM_LIMIT),
-        name="steps",
-    )(viscosity, *local, *received)
+        name=f"steps_{part}",
+    )(viscosity, *local, *received, *chained)
 
 
 def per_device(forcing, vel_axial, vel_radial, coupling, viscosity):
@@ -480,17 +499,20 @@
     local = (field, coupling.reshape(V * V, length, columns), vel_axial, vel_radial)
     params = pltpu.CompilerParams(vmem_limit_bytes=VMEM_LIMIT)
 
-    strip = shape_of((planes + PLANES) * WIDTH, columns)
-    up, down = pl.pallas_call(
-        pack_axial_kernel,
-        in_specs=whole(4),
-        out_specs=whole(2),
-        out_shape=(strip, strip),
-        compiler_params=params,
-        name="pack_axial",
-    )(*local)
-    low = shifted(up, "ax", 1)
-    high = shifted(down, "ax", -1)
+    def packed(part, *after):
+        share = planes // PARTS
+        strip = shape_of((share + (PLANES if part == 0 else 0)) * WIDTH, columns)
+        return pl.pallas_call(
+            functools.partial(pack_axial_kernel, begin=part * share, end=(part + 1) * share),
+            in_specs=whole(4) + [pl.BlockSpec(memory_space=pl.ANY) for _ in after],
+            out_specs=whole(2),
+            out_shape=(strip, strip),
+            compiler_params=params,
+            name=f"pack_axial_{part}",
+        )(*local, *after)
+
+    up, down = packed(0)
+    halos = [(shifted(up, "ax", 1), shifted(down, "ax", -1))]
 
     rim = shape_of(planes // PER + -(-PLANES // PER), length, columns)
     to_right, to_left = pl.pallas_call(
@@ -505,17 +527,24 @@
     right = shifted(to_left, "rad", -1)
 
     corner = shape_of(2 * rim.shape[0] * WIDTH, columns)
-    rim_up, rim_down = pl.pallas_call(
+    rim_up, rim_down, corners_packed = pl.pallas_call(
         pack_corner_kernel,
         in_specs=whole(2),
-        out_specs=whole(2),
-        out_shape=(corner, corner),
+        out_specs=whole(3),
+        out_shape=(corner, corner, shape_of(8, columns)),
         compiler_params=params,
         name="pack_corner",
     )(left, right)
     rim_low = shifted(rim_up, "ax", 1)
     rim_high = shifted(rim_down, "ax", -1)
-    response = steps_call(viscosity, local, low, high, left, right, rim_low, rim_high)
+    response = None
+    for part in range(1, PARTS):
+        up, down = packed(part, corners_packed)
+        halos.append((shifted(up, "ax", 1), shifted(down, "ax", -1)))
+    for part in range(PARTS):
+        response = steps_call(
+            part, response, viscosity, local, *halos[part], *halos[0], left, right, rim_low, rim_high
+        )
 
     flattened = response.reshape(vectors, variables * length * columns)
     devices = lax.axis_size("ax") * lax.axis_size("rad")

time: 130 us -> 149 us (1.15)
  Pallas kernels: 58.6 us -> 69.7 us
  starting transfers between devices: 25.2 us -> 31.7 us
  local copies, waits for them, and re-layouts: 8.03 us -> 9.87 us
    pallas_call x3 -> x5, Pallas kernels: 50.8 us -> 62 us  [the longest x2 54.9 us: steps_call(): pl.pallas_call(functools.partial(steps_kernel, turn=part), grid=(1,), in_...]
    ppermute x6 -> x8, starting transfers between devices: 13.9 us -> 19.3 us  [shifted(): lax.ppermute(block, axis, [(i, i + step) for i in range(size) if 0 <= i +...]
    unnamed x16 -> x22, local copies, waits for them, and re-layouts: 5.68 us -> 7.53 us
    ppermute x6 -> x8, waiting for transfers between devices: 19.6 us -> 19.6 us  [shifted(): lax.ppermute(block, axis, [(i, i + step) for i in range(size) if 0 <= i +...]
  transfers between devices with their start and end apart: 7 -> 9, of which waited for: 4 -> 3; matrix products, arithmetic and copies ran while one was open for 0% -> 0% of each run, Pallas kernels for 4% -> 23%
where the time goes in v5:
time: 149 us; the launch traced here: 148 us
  Pallas kernels  69.7 us (47%)
  waiting for transfers between devices  33 us (22%)
  starting transfers between devices  31.7 us (21%)
  local copies, waits for them, and re-layouts  9.87 us (7%)
  matrix products  3.35 us (2%)
    pallas_call x2, Pallas kernels, steps_call(): pl.pallas_call(functools.partial(steps_kernel, turn=part), grid=(1,), in_...  54.9 us
    ppermute x8, waiting for transfers between devices, shifted(): lax.ppermute(block, axis, [(i, i + step) for i in range(size) if 0 <= i +...  19.6 us
    ppermute x8, starting transfers between devices, shifted(): lax.ppermute(block, axis, [(i, i + step) for i in range(size) if 0 <= i +...  19.3 us
    all_to_all x1, waiting for transfers between devices, per_device(): parts = lax.all_to_all(copies, ('ax', 'rad'), 0, 0)  13.3 us
    all_to_all x1, starting transfers between devices, per_device(): parts = lax.all_to_all(copies, ('ax', 'rad'), 0, 0)  12.4 us
    unnamed x22, local copies, waits for them, and re-layouts  7.53 us
    pallas_call x2, Pallas kernels, packed(): pl.pallas_call(functools.partial(pack_axial_kernel, begin=part * share, e...  5.18 us
    pallas_call x1, Pallas kernels, factor_and_inverse(): pl.pallas_call(functools.partial(factor_kernel, rows_all=rows_all), out_s...  4.47 us
  transfers between devices with their start and end apart: 9, of which 3 were waited for; matrix products, arithmetic and copies ran while one was open for 0% of the time, Pallas kernels for 23%

profile of v5, /device:TPU:0, one launch (start us, length us, event | category | flops | bytes accessed | tf_op | source)
XLA Modules:
  0.0 148.5 jit_solution(9520752315310337008)
XLA Ops:
  0.6 3.3 %pack_radial.1 = (f32[24,16,128]{2,1,0:T(8,128)}, f32[24,16,128]{2,1,0:T(8,128)}) custom-call(f32[160,16,128]{2,1,0:T(8,128)} %bitcast.15, f32[25,16,128]{2,1,0:T(8,128)} %bitcast.22, f32[16,128]{1,0:T(8,128)} %axial_ref.9, f32[16,128]{1,0:T(8,128)} %radial_ref.9), custom_call_target="tpu_custom_call" | custom-call | tf_op jit(solution)/shard_map/pack_radial/pallas_call | solution.py:518
  3.9 1.3 collective-permute-start
  5.2 1.3 collective-permute-start.1
  6.5 2.7 %pack_axial_0.1 = (f32[1296,128]{1,0:T(8,128)}, f32[1296,128]{1,0:T(8,128)}) custom-call(f32[160,16,128]{2,1,0:T(8,128)} %bitcast.16, f32[25,16,128]{2,1,0:T(8,128)} %bitcast.23, f32[16,128]{1,0:T(8,128)} %axial_ref.9, f32[16,128]{1,0:T(8,128)} %radial_ref.9), custom_call_target="tpu_custom_call" | custom-call | tf_op jit(solution)/shard_map/pack_axial_0/pallas_call | solution.py:505
  9.2 4.4 %collective-permute-start.4 = (f32[1296,128]{1,0:T(8,128)}, f32[1296,128]{1,0:T(8,128)S(1)}, u32[]{:S(2)}, u32[]{:S(2)}) collective-permute-start(f32[1296,128]{1,0:T(8,128)} %get-tuple-element.18), channel_id=1, source_target_pairs={{0,8},{8,16},{16,24},{24,32},{32,40},{40,48},{48,56},{56,64},{64,7... | collective-permute-start | bytes 1990664 | tf_op jit(solution)/shard_map/ppermute | solution.py:459
  13.6 1.3 collective-permute-start.5
  14.9 0.7 copy-done.3
  15.6 0.7 copy-done.4
  16.2 1.9 %pack_corner.1 = (f32[576,128]{1,0:T(8,128)}, f32[576,128]{1,0:T(8,128)}, f32[8,128]{1,0:T(8,128)}) custom-call(f32[24,16,128]{2,1,0:T(8,128)} %copy-done.3, f32[24,16,128]{2,1,0:T(8,128)} %copy-done.4), custom_call_target="tpu_custom_call" | custom-call | tf_op jit(solution)/shard_map/pack_corner/pallas_call | solution.py:530
  18.1 4.7 %collective-permute-start.6 = (f32[576,128]{1,0:T(8,128)}, f32[576,128]{1,0:T(8,128)S(1)}, u32[]{:S(2)}, u32[]{:S(2)}) collective-permute-start(f32[576,128]{1,0:T(8,128)} %get-tuple-element.20), channel_id=1, source_target_pairs={{0,8},{8,16},{16,24},{24,32},{32,40},{40,48},{48,56},{56,64},{64,7... | collective-permute-start | bytes 884744 | tf_op jit(solution)/shard_map/ppermute | solution.py:459
  22.8 2.5 %pack_axial_1.1 = (f32[960,128]{1,0:T(8,128)}, f32[960,128]{1,0:T(8,128)}) custom-call(f32[160,16,128]{2,1,0:T(8,128)} %bitcast.17, f32[25,16,128]{2,1,0:T(8,128)} %bitcast.24, f32[16,128]{1,0:T(8,128)} %axial_ref.9, f32[16,128]{1,0:T(8,128)} %radial_ref.9, f32[8,128]{1,0:T(8,128)} %get-tuple-element.15.refs_0_), custom_call_target="tpu_custom_call" | custom-call | tf_op jit(solution)/shard_map/pack_axial_1/pallas_call | solution.py:505
  25.3 3.8 %collective-permute-start.2 = (f32[960,128]{1,0:T(8,128)}, f32[960,128]{1,0:T(8,128)S(1)}, u32[]{:S(2)}, u32[]{:S(2)}) collective-permute-start(f32[960,128]{1,0:T(8,128)} %get-tuple-element.16), channel_id=1, source_target_pairs={{0,8},{8,16},{16,24},{24,32},{32,40},{40,48},{48,56},{56,64},{64,7... | collective-permute-start | bytes 1474568 | tf_op jit(solution)/shard_map/ppermute | solution.py:459
  29.1 1.3 collective-permute-start.3
  30.4 3.5 %collective-permute-done.6.rim_low_ref = f32[576,128]{1,0:T(8,128)S(1)} collective-permute-done((f32[576,128]{1,0:T(8,128)}, f32[576,128]{1,0:T(8,128)S(1)}, u32[]{:S(2)}, u32[]{:S(2)}) %collective-permute-start.6) | collective-permute-done | bytes 294944 | tf_op jit(solution)/shard_map/ppermute | solution.py:459
  33.9 1.3 collective-permute-start.7
  35.2 16.1 %collective-permute-done.7.rim_high_ref = f32[576,128]{1,0:T(8,128)S(1)} collective-permute-done((f32[576,128]{1,0:T(8,128)S(1)}, f32[576,128]{1,0:T(8,128)S(1)}, u32[]{:S(2)}, u32[]{:S(2)}) %collective-permute-start.7) | collective-permute-done | bytes 294944 | tf_op jit(solution)/shard_map/ppermute | solution.py:459
  51.4 0.7 copy-done.6
  52.3 0.9 copy-done.1
  53.2 27.5 %steps_0.1.rest_0_ = f32[160,16,128]{2,1,0:T(8,128)} custom-call(f32[5]{0:T(128)} %viscosity_ref.3, f32[160,16,128]{2,1,0:T(8,128)} %bitcast.18, f32[25,16,128]{2,1,0:T(8,128)} %bitcast.25, f32[16,128]{1,0:T(8,128)} %axial_ref.9, f32[16,128]{1,0:T(8,128)} %radial_ref.9, f32[1296,128]{1,0:T(8,128)} %copy-done, f32[1296,128]{1,0:T(8,128)} %copy-done.1, ...), custom_call_target="tpu_custom_call" | custom-call | tf_op jit(solution)/shard_map/steps_0/pallas_call | solution.py:470
  80.6 0.8 copy-done.7
  81.4 0.8 copy-done.8
  82.2 27.4 %steps_1.1 = f32[160,16,128]{2,1,0:T(8,128)} custom-call(f32[5]{0:T(128)} %viscosity_ref.3, f32[160,16,128]{2,1,0:T(8,128)} %bitcast.19, f32[25,16,128]{2,1,0:T(8,128)} %bitcast.26, f32[16,128]{1,0:T(8,128)} %axial_ref.9, f32[16,128]{1,0:T(8,128)} %radial_ref.9, f32[960,128]{1,0:T(8,128)} %copy-done.7, ...), custom_call_target="tpu_custom_call", output_to_operand_aliasing={{}: (13, {})} | custom-call | tf_op jit(solution)/shard_map/steps_1/pallas_call | solution.py:470
  109.6 1.5 %reshape.17 = f32[32,10240]{1,0:T(8,128)S(1)} reshape(f32[160,16,128]{2,1,0:T(8,128)} %steps_1.1) | data formatting | bytes 2621440 | tf_op jit(solution)/shard_map/reshape | solution.py:549
  111.2 1.2 fusion.4
  112.4 0.8 broadcast_in_dim.3
  113.2 12.4 %all-to-all-start = ((f32[128,8,128]{2,1,0:T(8,128)}), f32[128,8,128]{2,1,0:T(8,128)S(1)}, u32[]{:S(2)}, u32[]{:S(2)}) async-start(f32[128,8,128]{2,1,0:T(8,128)} %broadcast_in_dim.3), calls=%async_computation | async-start | bytes 1048576 | tf_op jit(solution)/shard_map/all_to_all | solution.py:555
  125.6 0.2 copy.12
  125.9 13.3 %all-to-all-done.parts_ref = f32[128,8,128]{2,1,0:T(8,128)S(1)} async-done(((f32[128,8,128]{2,1,0:T(8,128)}), f32[128,8,128]{2,1,0:T(8,128)S(1)}, u32[]{:S(2)}, u32[]{:S(2)}) %all-to-all-start) | async-done | bytes 524320 | tf_op jit(solution)/shard_map/all_to_all | solution.py:555
  139.2 0.8 copy-done.2
  140.0 4.5 %factor.1 = (f32[32,32]{1,0:T(8,128)}, f32[32,32]{1,0:T(8,128)}) custom-call(f32[128,8,128]{2,1,0:T(8,128)} %copy-done.2), custom_call_target="tpu_custom_call" | custom-call | tf_op jit(solution)/shard_map/factor/pallas_call | solution.py:446
  144.5 2.2 %fusion = f32[32,5,16,128]{3,0,2,1:T(8,128)S(1)} fusion(f32[5,16,128,32]{2,1,0,3:T(8,128)S(1)} %bitcast.21, f32[32,32]{1,0:T(8,128)} %get-tuple-element.22), kind=kOutput, calls=%fused_computation | convolution fusion | flops 125829120 | bytes 2625536 | tf_op jit(solution)/shard_map/dot_general | solution.py:557
  146.7 1.8 %copy.10 = f32[32,5,16,128]{3,2,1,0:T(8,128)} copy(f32[32,5,16,128]{3,0,2,1:T(8,128)S(1)} %fusion) | data formatting | bytes 2621440
  (21 shorter events, 0.4 us)
Async XLA Ops:
  3.9 11.0 %collective-permute-start = (f32[24,16,128]{2,1,0:T(8,128)}, f32[24,16,128]{2,1,0:T(8,128)S(1)}, u32[]{:S(2)}, u32[]{:S(2)}) collective-permute-start(f32[24,16,128]{2,1,0:T(8,128)} %get-tuple-element.13), channel_id=1, source_target_pairs={{0,1},{1,2},{2,3},{3,4},{4,5},{5,6},{6,7},{8,9},{9,10},{10,11},{11... | collective-permute-start | bytes 589832 | tf_op jit(solution)/shard_map/ppermute | solution.py:459
  5.2 9.7 %collective-permute-start.1 = (f32[24,16,128]{2,1,0:T(8,128)}, f32[24,16,128]{2,1,0:T(8,128)S(1)}, u32[]{:S(2)}, u32[]{:S(2)}) collective-permute-start(f32[24,16,128]{2,1,0:T(8,128)} %get-tuple-element.14), channel_id=1, source_target_pairs={{1,0},{2,1},{3,2},{4,3},{5,4},{6,5},{7,6},{9,8},{10,9},{11,10},{12... | collective-permute-start | bytes 589832 | tf_op jit(solution)/shard_map/ppermute | solution.py:459
  9.2 42.1 %collective-permute-start.4 = (f32[1296,128]{1,0:T(8,128)}, f32[1296,128]{1,0:T(8,128)S(1)}, u32[]{:S(2)}, u32[]{:S(2)}) collective-permute-start(f32[1296,128]{1,0:T(8,128)} %get-tuple-element.18), channel_id=1, source_target_pairs={{0,8},{8,16},{16,24},{24,32},{32,40},{40,48},{48,56},{56,64},{64,7... | collective-permute-start | bytes 1990664 | tf_op jit(solution)/shard_map/ppermute | solution.py:459
  13.6 37.8 %collective-permute-start.5 = (f32[1296,128]{1,0:T(8,128)}, f32[1296,128]{1,0:T(8,128)S(1)}, u32[]{:S(2)}, u32[]{:S(2)}) collective-permute-start(f32[1296,128]{1,0:T(8,128)} %get-tuple-element.19), channel_id=1, source_target_pairs={{8,0},{16,8},{24,16},{32,24},{40,32},{48,40},{56,48},{64,56},{72,6... | collective-permute-start | bytes 1990664 | tf_op jit(solution)/shard_map/ppermute | solution.py:459
  14.9 0.7 copy-start.3
  15.6 0.7 copy-start.4
  18.1 15.8 %copy-start.9 = (f32[576,128]{1,0:T(8,128)S(1)}, f32[576,128]{1,0:T(8,128)}, u32[]{:S(2)}) copy-start(f32[576,128]{1,0:T(8,128)} %get-tuple-element.21) | copy-start | bytes 884740
  18.1 15.8 %collective-permute-start.6 = (f32[576,128]{1,0:T(8,128)}, f32[576,128]{1,0:T(8,128)S(1)}, u32[]{:S(2)}, u32[]{:S(2)}) collective-permute-start(f32[576,128]{1,0:T(8,128)} %get-tuple-element.20), channel_id=1, source_target_pairs={{0,8},{8,16},{16,24},{24,32},{32,40},{40,48},{48,56},{56,64},{64,7... | collective-permute-start | bytes 884744 | tf_op jit(solution)/shard_map/ppermute | solution.py:459
  25.3 55.3 %collective-permute-start.2 = (f32[960,128]{1,0:T(8,128)}, f32[960,128]{1,0:T(8,128)S(1)}, u32[]{:S(2)}, u32[]{:S(2)}) collective-permute-start(f32[960,128]{1,0:T(8,128)} %get-tuple-element.16), channel_id=1, source_target_pairs={{0,8},{8,16},{16,24},{24,32},{32,40},{40,48},{48,56},{56,64},{64,7... | collective-permute-start | bytes 1474568 | tf_op jit(solution)/shard_map/ppermute | solution.py:459
  29.1 51.5 %collective-permute-start.3 = (f32[960,128]{1,0:T(8,128)}, f32[960,128]{1,0:T(8,128)S(1)}, u32[]{:S(2)}, u32[]{:S(2)}) collective-permute-start(f32[960,128]{1,0:T(8,128)} %get-tuple-element.17), channel_id=1, source_target_pairs={{8,0},{16,8},{24,16},{32,24},{40,32},{48,40},{56,48},{64,56},{72,6... | collective-permute-start | bytes 1474568 | tf_op jit(solution)/shard_map/ppermute | solution.py:459
  33.9 17.5 %copy-start.5 = (f32[576,128]{1,0:T(8,128)}, f32[576,128]{1,0:T(8,128)S(1)}, u32[]{:S(2)}) copy-start(f32[576,128]{1,0:T(8,128)S(1)} %collective-permute-done.6.rim_low_ref) | copy-start | bytes 884740
  33.9 17.4 %collective-permute-start.7 = (f32[576,128]{1,0:T(8,128)S(1)}, f32[576,128]{1,0:T(8,128)S(1)}, u32[]{:S(2)}, u32[]{:S(2)}) collective-permute-start(f32[576,128]{1,0:T(8,128)S(1)} %copy-done.9), channel_id=1, source_target_pairs={{8,0},{16,8},{24,16},{32,24},{40,32},{48,40},{56,48},{64,56},{72,6... | collective-permute-start | bytes 884744 | tf_op jit(solution)/shard_map/ppermute | solution.py:459
  51.3 0.7 copy-start.6
  51.3 1.0 copy-start
  52.3 0.9 copy-start.1
  80.6 0.8 copy-start.7
  81.4 0.8 copy-start.8
  113.2 26.0 %all-to-all-start = ((f32[128,8,128]{2,1,0:T(8,128)}), f32[128,8,128]{2,1,0:T(8,128)S(1)}, u32[]{:S(2)}, u32[]{:S(2)}) async-start(f32[128,8,128]{2,1,0:T(8,128)} %broadcast_in_dim.3), calls=%async_computation | async-start | bytes 1048576 | tf_op jit(solution)/shard_map/all_to_all | solution.py:555
  139.2 0.8 copy-start.2

commit v6 on v4

--- a/solution.py
+++ b/solution.py
@@ -522,8 +522,11 @@
     rows_all = variables * length * columns * devices
     local_gram = jnp.dot(flattened, flattened.T, precision=lax.Precision.HIGHEST)
     packed = jnp.concatenate([local_gram[8 * i : 8 * i + 8] for i in range(4)], axis=1)
-    copies = jnp.broadcast_to(packed, (devices, 8, 128))
-    parts = lax.all_to_all(copies, ("ax", "rad"), 0, 0)
+    pairs = [(i, i ^ 1) for i in range(lax.axis_size("rad"))]
+    packed = packed + lax.ppermute(packed, "rad", pairs)
+    copies = jnp.broadcast_to(packed, (devices // 2, 8, 128))
+    halves = [list(range(parity, devices, 2)) for parity in range(2)]
+    parts = lax.all_to_all(copies, ("ax", "rad"), 0, 0, axis_index_groups=halves)
     upper_factor, lower_inverse = factor_and_inverse(parts, vectors, rows_all)
     basis = jnp.dot(lower_inverse, flattened, precision=lax.Precision.HIGHEST).reshape(forcing.shape)
     return (basis, upper_factor)

time: 130 us -> 128 us (0.985)
  waiting for transfers between devices: 32.9 us -> 31.2 us
    all_to_all x1, waiting for transfers between devices: 13.3 us -> 10.5 us  [per_device(): lax.all_to_all(copies, ('ax', 'rad'), 0, 0, axis_index_groups=halves)]
  transfers between devices with their start and end apart: 7 -> 8, of which waited for: 4 -> 5; matrix products, arithmetic and copies ran while one was open for 0% -> 0% of each run, Pallas kernels for 4% -> 4%
where the time goes in v6:
time: 128 us; the launch traced here: 127 us
  Pallas kernels  58.4 us (46%)
  waiting for transfers between devices  31.2 us (24%)
  starting transfers between devices  25.6 us (20%)
  local copies, waits for them, and re-layouts  7.8 us (6%)
  matrix products  3.35 us (3%)
    pallas_call x1, Pallas kernels, steps_call(): pl.pallas_call(steps_kernel, in_specs=[pl.BlockSpec(memory_space=pltpu.SM...  45.7 us
    ppermute x6, waiting for transfers between devices, shifted(): lax.ppermute(block, axis, [(i, i + step) for i in range(size) if 0 <= i +...  19.6 us
    ppermute x6, starting transfers between devices, shifted(): lax.ppermute(block, axis, [(i, i + step) for i in range(size) if 0 <= i +...  13.9 us
    all_to_all x1, starting transfers between devices, per_device(): lax.all_to_all(copies, ('ax', 'rad'), 0, 0, axis_index_groups=halves)  11.7 us
    all_to_all x1, waiting for transfers between devices, per_device(): lax.all_to_all(copies, ('ax', 'rad'), 0, 0, axis_index_groups=halves)  10.5 us
    unnamed x16, local copies, waits for them, and re-layouts  5.56 us
    pallas_call x1, Pallas kernels, factor_and_inverse(): pl.pallas_call(functools.partial(factor_kernel, rows_all=rows_all), out_s...  4.31 us
    pallas_call x1, Pallas kernels, per_device(): pl.pallas_call(pack_radial_kernel, in_specs=whole(4), out_specs=whole(2),...  3.3 us
  transfers between devices with their start and end apart: 8, of which 5 were waited for; matrix products, arithmetic and copies ran while one was open for 0% of the time, Pallas kernels for 4%

profile of v6, /device:TPU:0, one launch (start us, length us, event | category | flops | bytes accessed | tf_op | source)
XLA Modules:
  0.0 127.3 jit_solution(4149070652580851392)
XLA Ops:
  0.6 3.1 %pack_axial.1 = (f32[2256,128]{1,0:T(8,128)}, f32[2256,128]{1,0:T(8,128)}) custom-call(f32[160,16,128]{2,1,0:T(8,128)} %bitcast.16, f32[25,16,128]{2,1,0:T(8,128)} %bitcast.20, f32[16,128]{1,0:T(8,128)} %axial_ref.5, f32[16,128]{1,0:T(8,128)} %radial_ref.5), custom_call_target="tpu_custom_call" | custom-call | tf_op jit(solution)/shard_map/pack_axial/pallas_call | solution.py:484
  3.8 4.0 %collective-permute-start = (f32[2256,128]{1,0:T(8,128)}, f32[2256,128]{1,0:T(8,128)S(1)}, u32[]{:S(2)}, u32[]{:S(2)}) collective-permute-start(f32[2256,128]{1,0:T(8,128)} %get-tuple-element.10), channel_id=1, source_target_pairs={{0,8},{8,16},{16,24},{24,32},{32,40},{40,48},{48,56},{56,64},{64,7... | collective-permute-start | bytes 3465224 | tf_op jit(solution)/shard_map/ppermute | solution.py:447
  7.7 1.3 %collective-permute-start.1 = (f32[2256,128]{1,0:T(8,128)}, f32[2256,128]{1,0:T(8,128)S(1)}, u32[]{:S(2)}, u32[]{:S(2)}) collective-permute-start(f32[2256,128]{1,0:T(8,128)} %get-tuple-element.11), channel_id=1, source_target_pairs={{8,0},{16,8},{24,16},{32,24},{40,32},{48,40},{56,48},{64,56},{72,6... | collective-permute-start | bytes 3465224 | tf_op jit(solution)/shard_map/ppermute | solution.py:447
  9.0 3.3 %pack_radial.1 = (f32[24,16,128]{2,1,0:T(8,128)}, f32[24,16,128]{2,1,0:T(8,128)}) custom-call(f32[160,16,128]{2,1,0:T(8,128)} %bitcast.17, f32[25,16,128]{2,1,0:T(8,128)} %bitcast.21, f32[16,128]{1,0:T(8,128)} %axial_ref.5, f32[16,128]{1,0:T(8,128)} %radial_ref.5), custom_call_target="tpu_custom_call" | custom-call | tf_op jit(solution)/shard_map/pack_radial/pallas_call | solution.py:496
  12.3 1.5 %collective-permute-start.2 = (f32[24,16,128]{2,1,0:T(8,128)}, f32[24,16,128]{2,1,0:T(8,128)S(1)}, u32[]{:S(2)}, u32[]{:S(2)}) collective-permute-start(f32[24,16,128]{2,1,0:T(8,128)} %get-tuple-element.12), channel_id=1, source_target_pairs={{0,1},{1,2},{2,3},{3,4},{4,5},{5,6},{6,7},{8,9},{9,10},{10,11},{11... | collective-permute-start | bytes 589832 | tf_op jit(solution)/shard_map/ppermute | solution.py:447
  13.8 1.3 %collective-permute-start.3 = (f32[24,16,128]{2,1,0:T(8,128)}, f32[24,16,128]{2,1,0:T(8,128)S(1)}, u32[]{:S(2)}, u32[]{:S(2)}) collective-permute-start(f32[24,16,128]{2,1,0:T(8,128)} %get-tuple-element.13), channel_id=1, source_target_pairs={{1,0},{2,1},{3,2},{4,3},{5,4},{6,5},{7,6},{9,8},{10,9},{11,10},{12... | collective-permute-start | bytes 589832 | tf_op jit(solution)/shard_map/ppermute | solution.py:447
  15.1 0.0 collective-permute-done.2.left_ref
  15.1 3.9 %collective-permute-done.3.right_ref = f32[24,16,128]{2,1,0:T(8,128)S(1)} collective-permute-done((f32[24,16,128]{2,1,0:T(8,128)}, f32[24,16,128]{2,1,0:T(8,128)S(1)}, u32[]{:S(2)}, u32[]{:S(2)}) %collective-permute-start.3) | collective-permute-done | bytes 196640 | tf_op jit(solution)/shard_map/ppermute | solution.py:447
  19.0 0.7 copy-done.4
  19.7 1.9 %pack_corner.1 = (f32[576,128]{1,0:T(8,128)}, f32[576,128]{1,0:T(8,128)}) custom-call(f32[24,16,128]{2,1,0:T(8,128)} %copy-done.3, f32[24,16,128]{2,1,0:T(8,128)} %copy-done.4), custom_call_target="tpu_custom_call" | custom-call | tf_op jit(solution)/shard_map/pack_corner/pallas_call | solution.py:508
  21.6 4.6 %collective-permute-start.4 = (f32[576,128]{1,0:T(8,128)}, f32[576,128]{1,0:T(8,128)S(1)}, u32[]{:S(2)}, u32[]{:S(2)}) collective-permute-start(f32[576,128]{1,0:T(8,128)} %get-tuple-element.14), channel_id=1, source_target_pairs={{0,8},{8,16},{16,24},{24,32},{32,40},{40,48},{48,56},{56,64},{64,7... | collective-permute-start | bytes 884744 | tf_op jit(solution)/shard_map/ppermute | solution.py:447
  26.1 1.3 %collective-permute-start.5 = (f32[576,128]{1,0:T(8,128)}, f32[576,128]{1,0:T(8,128)S(1)}, u32[]{:S(2)}, u32[]{:S(2)}) collective-permute-start(f32[576,128]{1,0:T(8,128)} %get-tuple-element.15), channel_id=1, source_target_pairs={{8,0},{16,8},{24,16},{32,24},{40,32},{48,40},{56,48},{64,56},{72,6... | collective-permute-start | bytes 884744 | tf_op jit(solution)/shard_map/ppermute | solution.py:447
  27.4 11.5 %collective-permute-done.4.rim_low_ref = f32[576,128]{1,0:T(8,128)S(1)} collective-permute-done((f32[576,128]{1,0:T(8,128)}, f32[576,128]{1,0:T(8,128)S(1)}, u32[]{:S(2)}, u32[]{:S(2)}) %collective-permute-start.4) | collective-permute-done | bytes 294944 | tf_op jit(solution)/shard_map/ppermute | solution.py:447
  39.0 4.2 %collective-permute-done.5.rim_high_ref = f32[576,128]{1,0:T(8,128)S(1)} collective-permute-done((f32[576,128]{1,0:T(8,128)}, f32[576,128]{1,0:T(8,128)S(1)}, u32[]{:S(2)}, u32[]{:S(2)}) %collective-permute-start.5) | collective-permute-done | bytes 294944 | tf_op jit(solution)/shard_map/ppermute | solution.py:447
  43.2 0.0 collective-permute-done.1.high_ref
  43.2 0.7 copy-done.6
  43.9 0.4 copy-done
  44.3 1.0 copy-done.1
  45.3 45.7 %steps.1 = f32[160,16,128]{2,1,0:T(8,128)} custom-call(f32[5]{0:T(128)} %viscosity_ref.1, f32[160,16,128]{2,1,0:T(8,128)} %bitcast.18, f32[25,16,128]{2,1,0:T(8,128)} %bitcast.22, f32[16,128]{1,0:T(8,128)} %axial_ref.5, f32[16,128]{1,0:T(8,128)} %radial_ref.5, f32[2256,128]{1,0:T(8,128)} %copy-done, f32[2256,128]{1,0:T(8,128)} %copy-done.1, ...), custom_call_target="tpu_custom_call" | custom-call | tf_op jit(solution)/shard_map/steps/pallas_call | solution.py:455
  91.1 1.5 %reshape.17 = f32[32,10240]{1,0:T(8,128)S(1)} reshape(f32[160,16,128]{2,1,0:T(8,128)} %steps.1) | data formatting | bytes 2621440 | tf_op jit(solution)/shard_map/reshape | solution.py:520
  92.6 1.2 fusion.4
  93.8 0.1 pad_maximum_fusion
  93.8 0.0 collective-permute-start.6
  93.9 1.2 collective-permute-done.6
  95.0 0.7 broadcast_in_dim.3
  95.8 11.7 %all-to-all-start = ((f32[64,8,128]{2,1,0:T(8,128)}), f32[64,8,128]{2,1,0:T(8,128)S(1)}, u32[]{:S(2)}, u32[]{:S(2)}) async-start(f32[64,8,128]{2,1,0:T(8,128)} %broadcast_in_dim.3), calls=%async_computation | async-start | bytes 524288 | tf_op jit(solution)/shard_map/all_to_all | solution.py:529
  107.5 0.2 copy.11
  107.7 10.5 %all-to-all-done.parts_ref = f32[64,8,128]{2,1,0:T(8,128)S(1)} async-done(((f32[64,8,128]{2,1,0:T(8,128)}), f32[64,8,128]{2,1,0:T(8,128)S(1)}, u32[]{:S(2)}, u32[]{:S(2)}) %all-to-all-start) | async-done | bytes 262176 | tf_op jit(solution)/shard_map/all_to_all | solution.py:529
  118.2 0.7 copy-done.2
  118.9 4.3 %factor.1 = (f32[32,32]{1,0:T(8,128)}, f32[32,32]{1,0:T(8,128)}) custom-call(f32[64,8,128]{2,1,0:T(8,128)} %copy-done.2), custom_call_target="tpu_custom_call" | custom-call | tf_op jit(solution)/shard_map/factor/pallas_call | solution.py:434
  123.2 2.2 %fusion = f32[32,5,16,128]{3,0,2,1:T(8,128)S(1)} fusion(f32[5,16,128,32]{2,1,0,3:T(8,128)S(1)} %bitcast.19, f32[32,32]{1,0:T(8,128)} %get-tuple-element.16), kind=kOutput, calls=%fused_computation | convolution fusion | flops 125829120 | bytes 2625536 | tf_op jit(solution)/shard_map/dot_general | solution.py:531
  125.4 1.8 %copy.9 = f32[32,5,16,128]{3,2,1,0:T(8,128)} copy(f32[32,5,16,128]{3,0,2,1:T(8,128)S(1)} %fusion) | data formatting | bytes 2621440
  (12 shorter events, 0.0 us)
Async XLA Ops:
  3.8 39.4 %collective-permute-start = (f32[2256,128]{1,0:T(8,128)}, f32[2256,128]{1,0:T(8,128)S(1)}, u32[]{:S(2)}, u32[]{:S(2)}) collective-permute-start(f32[2256,128]{1,0:T(8,128)} %get-tuple-element.10), channel_id=1, source_target_pairs={{0,8},{8,16},{16,24},{24,32},{32,40},{40,48},{48,56},{56,64},{64,7... | collective-permute-start | bytes 3465224 | tf_op jit(solution)/shard_map/ppermute | solution.py:447
  7.7 35.5 %collective-permute-start.1 = (f32[2256,128]{1,0:T(8,128)}, f32[2256,128]{1,0:T(8,128)S(1)}, u32[]{:S(2)}, u32[]{:S(2)}) collective-permute-start(f32[2256,128]{1,0:T(8,128)} %get-tuple-element.11), channel_id=1, source_target_pairs={{8,0},{16,8},{24,16},{32,24},{40,32},{48,40},{56,48},{64,56},{72,6... | collective-permute-start | bytes 3465224 | tf_op jit(solution)/shard_map/ppermute | solution.py:447
  12.3 2.8 %collective-permute-start.2 = (f32[24,16,128]{2,1,0:T(8,128)}, f32[24,16,128]{2,1,0:T(8,128)S(1)}, u32[]{:S(2)}, u32[]{:S(2)}) collective-permute-start(f32[24,16,128]{2,1,0:T(8,128)} %get-tuple-element.12), channel_id=1, source_target_pairs={{0,1},{1,2},{2,3},{3,4},{4,5},{5,6},{6,7},{8,9},{9,10},{10,11},{11... | collective-permute-start | bytes 589832 | tf_op jit(solution)/shard_map/ppermute | solution.py:447
  13.8 5.2 %collective-permute-start.3 = (f32[24,16,128]{2,1,0:T(8,128)}, f32[24,16,128]{2,1,0:T(8,128)S(1)}, u32[]{:S(2)}, u32[]{:S(2)}) collective-permute-start(f32[24,16,128]{2,1,0:T(8,128)} %get-tuple-element.13), channel_id=1, source_target_pairs={{1,0},{2,1},{3,2},{4,3},{5,4},{6,5},{7,6},{9,8},{10,9},{11,10},{12... | collective-permute-start | bytes 589832 | tf_op jit(solution)/shard_map/ppermute | solution.py:447
  15.1 3.9 %copy-start.3 = (f32[24,16,128]{2,1,0:T(8,128)}, f32[24,16,128]{2,1,0:T(8,128)S(1)}, u32[]{:S(2)}) copy-start(f32[24,16,128]{2,1,0:T(8,128)S(1)} %collective-permute-done.2.left_ref) | copy-start | bytes 589828
  19.0 0.7 copy-start.4
  21.6 17.4 %collective-permute-start.4 = (f32[576,128]{1,0:T(8,128)}, f32[576,128]{1,0:T(8,128)S(1)}, u32[]{:S(2)}, u32[]{:S(2)}) collective-permute-start(f32[576,128]{1,0:T(8,128)} %get-tuple-element.14), channel_id=1, source_target_pairs={{0,8},{8,16},{16,24},{24,32},{32,40},{40,48},{48,56},{56,64},{64,7... | collective-permute-start | bytes 884744 | tf_op jit(solution)/shard_map/ppermute | solution.py:447
  26.1 17.0 %collective-permute-start.5 = (f32[576,128]{1,0:T(8,128)}, f32[576,128]{1,0:T(8,128)S(1)}, u32[]{:S(2)}, u32[]{:S(2)}) collective-permute-start(f32[576,128]{1,0:T(8,128)} %get-tuple-element.15), channel_id=1, source_target_pairs={{8,0},{16,8},{24,16},{32,24},{40,32},{48,40},{56,48},{64,56},{72,6... | collective-permute-start | bytes 884744 | tf_op jit(solution)/shard_map/ppermute | solution.py:447
  39.0 4.2 %copy-start.5 = (f32[576,128]{1,0:T(8,128)}, f32[576,128]{1,0:T(8,128)S(1)}, u32[]{:S(2)}) copy-start(f32[576,128]{1,0:T(8,128)S(1)} %collective-permute-done.4.rim_low_ref) | copy-start | bytes 884740
  43.2 0.7 copy-start.6
  43.2 1.1 copy-start
  44.3 1.0 copy-start.1
  93.8 1.2 collective-permute-start.6
  95.8 22.5 %all-to-all-start = ((f32[64,8,128]{2,1,0:T(8,128)}), f32[64,8,128]{2,1,0:T(8,128)S(1)}, u32[]{:S(2)}, u32[]{:S(2)}) async-start(f32[64,8,128]{2,1,0:T(8,128)} %broadcast_in_dim.3), calls=%async_computation | async-start | bytes 524288 | tf_op jit(solution)/shard_map/all_to_all | solution.py:529
  118.2 0.7 copy-start.2

commit v7 on v6

--- a/solution.py
+++ b/solution.py
@@ -418,11 +418,15 @@
     pieces = [total] + [pltpu.roll(total, 128 - 32 * i, axis=1) for i in range(1, 4)]
     work = jnp.concatenate(pieces, axis=0)
     work = jnp.where(lane < order, work, jnp.where(lane == row + order, 1.0, 0.0))
-    for j in range(order - 1):
-        pivot_row = work[j : j + 1, :]
-        scale = pivot_row / pivot_row[:, j : j + 1]
-        column = jnp.where(row > j, jnp.broadcast_to(work[:, j : j + 1], work.shape), 0.0)
-        work = work - column * scale
+    for j in range(0, order, 2):
+        one, two = work[j : j + 1, :], work[j + 1 : j + 2, :]
+        left, right = [jnp.broadcast_to(work[:, i : i + 1], work.shape) for i in (j, j + 1)]
+        scale = one / one[:, j : j + 1]
+        step = one[:, j + 1 : j + 2] / one[:, j : j + 1]
+        two_cleared = two - two[:, j : j + 1] * scale
+        pivot = two[:, j + 1 : j + 2] - two[:, j : j + 1] * step
+        lower = jnp.where(row > j + 1, left * scale + (right - left * step) * (two_cleared / pivot), 0.0)
+        work = jnp.where(row == j + 1, two_cleared, work - lower)
     diagonal = jnp.sum(jnp.where(lane == row, work, 0.0), axis=1, keepdims=True)
     work = work / jnp.sqrt(diagonal)
     factor_ref[...] = jnp.where(lane >= row, work, 0.0)[:, :order]

time: 128 us -> 130 us (1.016)
  Pallas kernels: 58.4 us -> 60.3 us
    pallas_call x1, Pallas kernels: 4.31 us -> 6.24 us  [factor_and_inverse(): pl.pallas_call(functools.partial(factor_kernel, rows_all=rows_all), out_s...]
where the time goes in v7:
time: 130 us; the launch traced here: 129 us
  Pallas kernels  60.3 us (46%)
  waiting for transfers between devices  31.2 us (24%)
  starting transfers between devices  25.6 us (20%)
  local copies, waits for them, and re-layouts  7.8 us (6%)
  matrix products  3.35 us (3%)
    pallas_call x1, Pallas kernels, steps_call(): pl.pallas_call(steps_kernel, in_specs=[pl.BlockSpec(memory_space=pltpu.SM...  45.7 us
    ppermute x6, waiting for transfers between devices, shifted(): lax.ppermute(block, axis, [(i, i + step) for i in range(size) if 0 <= i +...  19.6 us
    ppermute x6, starting transfers between devices, shifted(): lax.ppermute(block, axis, [(i, i + step) for i in range(size) if 0 <= i +...  13.9 us
    all_to_all x1, starting transfers between devices, per_device(): lax.all_to_all(copies, ('ax', 'rad'), 0, 0, axis_index_groups=halves)  11.7 us
    all_to_all x1, waiting for transfers between devices, per_device(): lax.all_to_all(copies, ('ax', 'rad'), 0, 0, axis_index_groups=halves)  10.5 us
    pallas_call x1, Pallas kernels, factor_and_inverse(): pl.pallas_call(functools.partial(factor_kernel, rows_all=rows_all), out_s...  6.24 us
    unnamed x16, local copies, waits for them, and re-layouts  5.56 us
    pallas_call x1, Pallas kernels, per_device(): pl.pallas_call(pack_radial_kernel, in_specs=whole(4), out_specs=whole(2),...  3.3 us
  transfers between devices with their start and end apart: 8, of which 5 were waited for; matrix products, arithmetic and copies ran while one was open for 0% of the time, Pallas kernels for 4%

profile of v7, /device:TPU:0, one launch (start us, length us, event | category | flops | bytes accessed | tf_op | source)
XLA Modules:
  0.0 129.2 jit_solution(12919610411311499968)
XLA Ops:
  0.6 3.1 %pack_axial.1 = (f32[2256,128]{1,0:T(8,128)}, f32[2256,128]{1,0:T(8,128)}) custom-call(f32[160,16,128]{2,1,0:T(8,128)} %bitcast.16, f32[25,16,128]{2,1,0:T(8,128)} %bitcast.20, f32[16,128]{1,0:T(8,128)} %axial_ref.5, f32[16,128]{1,0:T(8,128)} %radial_ref.5), custom_call_target="tpu_custom_call" | custom-call | tf_op jit(solution)/shard_map/pack_axial/pallas_call | solution.py:488
  3.8 4.0 %collective-permute-start = (f32[2256,128]{1,0:T(8,128)}, f32[2256,128]{1,0:T(8,128)S(1)}, u32[]{:S(2)}, u32[]{:S(2)}) collective-permute-start(f32[2256,128]{1,0:T(8,128)} %get-tuple-element.10), channel_id=1, source_target_pairs={{0,8},{8,16},{16,24},{24,32},{32,40},{40,48},{48,56},{56,64},{64,7... | collective-permute-start | bytes 3465224 | tf_op jit(solution)/shard_map/ppermute | solution.py:451
  7.7 1.3 %collective-permute-start.1 = (f32[2256,128]{1,0:T(8,128)}, f32[2256,128]{1,0:T(8,128)S(1)}, u32[]{:S(2)}, u32[]{:S(2)}) collective-permute-start(f32[2256,128]{1,0:T(8,128)} %get-tuple-element.11), channel_id=1, source_target_pairs={{8,0},{16,8},{24,16},{32,24},{40,32},{48,40},{56,48},{64,56},{72,6... | collective-permute-start | bytes 3465224 | tf_op jit(solution)/shard_map/ppermute | solution.py:451
  9.0 3.3 %pack_radial.1 = (f32[24,16,128]{2,1,0:T(8,128)}, f32[24,16,128]{2,1,0:T(8,128)}) custom-call(f32[160,16,128]{2,1,0:T(8,128)} %bitcast.17, f32[25,16,128]{2,1,0:T(8,128)} %bitcast.21, f32[16,128]{1,0:T(8,128)} %axial_ref.5, f32[16,128]{1,0:T(8,128)} %radial_ref.5), custom_call_target="tpu_custom_call" | custom-call | tf_op jit(solution)/shard_map/pack_radial/pallas_call | solution.py:500
  12.3 1.5 %collective-permute-start.2 = (f32[24,16,128]{2,1,0:T(8,128)}, f32[24,16,128]{2,1,0:T(8,128)S(1)}, u32[]{:S(2)}, u32[]{:S(2)}) collective-permute-start(f32[24,16,128]{2,1,0:T(8,128)} %get-tuple-element.12), channel_id=1, source_target_pairs={{0,1},{1,2},{2,3},{3,4},{4,5},{5,6},{6,7},{8,9},{9,10},{10,11},{11... | collective-permute-start | bytes 589832 | tf_op jit(solution)/shard_map/ppermute | solution.py:451
  13.8 1.3 %collective-permute-start.3 = (f32[24,16,128]{2,1,0:T(8,128)}, f32[24,16,128]{2,1,0:T(8,128)S(1)}, u32[]{:S(2)}, u32[]{:S(2)}) collective-permute-start(f32[24,16,128]{2,1,0:T(8,128)} %get-tuple-element.13), channel_id=1, source_target_pairs={{1,0},{2,1},{3,2},{4,3},{5,4},{6,5},{7,6},{9,8},{10,9},{11,10},{12... | collective-permute-start | bytes 589832 | tf_op jit(solution)/shard_map/ppermute | solution.py:451
  15.1 0.0 collective-permute-done.2.left_ref
  15.1 3.9 %collective-permute-done.3.right_ref = f32[24,16,128]{2,1,0:T(8,128)S(1)} collective-permute-done((f32[24,16,128]{2,1,0:T(8,128)}, f32[24,16,128]{2,1,0:T(8,128)S(1)}, u32[]{:S(2)}, u32[]{:S(2)}) %collective-permute-start.3) | collective-permute-done | bytes 196640 | tf_op jit(solution)/shard_map/ppermute | solution.py:451
  19.0 0.7 copy-done.4
  19.7 1.9 %pack_corner.1 = (f32[576,128]{1,0:T(8,128)}, f32[576,128]{1,0:T(8,128)}) custom-call(f32[24,16,128]{2,1,0:T(8,128)} %copy-done.3, f32[24,16,128]{2,1,0:T(8,128)} %copy-done.4), custom_call_target="tpu_custom_call" | custom-call | tf_op jit(solution)/shard_map/pack_corner/pallas_call | solution.py:512
  21.6 4.6 %collective-permute-start.4 = (f32[576,128]{1,0:T(8,128)}, f32[576,128]{1,0:T(8,128)S(1)}, u32[]{:S(2)}, u32[]{:S(2)}) collective-permute-start(f32[576,128]{1,0:T(8,128)} %get-tuple-element.14), channel_id=1, source_target_pairs={{0,8},{8,16},{16,24},{24,32},{32,40},{40,48},{48,56},{56,64},{64,7... | collective-permute-start | bytes 884744 | tf_op jit(solution)/shard_map/ppermute | solution.py:451
  26.1 1.3 %collective-permute-start.5 = (f32[576,128]{1,0:T(8,128)}, f32[576,128]{1,0:T(8,128)S(1)}, u32[]{:S(2)}, u32[]{:S(2)}) collective-permute-start(f32[576,128]{1,0:T(8,128)} %get-tuple-element.15), channel_id=1, source_target_pairs={{8,0},{16,8},{24,16},{32,24},{40,32},{48,40},{56,48},{64,56},{72,6... | collective-permute-start | bytes 884744 | tf_op jit(solution)/shard_map/ppermute | solution.py:451
  27.4 11.5 %collective-permute-done.4.rim_low_ref = f32[576,128]{1,0:T(8,128)S(1)} collective-permute-done((f32[576,128]{1,0:T(8,128)}, f32[576,128]{1,0:T(8,128)S(1)}, u32[]{:S(2)}, u32[]{:S(2)}) %collective-permute-start.4) | collective-permute-done | bytes 294944 | tf_op jit(solution)/shard_map/ppermute | solution.py:451
  39.0 4.2 %collective-permute-done.5.rim_high_ref = f32[576,128]{1,0:T(8,128)S(1)} collective-permute-done((f32[576,128]{1,0:T(8,128)}, f32[576,128]{1,0:T(8,128)S(1)}, u32[]{:S(2)}, u32[]{:S(2)}) %collective-permute-start.5) | collective-permute-done | bytes 294944 | tf_op jit(solution)/shard_map/ppermute | solution.py:451
  43.2 0.0 collective-permute-done.1.high_ref
  43.2 0.7 copy-done.6
  43.9 0.4 copy-done
  44.3 1.0 copy-done.1
  45.3 45.7 %steps.1 = f32[160,16,128]{2,1,0:T(8,128)} custom-call(f32[5]{0:T(128)} %viscosity_ref.1, f32[160,16,128]{2,1,0:T(8,128)} %bitcast.18, f32[25,16,128]{2,1,0:T(8,128)} %bitcast.22, f32[16,128]{1,0:T(8,128)} %axial_ref.5, f32[16,128]{1,0:T(8,128)} %radial_ref.5, f32[2256,128]{1,0:T(8,128)} %copy-done, f32[2256,128]{1,0:T(8,128)} %copy-done.1, ...), custom_call_target="tpu_custom_call" | custom-call | tf_op jit(solution)/shard_map/steps/pallas_call | solution.py:459
  91.1 1.5 %reshape.17 = f32[32,10240]{1,0:T(8,128)S(1)} reshape(f32[160,16,128]{2,1,0:T(8,128)} %steps.1) | data formatting | bytes 2621440 | tf_op jit(solution)/shard_map/reshape | solution.py:524
  92.6 1.2 fusion.4
  93.8 0.1 pad_maximum_fusion
  93.8 0.0 collective-permute-start.6
  93.9 1.2 collective-permute-done.6
  95.0 0.7 broadcast_in_dim.3
  95.8 11.7 %all-to-all-start = ((f32[64,8,128]{2,1,0:T(8,128)}), f32[64,8,128]{2,1,0:T(8,128)S(1)}, u32[]{:S(2)}, u32[]{:S(2)}) async-start(f32[64,8,128]{2,1,0:T(8,128)} %broadcast_in_dim.3), calls=%async_computation | async-start | bytes 524288 | tf_op jit(solution)/shard_map/all_to_all | solution.py:533
  107.5 0.2 copy.11
  107.7 10.5 %all-to-all-done.parts_ref = f32[64,8,128]{2,1,0:T(8,128)S(1)} async-done(((f32[64,8,128]{2,1,0:T(8,128)}), f32[64,8,128]{2,1,0:T(8,128)S(1)}, u32[]{:S(2)}, u32[]{:S(2)}) %all-to-all-start) | async-done | bytes 262176 | tf_op jit(solution)/shard_map/all_to_all | solution.py:533
  118.2 0.7 copy-done.2
  118.9 6.2 %factor.1 = (f32[32,32]{1,0:T(8,128)}, f32[32,32]{1,0:T(8,128)}) custom-call(f32[64,8,128]{2,1,0:T(8,128)} %copy-done.2), custom_call_target="tpu_custom_call" | custom-call | tf_op jit(solution)/shard_map/factor/pallas_call | solution.py:438
  125.2 2.2 %fusion = f32[32,5,16,128]{3,0,2,1:T(8,128)S(1)} fusion(f32[5,16,128,32]{2,1,0,3:T(8,128)S(1)} %bitcast.19, f32[32,32]{1,0:T(8,128)} %get-tuple-element.16), kind=kOutput, calls=%fused_computation | convolution fusion | flops 125829120 | bytes 2625536 | tf_op jit(solution)/shard_map/dot_general | solution.py:535
  127.4 1.8 %copy.9 = f32[32,5,16,128]{3,2,1,0:T(8,128)} copy(f32[32,5,16,128]{3,0,2,1:T(8,128)S(1)} %fusion) | data formatting | bytes 2621440
  (12 shorter events, 0.0 us)
Async XLA Ops:
  3.8 39.4 %collective-permute-start = (f32[2256,128]{1,0:T(8,128)}, f32[2256,128]{1,0:T(8,128)S(1)}, u32[]{:S(2)}, u32[]{:S(2)}) collective-permute-start(f32[2256,128]{1,0:T(8,128)} %get-tuple-element.10), channel_id=1, source_target_pairs={{0,8},{8,16},{16,24},{24,32},{32,40},{40,48},{48,56},{56,64},{64,7... | collective-permute-start | bytes 3465224 | tf_op jit(solution)/shard_map/ppermute | solution.py:451
  7.7 35.5 %collective-permute-start.1 = (f32[2256,128]{1,0:T(8,128)}, f32[2256,128]{1,0:T(8,128)S(1)}, u32[]{:S(2)}, u32[]{:S(2)}) collective-permute-start(f32[2256,128]{1,0:T(8,128)} %get-tuple-element.11), channel_id=1, source_target_pairs={{8,0},{16,8},{24,16},{32,24},{40,32},{48,40},{56,48},{64,56},{72,6... | collective-permute-start | bytes 3465224 | tf_op jit(solution)/shard_map/ppermute | solution.py:451
  12.3 2.8 %collective-permute-start.2 = (f32[24,16,128]{2,1,0:T(8,128)}, f32[24,16,128]{2,1,0:T(8,128)S(1)}, u32[]{:S(2)}, u32[]{:S(2)}) collective-permute-start(f32[24,16,128]{2,1,0:T(8,128)} %get-tuple-element.12), channel_id=1, source_target_pairs={{0,1},{1,2},{2,3},{3,4},{4,5},{5,6},{6,7},{8,9},{9,10},{10,11},{11... | collective-permute-start | bytes 589832 | tf_op jit(solution)/shard_map/ppermute | solution.py:451
  13.8 5.2 %collective-permute-start.3 = (f32[24,16,128]{2,1,0:T(8,128)}, f32[24,16,128]{2,1,0:T(8,128)S(1)}, u32[]{:S(2)}, u32[]{:S(2)}) collective-permute-start(f32[24,16,128]{2,1,0:T(8,128)} %get-tuple-element.13), channel_id=1, source_target_pairs={{1,0},{2,1},{3,2},{4,3},{5,4},{6,5},{7,6},{9,8},{10,9},{11,10},{12... | collective-permute-start | bytes 589832 | tf_op jit(solution)/shard_map/ppermute | solution.py:451
  15.1 3.9 %copy-start.3 = (f32[24,16,128]{2,1,0:T(8,128)}, f32[24,16,128]{2,1,0:T(8,128)S(1)}, u32[]{:S(2)}) copy-start(f32[24,16,128]{2,1,0:T(8,128)S(1)} %collective-permute-done.2.left_ref) | copy-start | bytes 589828
  19.0 0.7 copy-start.4
  21.6 17.4 %collective-permute-start.4 = (f32[576,128]{1,0:T(8,128)}, f32[576,128]{1,0:T(8,128)S(1)}, u32[]{:S(2)}, u32[]{:S(2)}) collective-permute-start(f32[576,128]{1,0:T(8,128)} %get-tuple-element.14), channel_id=1, source_target_pairs={{0,8},{8,16},{16,24},{24,32},{32,40},{40,48},{48,56},{56,64},{64,7... | collective-permute-start | bytes 884744 | tf_op jit(solution)/shard_map/ppermute | solution.py:451
  26.1 17.0 %collective-permute-start.5 = (f32[576,128]{1,0:T(8,128)}, f32[576,128]{1,0:T(8,128)S(1)}, u32[]{:S(2)}, u32[]{:S(2)}) collective-permute-start(f32[576,128]{1,0:T(8,128)} %get-tuple-element.15), channel_id=1, source_target_pairs={{8,0},{16,8},{24,16},{32,24},{40,32},{48,40},{56,48},{64,56},{72,6... | collective-permute-start | bytes 884744 | tf_op jit(solution)/shard_map/ppermute | solution.py:451
  39.0 4.2 %copy-start.5 = (f32[576,128]{1,0:T(8,128)}, f32[576,128]{1,0:T(8,128)S(1)}, u32[]{:S(2)}) copy-start(f32[576,128]{1,0:T(8,128)S(1)} %collective-permute-done.4.rim_low_ref) | copy-start | bytes 884740
  43.2 0.7 copy-start.6
  43.2 1.1 copy-start
  44.3 1.0 copy-start.1
  93.8 1.2 collective-permute-start.6
  95.8 22.5 %all-to-all-start = ((f32[64,8,128]{2,1,0:T(8,128)}), f32[64,8,128]{2,1,0:T(8,128)S(1)}, u32[]{:S(2)}, u32[]{:S(2)}) async-start(f32[64,8,128]{2,1,0:T(8,128)} %broadcast_in_dim.3), calls=%async_computation | async-start | bytes 524288 | tf_op jit(solution)/shard_map/all_to_all | solution.py:533
  118.2 0.7 copy-start.2

commit v8 on v4

--- a/solution.py
+++ b/solution.py
@@ -522,8 +522,12 @@
     rows_all = variables * length * columns * devices
     local_gram = jnp.dot(flattened, flattened.T, precision=lax.Precision.HIGHEST)
     packed = jnp.concatenate([local_gram[8 * i : 8 * i + 8] for i in range(4)], axis=1)
-    copies = jnp.broadcast_to(packed, (devices, 8, 128))
-    parts = lax.all_to_all(copies, ("ax", "rad"), 0, 0)
+    for gap in (1, 2):
+        pairs = [(i, i ^ gap) for i in range(lax.axis_size("rad"))]
+        packed = packed + lax.ppermute(packed, "rad", pairs)
+    copies = jnp.broadcast_to(packed, (devices // 4, 8, 128))
+    quarters = [list(range(first, devices, 4)) for first in range(4)]
+    parts = lax.all_to_all(copies, ("ax", "rad"), 0, 0, axis_index_groups=quarters)
     upper_factor, lower_inverse = factor_and_inverse(parts, vectors, rows_all)
     basis = jnp.dot(lower_inverse, flattened, precision=lax.Precision.HIGHEST).reshape(forcing.shape)
     return (basis, upper_factor)

time: 130 us -> 130 us (level)
  starting transfers between devices: 25.2 us -> 26.5 us
    all_to_all x1, waiting for transfers between devices: 13.3 us -> 9.72 us  [per_device(): lax.all_to_all(copies, ('ax', 'rad'), 0, 0, axis_index_groups=quarters)]
    ppermute x0 -> x2, waiting for transfers between devices: none -> 3.18 us  [per_device(): packed = packed + lax.ppermute(packed, 'rad', pairs)]
    ppermute x0 -> x2, starting transfers between devices: none -> 1.6 us  [per_device(): packed = packed + lax.ppermute(packed, 'rad', pairs)]
  transfers between devices with their start and end apart: 7 -> 9, of which waited for: 4 -> 6; matrix products, arithmetic and copies ran while one was open for 0% -> 0% of each run, Pallas kernels for 4% -> 4%
where the time goes in v8:
time: 130 us; the launch traced here: 129 us
  Pallas kernels  58.3 us (45%)
  waiting for transfers between devices  32.5 us (25%)
  starting transfers between devices  26.5 us (20%)
  local copies, waits for them, and re-layouts  7.69 us (6%)
  matrix products  3.35 us (3%)
    pallas_call x1, Pallas kernels, steps_call(): pl.pallas_call(steps_kernel, in_specs=[pl.BlockSpec(memory_space=pltpu.SM...  45.7 us
    ppermute x6, waiting for transfers between devices, shifted(): lax.ppermute(block, axis, [(i, i + step) for i in range(size) if 0 <= i +...  19.6 us
    ppermute x6, starting transfers between devices, shifted(): lax.ppermute(block, axis, [(i, i + step) for i in range(size) if 0 <= i +...  13.9 us
    all_to_all x1, starting transfers between devices, per_device(): lax.all_to_all(copies, ('ax', 'rad'), 0, 0, axis_index_groups=quarters)  11.1 us
    all_to_all x1, waiting for transfers between devices, per_device(): lax.all_to_all(copies, ('ax', 'rad'), 0, 0, axis_index_groups=quarters)  9.72 us
    unnamed x16, local copies, waits for them, and re-layouts  5.5 us
    pallas_call x1, Pallas kernels, factor_and_inverse(): pl.pallas_call(functools.partial(factor_kernel, rows_all=rows_all), out_s...  4.24 us
    pallas_call x1, Pallas kernels, per_device(): pl.pallas_call(pack_radial_kernel, in_specs=whole(4), out_specs=whole(2),...  3.29 us
  transfers between devices with their start and end apart: 9, of which 6 were waited for; matrix products, arithmetic and copies ran while one was open for 0% of the time, Pallas kernels for 4%

profile of v8, /device:TPU:0, one launch (start us, length us, event | category | flops | bytes accessed | tf_op | source)
XLA Modules:
  0.0 129.3 jit_solution(6970540665743954702)
XLA Ops:
  0.6 3.1 %pack_axial.1 = (f32[2256,128]{1,0:T(8,128)}, f32[2256,128]{1,0:T(8,128)}) custom-call(f32[160,16,128]{2,1,0:T(8,128)} %bitcast.16, f32[25,16,128]{2,1,0:T(8,128)} %bitcast.20, f32[16,128]{1,0:T(8,128)} %axial_ref.5, f32[16,128]{1,0:T(8,128)} %radial_ref.5), custom_call_target="tpu_custom_call" | custom-call | tf_op jit(solution)/shard_map/pack_axial/pallas_call | solution.py:484
  3.8 4.0 %collective-permute-start = (f32[2256,128]{1,0:T(8,128)}, f32[2256,128]{1,0:T(8,128)S(1)}, u32[]{:S(2)}, u32[]{:S(2)}) collective-permute-start(f32[2256,128]{1,0:T(8,128)} %get-tuple-element.10), channel_id=1, source_target_pairs={{0,8},{8,16},{16,24},{24,32},{32,40},{40,48},{48,56},{56,64},{64,7... | collective-permute-start | bytes 3465224 | tf_op jit(solution)/shard_map/ppermute | solution.py:447
  7.7 1.3 collective-permute-start.1
  9.0 3.3 %pack_radial.1 = (f32[24,16,128]{2,1,0:T(8,128)}, f32[24,16,128]{2,1,0:T(8,128)}) custom-call(f32[160,16,128]{2,1,0:T(8,128)} %bitcast.17, f32[25,16,128]{2,1,0:T(8,128)} %bitcast.21, f32[16,128]{1,0:T(8,128)} %axial_ref.5, f32[16,128]{1,0:T(8,128)} %radial_ref.5), custom_call_target="tpu_custom_call" | custom-call | tf_op jit(solution)/shard_map/pack_radial/pallas_call | solution.py:496
  12.3 1.5 %collective-permute-start.2 = (f32[24,16,128]{2,1,0:T(8,128)}, f32[24,16,128]{2,1,0:T(8,128)S(1)}, u32[]{:S(2)}, u32[]{:S(2)}) collective-permute-start(f32[24,16,128]{2,1,0:T(8,128)} %get-tuple-element.12), channel_id=1, source_target_pairs={{0,1},{1,2},{2,3},{3,4},{4,5},{5,6},{6,7},{8,9},{9,10},{10,11},{11... | collective-permute-start | bytes 589832 | tf_op jit(solution)/shard_map/ppermute | solution.py:447
  13.8 1.3 collective-permute-start.3
  15.1 3.9 %collective-permute-done.3.right_ref = f32[24,16,128]{2,1,0:T(8,128)S(1)} collective-permute-done((f32[24,16,128]{2,1,0:T(8,128)}, f32[24,16,128]{2,1,0:T(8,128)S(1)}, u32[]{:S(2)}, u32[]{:S(2)}) %collective-permute-start.3) | collective-permute-done | bytes 196640 | tf_op jit(solution)/shard_map/ppermute | solution.py:447
  19.0 0.7 copy-done.3
  19.6 1.9 %pack_corner.1 = (f32[576,128]{1,0:T(8,128)}, f32[576,128]{1,0:T(8,128)}) custom-call(f32[24,16,128]{2,1,0:T(8,128)} %copy-done.2, f32[24,16,128]{2,1,0:T(8,128)} %copy-done.3), custom_call_target="tpu_custom_call" | custom-call | tf_op jit(solution)/shard_map/pack_corner/pallas_call | solution.py:508
  21.6 4.6 %collective-permute-start.4 = (f32[576,128]{1,0:T(8,128)}, f32[576,128]{1,0:T(8,128)S(1)}, u32[]{:S(2)}, u32[]{:S(2)}) collective-permute-start(f32[576,128]{1,0:T(8,128)} %get-tuple-element.14), channel_id=1, source_target_pairs={{0,8},{8,16},{16,24},{24,32},{32,40},{40,48},{48,56},{56,64},{64,7... | collective-permute-start | bytes 884744 | tf_op jit(solution)/shard_map/ppermute | solution.py:447
  26.1 1.3 collective-permute-start.5
  27.4 11.6 %collective-permute-done.4.rim_low_ref = f32[576,128]{1,0:T(8,128)S(1)} collective-permute-done((f32[576,128]{1,0:T(8,128)}, f32[576,128]{1,0:T(8,128)S(1)}, u32[]{:S(2)}, u32[]{:S(2)}) %collective-permute-start.4) | collective-permute-done | bytes 294944 | tf_op jit(solution)/shard_map/ppermute | solution.py:447
  39.0 4.2 %collective-permute-done.5.rim_high_ref = f32[576,128]{1,0:T(8,128)S(1)} collective-permute-done((f32[576,128]{1,0:T(8,128)}, f32[576,128]{1,0:T(8,128)S(1)}, u32[]{:S(2)}, u32[]{:S(2)}) %collective-permute-start.5) | collective-permute-done | bytes 294944 | tf_op jit(solution)/shard_map/ppermute | solution.py:447
  43.2 0.7 copy-done.6
  43.9 0.4 copy-done
  44.3 1.0 copy-done.1
  45.3 45.7 %steps.1 = f32[160,16,128]{2,1,0:T(8,128)} custom-call(f32[5]{0:T(128)} %viscosity_ref.1, f32[160,16,128]{2,1,0:T(8,128)} %bitcast.18, f32[25,16,128]{2,1,0:T(8,128)} %bitcast.22, f32[16,128]{1,0:T(8,128)} %axial_ref.5, f32[16,128]{1,0:T(8,128)} %radial_ref.5, f32[2256,128]{1,0:T(8,128)} %copy-done, f32[2256,128]{1,0:T(8,128)} %copy-done.1, ...), custom_call_target="tpu_custom_call" | custom-call | tf_op jit(solution)/shard_map/steps/pallas_call | solution.py:455
  91.1 1.5 %reshape.17 = f32[32,10240]{1,0:T(8,128)S(1)} reshape(f32[160,16,128]{2,1,0:T(8,128)} %steps.1) | data formatting | bytes 2621440 | tf_op jit(solution)/shard_map/reshape | solution.py:520
  92.6 1.2 fusion.4
  93.8 0.1 pad_maximum_fusion
  93.8 0.0 collective-permute-start.6
  93.9 1.2 collective-permute-done.6
  95.0 1.6 %collective-permute-start.7 = (f32[8,128]{1,0:T(8,128)S(1)}, f32[8,128]{1,0:T(8,128)S(1)}, u32[]{:S(2)}, u32[]{:S(2)}) collective-permute-start(f32[8,128]{1,0:T(8,128)S(1)} %add.6), channel_id=1, source_target_pairs={{0,2},{1,3},{2,0},{3,1},{4,6},{5,7},{6,4},{7,5},{8,10},{9,11},{10,... | collective-permute-start | bytes 12296 | tf_op jit(solution)/shard_map/ppermute | solution.py:527
  96.6 2.0 %collective-permute-done.7 = f32[8,128]{1,0:T(8,128)S(1)} collective-permute-done((f32[8,128]{1,0:T(8,128)S(1)}, f32[8,128]{1,0:T(8,128)S(1)}, u32[]{:S(2)}, u32[]{:S(2)}) %collective-permute-start.7) | collective-permute-done | bytes 4128 | tf_op jit(solution)/shard_map/ppermute | solution.py:527
  98.6 0.7 broadcast_in_dim.3
  99.3 11.1 %all-to-all-start = ((f32[32,8,128]{2,1,0:T(8,128)}), f32[32,8,128]{2,1,0:T(8,128)S(1)}, u32[]{:S(2)}, u32[]{:S(2)}) async-start(f32[32,8,128]{2,1,0:T(8,128)} %broadcast_in_dim.3), calls=%async_computation | async-start | bytes 262144 | tf_op jit(solution)/shard_map/all_to_all | solution.py:530
  110.4 0.2 copy.11
  110.6 9.7 %all-to-all-done.parts_ref = f32[32,8,128]{2,1,0:T(8,128)S(1)} async-done(((f32[32,8,128]{2,1,0:T(8,128)}), f32[32,8,128]{2,1,0:T(8,128)S(1)}, u32[]{:S(2)}, u32[]{:S(2)}) %all-to-all-start) | async-done | bytes 131104 | tf_op jit(solution)/shard_map/all_to_all | solution.py:530
  120.4 0.7 copy-done.4
  121.0 4.2 %factor.1 = (f32[32,32]{1,0:T(8,128)}, f32[32,32]{1,0:T(8,128)}) custom-call(f32[32,8,128]{2,1,0:T(8,128)} %copy-done.4), custom_call_target="tpu_custom_call" | custom-call | tf_op jit(solution)/shard_map/factor/pallas_call | solution.py:434
  125.3 2.2 %fusion = f32[32,5,16,128]{3,0,2,1:T(8,128)S(1)} fusion(f32[5,16,128,32]{2,1,0,3:T(8,128)S(1)} %bitcast.19, f32[32,32]{1,0:T(8,128)} %get-tuple-element.16), kind=kOutput, calls=%fused_computation | convolution fusion | flops 125829120 | bytes 2625536 | tf_op jit(solution)/shard_map/dot_general | solution.py:532
  127.5 1.8 %copy.9 = f32[32,5,16,128]{3,2,1,0:T(8,128)} copy(f32[32,5,16,128]{3,0,2,1:T(8,128)S(1)} %fusion) | data formatting | bytes 2621440
  (15 shorter events, 0.0 us)
Async XLA Ops:
  3.8 39.4 %collective-permute-start = (f32[2256,128]{1,0:T(8,128)}, f32[2256,128]{1,0:T(8,128)S(1)}, u32[]{:S(2)}, u32[]{:S(2)}) collective-permute-start(f32[2256,128]{1,0:T(8,128)} %get-tuple-element.10), channel_id=1, source_target_pairs={{0,8},{8,16},{16,24},{24,32},{32,40},{40,48},{48,56},{56,64},{64,7... | collective-permute-start | bytes 3465224 | tf_op jit(solution)/shard_map/ppermute | solution.py:447
  7.7 35.5 %collective-permute-start.1 = (f32[2256,128]{1,0:T(8,128)}, f32[2256,128]{1,0:T(8,128)S(1)}, u32[]{:S(2)}, u32[]{:S(2)}) collective-permute-start(f32[2256,128]{1,0:T(8,128)} %get-tuple-element.11), channel_id=1, source_target_pairs={{8,0},{16,8},{24,16},{32,24},{40,32},{48,40},{56,48},{64,56},{72,6... | collective-permute-start | bytes 3465224 | tf_op jit(solution)/shard_map/ppermute | solution.py:447
  12.3 2.8 %collective-permute-start.2 = (f32[24,16,128]{2,1,0:T(8,128)}, f32[24,16,128]{2,1,0:T(8,128)S(1)}, u32[]{:S(2)}, u32[]{:S(2)}) collective-permute-start(f32[24,16,128]{2,1,0:T(8,128)} %get-tuple-element.12), channel_id=1, source_target_pairs={{0,1},{1,2},{2,3},{3,4},{4,5},{5,6},{6,7},{8,9},{9,10},{10,11},{11... | collective-permute-start | bytes 589832 | tf_op jit(solution)/shard_map/ppermute | solution.py:447
  13.8 5.2 %collective-permute-start.3 = (f32[24,16,128]{2,1,0:T(8,128)}, f32[24,16,128]{2,1,0:T(8,128)S(1)}, u32[]{:S(2)}, u32[]{:S(2)}) collective-permute-start(f32[24,16,128]{2,1,0:T(8,128)} %get-tuple-element.13), channel_id=1, source_target_pairs={{1,0},{2,1},{3,2},{4,3},{5,4},{6,5},{7,6},{9,8},{10,9},{11,10},{12... | collective-permute-start | bytes 589832 | tf_op jit(solution)/shard_map/ppermute | solution.py:447
  15.1 3.9 %copy-start.2 = (f32[24,16,128]{2,1,0:T(8,128)}, f32[24,16,128]{2,1,0:T(8,128)S(1)}, u32[]{:S(2)}) copy-start(f32[24,16,128]{2,1,0:T(8,128)S(1)} %collective-permute-done.2.left_ref) | copy-start | bytes 589828
  19.0 0.7 copy-start.3
  21.6 17.4 %collective-permute-start.4 = (f32[576,128]{1,0:T(8,128)}, f32[576,128]{1,0:T(8,128)S(1)}, u32[]{:S(2)}, u32[]{:S(2)}) collective-permute-start(f32[576,128]{1,0:T(8,128)} %get-tuple-element.14), channel_id=1, source_target_pairs={{0,8},{8,16},{16,24},{24,32},{32,40},{40,48},{48,56},{56,64},{64,7... | collective-permute-start | bytes 884744 | tf_op jit(solution)/shard_map/ppermute | solution.py:447
  26.1 17.1 %collective-permute-start.5 = (f32[576,128]{1,0:T(8,128)}, f32[576,128]{1,0:T(8,128)S(1)}, u32[]{:S(2)}, u32[]{:S(2)}) collective-permute-start(f32[576,128]{1,0:T(8,128)} %get-tuple-element.15), channel_id=1, source_target_pairs={{8,0},{16,8},{24,16},{32,24},{40,32},{48,40},{56,48},{64,56},{72,6... | collective-permute-start | bytes 884744 | tf_op jit(solution)/shard_map/ppermute | solution.py:447
  39.0 4.2 %copy-start.5 = (f32[576,128]{1,0:T(8,128)}, f32[576,128]{1,0:T(8,128)S(1)}, u32[]{:S(2)}) copy-start(f32[576,128]{1,0:T(8,128)S(1)} %collective-permute-done.4.rim_low_ref) | copy-start | bytes 884740
  43.2 0.7 copy-start.6
  43.2 1.1 copy-start
  44.3 1.0 copy-start.1
  93.8 1.2 collective-permute-start.6
  95.0 3.6 %collective-permute-start.7 = (f32[8,128]{1,0:T(8,128)S(1)}, f32[8,128]{1,0:T(8,128)S(1)}, u32[]{:S(2)}, u32[]{:S(2)}) collective-permute-start(f32[8,128]{1,0:T(8,128)S(1)} %add.6), channel_id=1, source_target_pairs={{0,2},{1,3},{2,0},{3,1},{4,6},{5,7},{6,4},{7,5},{8,10},{9,11},{10,... | collective-permute-start | bytes 12296 | tf_op jit(solution)/shard_map/ppermute | solution.py:527
  99.3 21.1 %all-to-all-start = ((f32[32,8,128]{2,1,0:T(8,128)}), f32[32,8,128]{2,1,0:T(8,128)S(1)}, u32[]{:S(2)}, u32[]{:S(2)}) async-start(f32[32,8,128]{2,1,0:T(8,128)} %broadcast_in_dim.3), calls=%async_computation | async-start | bytes 262144 | tf_op jit(solution)/shard_map/all_to_all | solution.py:530
  120.4 0.7 copy-start.4
